TPU v7x, 128 devices: a whole 4x4x4 slice. The times are simulated.
128 devices in a mesh: dp: 16 (over z, x), expert: 8 (over y, core).
Axes of the slice: x: 4, y: 4, z: 4, core: 2. Of those that a mesh axis runs over, the one named last changes fastest.
Arguments:
- tokens: bfloat16 [16384, 1280], P(('dp', 'expert')), may hold values from -6 to 6
- routes: int32 [16384, 2], P(('dp', 'expert')), may hold values from 0 to 31, all different within a row; in each aligned block of 128 rows (0 to 127, 128 to 255, ...) at most 10 rows name the same one
- combine: float32 [16384, 2], P(('dp', 'expert')), may hold values from 0.1 to 1
- w_in: bfloat16 [1280, 163840], P(None, ('dp', 'expert')), may hold values from -0.15625 to 0.15625
- w_out: bfloat16 [163840, 1280], P(('dp', 'expert')), may hold values from -0.078125 to 0.078125
- out_grad: bfloat16 [16384, 1280], P(('dp', 'expert')), may hold values from -6 to 6
- head_w: bfloat16 [1280, 17408], P(None, 'expert'), may hold values from -0.5 to 0.5
- labels: int32 [64, 4], P('dp'), may hold values from 0 to 17407
Outputs:
- mixed_out: bfloat16 [16384, 1280], P(('dp', 'expert'))
- d_tokens: bfloat16 [16384, 1280], P(('dp', 'expert'))
- d_combine: float32 [16384, 2], P(('dp', 'expert'))
- d_w_in: bfloat16 [1280, 163840], P(None, ('dp', 'expert'))
- d_w_out: bfloat16 [163840, 1280], P(('dp', 'expert'))
- image_loss: float32 [64], P('dp')
- d_pooled: float32 [64, 1280], P('dp')
- d_head: bfloat16 [1280, 17408], P('dp', 'expert')
Inputs may be any that keep to these rules, and one draw needn't show every extreme that they name: `routes`: in the 128 rows of each device no expert is named by more than 10 rows, a bound that some block reaches; the two entries of a row differ. `labels`: entries of one image may repeat.
All inputs are finite; a program needn't handle non-finite values.
Results may differ from a plain program's by a relative error of at most 0.015.
Values may be sent and summed in bfloat16 or wider, within the bound.
No kernel may reach another device: no remote copies, remote signals or barrier semaphores. Data moves between devices by JAX's collectives and lax.ppermute only.
A program may use at most 192 MiB of HBM per device.

v0:
```python
import jax
import jax.numpy as jnp
from jax import lax
from jax.sharding import PartitionSpec as P

D = 1280
EXPERTS = 32
PATCHES = 256
CLASSES = 17408


beta_rate = 0.99
norm_eps = 1e-06


def gelu_fn(values):
    return jax.nn.gelu(values, approximate=True)


def normalize(pooled):
    center = jnp.mean(pooled, axis=1, keepdims=True)
    spread = jnp.mean(jnp.square(pooled - center), axis=1, keepdims=True)
    return (pooled - center) * lax.rsqrt(spread + norm_eps)


def weighted_focal(logit_vals, targets, class_weight):
    nll_vals = targets * jax.nn.softplus(-logit_vals) + (1.0 - targets) * jax.nn.softplus(
        logit_vals
    )
    return class_weight[None, :] * jnp.square(1.0 - jnp.exp(-nll_vals)) * nll_vals


def expert_pass(xs_rows, grad_rows, w_first, w_second):
    h_pre = jnp.dot(xs_rows, w_first, preferred_element_type=jnp.float32)
    hidden, gelu_back = jax.vjp(gelu_fn, h_pre)
    hidden_bf = hidden.astype(jnp.bfloat16)
    expert_out = jnp.dot(hidden_bf, w_second, preferred_element_type=jnp.float32)
    d_hidden = lax.dot_general(
        grad_rows, w_second, (((1,), (1,)), ((), ())), preferred_element_type=jnp.float32
    )
    d_pre = gelu_back(d_hidden)[0].astype(jnp.bfloat16)
    d_second = lax.dot_general(
        hidden_bf, grad_rows, (((0,), (0,)), ((), ())), preferred_element_type=jnp.float32
    ).astype(jnp.bfloat16)
    d_first = lax.dot_general(
        xs_rows, d_pre, (((0,), (0,)), ((), ())), preferred_element_type=jnp.float32
    ).astype(jnp.bfloat16)
    d_rows = lax.dot_general(
        d_pre, w_first, (((1,), (1,)), ((), ())), preferred_element_type=jnp.float32
    )
    return (expert_out, d_rows, d_first, d_second)


def to_experts(stacked):
    return lax.all_to_all(stacked, ("dp", "expert"), split_axis=1, concat_axis=1, tiled=True)


def to_sources(partials):
    return lax.all_to_all(partials, ("dp", "expert"), split_axis=0, concat_axis=0, tiled=True)


def shards(tokens, routes, combine, w_in, w_out, out_grad, head_w, labels):
    dp_size = lax.axis_size("dp")
    ex_size = lax.axis_size("expert")
    n_devices = dp_size * ex_size
    tok_rows = tokens.shape[0]
    capacity = 5 * tok_rows // 64
    share_count = n_devices // EXPERTS
    buffer_rows = EXPERTS * capacity
    flat_routes = routes.reshape(tok_rows * 2)
    route_hits = (flat_routes[:, None] == jnp.arange(EXPERTS, dtype=jnp.int32)[None, :]).astype(
        jnp.int32
    )
    earlier = jnp.cumsum(route_hits, axis=0) - route_hits
    slot_pos = jnp.sum(earlier * route_hits, axis=1)
    slot_index = flat_routes * capacity + slot_pos
    pair_table = (jnp.arange(buffer_rows, dtype=jnp.int32)[:, None] == slot_index[None, :]).astype(
        jnp.bfloat16
    )
    token_table = jnp.sum(pair_table.reshape(buffer_rows, tok_rows, 2), axis=2)
    pair_grad = (
        (combine[:, :, None] * out_grad.astype(jnp.float32)[:, None, :])
        .astype(jnp.bfloat16)
        .reshape(tok_rows * 2, D)
    )
    x_buf = jnp.dot(token_table, tokens, preferred_element_type=jnp.float32).astype(jnp.bfloat16)
    g_buf = jnp.dot(pair_table, pair_grad, preferred_element_type=jnp.float32).astype(jnp.bfloat16)
    stacked = jnp.stack([x_buf, g_buf]).reshape(2, EXPERTS, 1, capacity, D)
    stacked = jnp.broadcast_to(stacked, (2, EXPERTS, share_count, capacity, D)).reshape(
        2, n_devices, capacity, D
    )
    arrived = to_experts(stacked)
    xs_rows = arrived[0].reshape(n_devices * capacity, D)
    grad_rows = arrived[1].reshape(n_devices * capacity, D)
    expert_out, d_rows, d_w_in, d_w_out = expert_pass(xs_rows, grad_rows, w_in, w_out)
    back_out = to_sources(expert_out.reshape(n_devices, capacity, D))
    expert_sum = jnp.sum(back_out.reshape(EXPERTS, share_count, capacity, D), axis=1).reshape(
        buffer_rows, D
    )
    expert_vals = jnp.take(expert_sum, slot_index, axis=0).reshape(tok_rows, 2, D)
    mixed_out = (
        tokens.astype(jnp.float32) + jnp.sum(combine[:, :, None] * expert_vals, axis=1)
    ).astype(jnp.bfloat16)
    d_combine = jnp.sum(out_grad.astype(jnp.float32)[:, None, :] * expert_vals, axis=2)
    ex_index = lax.axis_index("expert")
    row_images = ex_size * tok_rows // PATCHES
    token_image = (ex_index * tok_rows + jnp.arange(tok_rows, dtype=jnp.int32)) // PATCHES
    image_table = (jnp.arange(row_images, dtype=jnp.int32)[:, None] == token_image[None, :]).astype(
        jnp.float32
    )
    pooled_part = jnp.dot(
        image_table, mixed_out.astype(jnp.float32), precision=lax.Precision.HIGHEST
    )
    class_cols = head_w.shape[1]
    class_ids = ex_index * class_cols + jnp.arange(class_cols, dtype=jnp.int32)
    targets = jnp.any(labels[:, :, None] == class_ids[None, None, :], axis=1).astype(jnp.float32)
    counts = lax.psum(jnp.sum(targets, axis=0), "dp")
    effective = (1.0 - beta_rate) / (1.0 - jnp.power(beta_rate, counts + 1.0))
    pooled_sum, effective_total = lax.psum((pooled_part, jnp.sum(effective)), "expert")
    back_parts = to_sources(d_rows.reshape(n_devices, capacity, D))
    back_sum = jnp.sum(back_parts.reshape(EXPERTS, share_count, capacity, D), axis=1).reshape(
        buffer_rows, D
    )
    expert_back = jnp.take(back_sum, slot_index, axis=0).reshape(tok_rows, 2, D)
    d_tokens = (out_grad.astype(jnp.float32) + jnp.sum(expert_back, axis=1)).astype(jnp.bfloat16)
    class_weight = effective * CLASSES / effective_total
    pooled = pooled_sum / PATCHES
    normed, norm_back = jax.vjp(normalize, pooled)
    normed_bf = normed.astype(jnp.bfloat16)
    logits = jnp.dot(normed_bf, head_w, preferred_element_type=jnp.float32)
    focal_terms, focal_back = jax.vjp(
        lambda logit_vals: weighted_focal(logit_vals, targets, class_weight), logits
    )
    d_logits = focal_back(jnp.ones_like(focal_terms))[0].astype(jnp.bfloat16)
    normed_part = lax.dot_general(
        d_logits, head_w, (((1,), (1,)), ((), ())), preferred_element_type=jnp.float32
    )
    d_normed, image_loss = lax.psum((normed_part, jnp.sum(focal_terms, axis=1)), "expert")
    d_pooled = norm_back(d_normed)[0]
    d_head = lax.psum_scatter(
        lax.dot_general(
            normed_bf, d_logits, (((0,), (0,)), ((), ())), preferred_element_type=jnp.float32
        ).astype(jnp.bfloat16),
        "dp",
        scatter_dimension=0,
        tiled=True,
    )
    return (mixed_out, d_tokens, d_combine, d_w_in, d_w_out, image_loss, d_pooled, d_head)


def solution(mesh):
    in_specs = (
        P(("dp", "expert"), None),
        P(("dp", "expert"), None),
        P(("dp", "expert"), None),
        P(None, ("dp", "expert")),
        P(("dp", "expert"), None),
        P(("dp", "expert"), None),
        P(None, "expert"),
        P("dp", None),
    )
    out_specs = (
        P(("dp", "expert"), None),
        P(("dp", "expert"), None),
        P(("dp", "expert"), None),
        P(None, ("dp", "expert")),
        P(("dp", "expert"), None),
        P("dp"),
        P("dp", None),
        P("dp", "expert"),
    )
    return jax.shard_map(shards, mesh=mesh, in_specs=in_specs, out_specs=out_specs, check_vma=False)
```

profile of v0, /device:TPU:0, one launch (start us, length us, event | category | flops | bytes accessed | tf_op | source)
XLA Modules:
  0.0 685.1 jit_solution(5458899573106623758)
XLA Ops:
  7.2 0.9 copy.46
  9.5 0.8 copy.45
  10.5 0.7 multiply_add_fusion.1
  11.2 2.2 convolution_convert_fusion.4
  13.5 2.2 stack.9
  15.7 2.4 mul.203
  18.0 3.0 mul.204
  21.1 2.7 convolution_convert_fusion.3
  23.7 2.2 stack.10
  25.9 2.0 maximum_bitcast_fusion
  27.9 1.7 copy.51
  29.6 3.8 broadcast_in_dim.16
  33.5 89.6 %all_to_all.15 = bf16[2,128,10,1280]{3,0,2,1:T(2,128)(2,1)S(1)} all-to-all(bf16[2,128,10,1280]{3,0,2,1:T(2,128)(2,1)S(1)} %bitcast.42), channel_id=1, replica_groups=mesh['dp'=16,'expert'=8] {'dp','expert'}, dimensions={1} | all-to-all | bytes 13107200 | tf_op jit(solution)/shard_map/all_to_all | solution.py:55
  123.1 40.3 %slice_reduce_fusion = (bf16[128,10,1280]{2,1,0:T(8,128)(2,1)}, bf16[128,10,1280]{2,1,0:T(8,128)(2,1)}) fusion(bf16[2,128,10,1280]{3,0,2,1:T(2,128)(2,1)S(1)} %all_to_all.15), kind=kLoop, calls=%fused_computation.16 | loop fusion | bytes 13107200 | tf_op jit(solution)/shard_map/slice | solution.py:94
  163.4 7.0 %reshape_squeeze.7 = bf16[1280,1280]{1,0:T(8,128)(2,1)} reshape(bf16[128,10,1280]{2,1,0:T(8,128)(2,1)} %get-tuple-element.49) | data formatting | bytes 6553600 | tf_op jit(solution)/shard_map/reshape;squeeze | solution.py:94
  170.4 7.0 %reshape_squeeze.6 = bf16[1280,1280]{1,0:T(8,128)(2,1)} reshape(bf16[128,10,1280]{2,1,0:T(8,128)(2,1)} %get-tuple-element.50) | data formatting | bytes 6553600 | tf_op jit(solution)/shard_map/reshape;squeeze | solution.py:93
  177.4 7.6 %fusion.37 = f32[1280,1280]{1,0:T(8,128)S(1)} fusion(bf16[1280,1280]{1,0:T(8,128)(2,1)} %reshape_squeeze.7, bf16[1280,1280]{1,0:T(8,128)(2,1)} %param.15), kind=kOutput, calls=%fused_computation.102 | convolution fusion | flops 4194304000 | bytes 13107200 | tf_op jit(solution)/shard_map/dot_general | solution.py:38
  185.0 9.4 %fusion.6 = (bf16[1280,1280]{1,0:T(8,128)(2,1)S(1)}, f32[1280,1280]{1,0:T(8,128)}) fusion(f32[1280,1280]{1,0:T(8,128)S(1)} %fusion.37, bf16[1280,1280]{1,0:T(8,128)(2,1)S(1)} %copy-done.4, bf16[1280,1280]{1,0:T(8,128)(2,1)S(1)} %copy-done), kind=kOutput, calls=%fused_computation.15 | convolution fusion | flops 4227072000 | bytes 22937600 | tf_op jit(solution)/shard_map/dot_general | solution.py:34
  194.4 1.8 copy-done.10
  196.2 6.5 fusion.38
  202.8 8.6 %reshape.154 = f32[128,10,1280]{2,1,0:T(8,128)} reshape(f32[1280,1280]{1,0:T(8,128)} %fusion.38) | data formatting | bytes 13107200 | tf_op jit(solution)/shard_map/reshape | solution.py:120
  211.4 6.3 all-to-all-start.2
  217.7 11.2 %fusion.36 = f32[1280,1280]{1,0:T(8,128)} fusion(bf16[1280,1280]{1,0:T(8,128)(2,1)S(1)} %copy-done.9, f32[1280,1280]{1,0:T(8,128)} %get-tuple-element.63), kind=kOutput, calls=%fused_computation.101 | convolution fusion | flops 4209049600 | bytes 16384000 | tf_op jit(solution)/shard_map/dot_general | solution.py:37
  228.9 8.6 %reshape.150 = f32[128,10,1280]{2,1,0:T(8,128)} reshape(f32[1280,1280]{1,0:T(8,128)} %fusion.36) | data formatting | bytes 13107200 | tf_op jit(solution)/shard_map/reshape | solution.py:96
  237.5 103.3 %all-to-all-done.2 = f32[128,10,1280]{2,1,0:T(8,128)} async-done(((f32[128,10,1280]{2,1,0:T(8,128)}), f32[128,10,1280]{2,1,0:T(8,128)}, u32[]{:S(2)}, u32[]{:S(2)}) %all-to-all-start.2) | async-done | bytes 6553632 | tf_op jit(solution)/shard_map/all_to_all | solution.py:59
  340.8 10.3 %all-to-all-start.1 = ((f32[128,10,1280]{2,1,0:T(8,128)}), f32[128,10,1280]{2,1,0:T(8,128)}, u32[]{:S(2)}, u32[]{:S(2)}) async-start(f32[128,10,1280]{2,1,0:T(8,128)} %reshape.150), calls=%async_computation.1 | async-start | bytes 20971520 | tf_op jit(solution)/shard_map/all_to_all | solution.py:59
  351.4 183.0 %psum.35 = f32[2176]{0:T(1024)S(1)} all-reduce(f32[2176]{0:T(1024)S(1)} %convert_reduce_fusion), channel_id=1, replica_groups=mesh['dp'=16,'expert'=8] {'dp'}, use_global_device_ids=true, to_apply=%region_11.13 | all-reduce | flops 2176 | bytes 17408 | tf_op jit(solution)/shard_map/psum | solution.py:117
  535.0 6.8 bitcast_reduce_fusion
  541.8 1.8 reshape.156
  543.7 6.8 bitcast_reduce_fusion.1
  550.5 1.8 reshape.152
  552.4 2.2 gather_fusion.1
  554.6 2.3 gather_fusion
  556.9 3.1 multiply_reduce_fusion
  560.0 0.8 reshape.153
  560.8 1.6 multiply_reduce_fusion.1
  562.6 27.7 %all-reduce.2 = (f32[4,1280]{1,0:T(4,128)S(1)}, f32[]{:T(128)}) all-reduce(f32[4,1280]{1,0:T(4,128)S(1)} %fusion.29, f32[]{:T(128)} %fusion.28), channel_id=1, replica_groups=mesh['dp'=16,'expert'=8] {'expert'}, use_global_device_ids=true, to_apply=%region_14.16 | all-reduce | flops 5121 | bytes 40968 | tf_op jit(solution)/shard_map/psum | solution.py:119
  591.3 3.6 multiply_reduce_fusion.2
  595.0 4.1 convolution_convert_fusion
  599.1 1.9 copy-done.5
  601.0 8.2 %convolution_convert_fusion.2 = bf16[1280,1280]{1,0:T(8,128)(2,1)} fusion(bf16[1280,1280]{1,0:T(8,128)(2,1)S(1)} %copy-done.5, bf16[1280,1280]{1,0:T(8,128)(2,1)} %copy-done.10), kind=kOutput, calls=%fused_computation.8 | convolution fusion | flops 4195942400 | bytes 9830400 | tf_op jit(solution)/shard_map/dot_general | solution.py:45
  609.2 10.1 %convolution_convert_fusion.1 = bf16[1280,1280]{1,0:T(8,128)(2,1)} fusion(bf16[1280,1280]{1,0:T(8,128)(2,1)S(1)} %copy-done.3, f32[1280,1280]{1,0:T(8,128)} %get-tuple-element.63), kind=kOutput, calls=%fused_computation.7 | convolution fusion | flops 4210688000 | bytes 13107200 | tf_op jit(solution)/shard_map/dot_general | solution.py:42
  619.4 1.6 fusion.34
  620.9 25.1 %all-reduce.1 = (f32[4]{0:T(128)}, f32[4,1280]{1,0:T(4,128)S(1)}) all-reduce(f32[4]{0:T(128)S(1)} %get-tuple-element.64, f32[4,1280]{1,0:T(4,128)S(1)} %fusion.34), channel_id=1, replica_groups=mesh['dp'=16,'expert'=8] {'expert'}, use_global_device_ids=true, to_apply=%region_18.21 | all-reduce | flops 5124 | bytes 40992 | tf_op jit(solution)/shard_map/psum | solution.py:138
  646.8 3.0 reshape.157
  649.8 3.7 reduce_sum.156
  654.6 1.9 add_convert_fusion
  656.6 21.2 %reduce-scatter.4.cloned.1.call-done = bf16[80,2176]{1,0:T(8,128)(2,1)} async-done(((bf16[1280,2176]{1,0:T(8,128)(2,1)}), bf16[80,2176]{1,0:T(8,128)(2,1)}) %reduce-scatter.4.cloned.1.call-update) | async-done | bytes 348176
  (62 shorter events, 5.7 us)
Async XLA Ops:
  7.2 177.8 %copy-start = (bf16[1280,1280]{1,0:T(8,128)(2,1)S(1)}, bf16[1280,1280]{1,0:T(8,128)(2,1)}, u32[]{:S(2)}) copy-start(bf16[1280,1280]{1,0:T(8,128)(2,1)} %param.14) | copy-start | bytes 9830404
  177.4 7.6 %copy-start.4 = (bf16[1280,1280]{1,0:T(8,128)(2,1)S(1)}, bf16[1280,1280]{1,0:T(8,128)(2,1)}, u32[]{:S(2)}) copy-start(bf16[1280,1280]{1,0:T(8,128)(2,1)} %reshape_squeeze.6) | copy-start | bytes 9830404
  194.4 1.8 copy-start.10
  211.4 6.3 copy-start.9
  211.4 129.4 %all-to-all-start.2 = ((f32[128,10,1280]{2,1,0:T(8,128)}), f32[128,10,1280]{2,1,0:T(8,128)}, u32[]{:S(2)}, u32[]{:S(2)}) async-start(f32[128,10,1280]{2,1,0:T(8,128)} %reshape.154), calls=%async_computation.2 | async-start | bytes 20971520 | tf_op jit(solution)/shard_map/all_to_all | solution.py:59
  237.5 113.6 %copy-start.8 = (s32[4,4]{1,0:T(4,128)S(1)}, s32[4,4]{1,0:T(4,128)}, u32[]{:S(2)}) copy-start(s32[4,4]{1,0:T(4,128)} %param.18) | copy-start | bytes 196
  340.8 202.9 %all-to-all-start.1 = ((f32[128,10,1280]{2,1,0:T(8,128)}), f32[128,10,1280]{2,1,0:T(8,128)}, u32[]{:S(2)}, u32[]{:S(2)}) async-start(f32[128,10,1280]{2,1,0:T(8,128)} %reshape.150), calls=%async_computation.1 | async-start | bytes 20971520 | tf_op jit(solution)/shard_map/all_to_all | solution.py:59
  351.1 326.7 %reduce-scatter.4.cloned.1.call-start = ((), (), s32[]{:S(2)}) async-start(), calls=%async_computation.4 | async-start | bytes 5918720
  554.6 2.3 copy-start.2
  556.9 5.5 copy-start.7
  562.5 32.5 %copy-start.6 = (bf16[128,1280]{1,0:T(8,128)(2,1)}, bf16[128,1280]{1,0:T(8,128)(2,1)S(1)}, u32[]{:S(2)}) copy-start(bf16[128,1280]{1,0:T(8,128)(2,1)S(1)} %add_convert_fusion.1) | copy-start | bytes 983044
  599.1 1.9 copy-start.5
  601.0 8.2 %copy-start.3 = (bf16[1280,1280]{1,0:T(8,128)(2,1)S(1)}, bf16[1280,1280]{1,0:T(8,128)(2,1)}, u32[]{:S(2)}) copy-start(bf16[1280,1280]{1,0:T(8,128)(2,1)} %reshape_squeeze.7) | copy-start | bytes 9830404
  601.0 18.3 %slice-start = ((s8[5570560]{0:T(1024)(128)(4,1)}), s8[4194304]{0:T(1024)(128)(4,1)S(1)}, s32[]{:S(2)}) async-start(s8[5570560]{0:T(1024)(128)(4,1)} %bitcast.43), calls=%async_computation.5 | async-start | bytes 8388608
  609.2 10.1 %slice-start.1 = ((s8[5570560]{0:T(1024)(128)(4,1)}), s8[1376256]{0:T(1024)(128)(4,1)S(1)}, s32[]{:S(2)}) async-start(s8[5570560]{0:T(1024)(128)(4,1)} %bitcast.43), calls=%async_computation.6 | async-start | bytes 2752512
  609.2 68.5 %copy-start.1 = (bf16[1280,1280]{1,0:T(8,128)(2,1)S(1)}, bf16[1280,1280]{1,0:T(8,128)(2,1)}, u32[]{:S(2)}) copy-start(bf16[1280,1280]{1,0:T(8,128)(2,1)} %param.14) | copy-start | bytes 9830404
Sparse Core Ops, SparseCore 0:
  599.2 78.4 reduce-scatter.3
where the time goes:
time: 692 us; the launch traced here: 685 us
  blocking collectives  325 us (47%)
  waiting for transfers between devices  124 us (18%)
  local copies, waits for them, and re-layouts  106 us (15%)
  matrix products  67.4 us (10%)
  other arithmetic  30.6 us (4%)
  starting transfers between devices  16.6 us (2%)
  between operations  14.8 us (2%)
    psum x1, blocking collectives, shards(): counts = lax.psum(jnp.sum(targets, axis=0), 'dp')  183 us
    all_to_all x2, waiting for transfers between devices, to_sources(): lax.all_to_all(partials, ('dp', 'expert'), split_axis=0, concat_axis=0, t...  103 us
    all_to_all x1, blocking collectives, to_experts(): lax.all_to_all(stacked, ('dp', 'expert'), split_axis=1, concat_axis=1, ti...  89.6 us
    slice x1, local copies, waits for them, and re-layouts, shards(): grad_rows = arrived[1].reshape(n_devices * capacity, D)  40.3 us
    psum x1, blocking collectives, shards(): lax.psum((pooled_part, jnp.sum(effective)), 'expert')  27.7 us
    psum x1, blocking collectives, shards(): lax.psum((normed_part, jnp.sum(focal_terms, axis=1)), 'expert')  25.1 us
    unnamed x2, waiting for transfers between devices  21.2 us
    all_to_all x2, starting transfers between devices, to_sources(): lax.all_to_all(partials, ('dp', 'expert'), split_axis=0, concat_axis=0, t...  16.5 us
  transfers between devices with their start and end apart: 3, of which 2 were waited for; matrix products, arithmetic and copies ran while one was open for 9% of the time, Pallas kernels for 0%

commit v1 on v0

v1 whole, which is shorter than its diff:
```python
import jax
import jax.numpy as jnp
from jax import lax
from jax.sharding import Mesh, PartitionSpec as P

D = 1280
EXPERTS = 32
PATCHES = 256
CLASSES = 17408
CAP = 10
CHIPS = 64
IMAGES = 64
BETA = 0.99
EPS = 1e-06

CHIP = ("dp", "yh", "yl")
EX = ("yh", "yl", "core")
ALL = ("dp", "yh", "yl", "core")
SWAP = [(0, 1), (1, 0)]
F32 = jnp.float32
BF16 = jnp.bfloat16


def dot(a, b, ca, cb):
    return lax.dot_general(a, b, (((ca,), (cb,)), ((), ())), preferred_element_type=F32)


def chip_swap(rows):
    packed = rows.reshape(CHIPS, CAP // 2, 2, D)
    return lax.all_to_all(packed, CHIP, 0, 0, tiled=True).reshape(CHIPS * CAP, D)


def both_cores(rows):
    return jnp.concatenate([rows, lax.ppermute(rows, "core", SWAP)], axis=0)


def reduce_cores(partial):
    half = CHIPS * CAP
    other = lax.ppermute(partial[half:].astype(BF16), "core", SWAP)
    return (partial[:half] + other.astype(F32)).astype(BF16)


def gelu_fn(values):
    return jax.nn.gelu(values, approximate=True)


def normalize(pooled):
    center = jnp.mean(pooled, axis=1, keepdims=True)
    spread = jnp.mean(jnp.square(pooled - center), axis=1, keepdims=True)
    return (pooled - center) * lax.rsqrt(spread + EPS)


def weighted_focal(logit_vals, targets, class_weight):
    nll_vals = targets * jax.nn.softplus(-logit_vals) + (1.0 - targets) * jax.nn.softplus(
        logit_vals
    )
    return class_weight[None, :] * jnp.square(1.0 - jnp.exp(-nll_vals)) * nll_vals


def effective_of(counts):
    return (1.0 - BETA) / (1.0 - jnp.power(BETA, counts + 1.0))


def shards(tokens, routes, combine, w_in, w_out, out_grad, head_w, labels):
    tok = tokens.shape[0]
    dp_index = lax.axis_index("dp")
    ex_index = lax.axis_index(EX)
    expert_ids = jnp.arange(EXPERTS, dtype=jnp.int32)
    hit0 = routes[:, 0:1] == expert_ids[None, :]
    hit1 = routes[:, 1:2] == expert_ids[None, :]
    t_ids = jnp.arange(tok, dtype=jnp.int32)
    before = (t_ids[:, None] > t_ids[None, :]).astype(BF16)
    earlier = dot(before, (hit0 | hit1).astype(BF16), 1, 0).astype(jnp.int32)
    pos0 = jnp.sum(jnp.where(hit0, earlier, 0), axis=1)
    pos1 = jnp.sum(jnp.where(hit1, earlier, 0), axis=1)
    row0 = routes[:, 0] * (2 * CAP) + pos0
    row1 = routes[:, 1] * (2 * CAP) + pos1
    row = jnp.concatenate([row0, row1])
    r_ids = jnp.arange(CHIPS * CAP, dtype=jnp.int32)
    base = r_ids - CAP * ((r_ids // CAP) % 2)
    table = (base[:, None] == row[None, :]).astype(BF16)
    x_send = dot(table[:, :tok] + table[:, tok:], tokens, 1, 0).astype(BF16)
    grad_f = out_grad.astype(F32)
    pair_grad = jnp.concatenate(
        [(combine[:, 0:1] * grad_f).astype(BF16), (combine[:, 1:2] * grad_f).astype(BF16)], axis=0
    )
    g_send = dot(table, pair_grad, 1, 0).astype(BF16)
    xs = both_cores(chip_swap(x_send))
    gs = both_cores(chip_swap(g_send))
    h_pre = dot(xs, w_in, 1, 0)
    hidden, gelu_back = jax.vjp(gelu_fn, h_pre)
    hidden = hidden.astype(BF16)
    back_out = chip_swap(reduce_cores(dot(hidden, w_out, 1, 0)))
    d_pre = gelu_back(dot(gs, w_out, 1, 1))[0].astype(BF16)
    back_rows = chip_swap(reduce_cores(dot(d_pre, w_in, 1, 1)))
    d_w_out = dot(hidden, gs, 0, 0).astype(BF16)
    d_w_in = dot(xs, d_pre, 0, 0).astype(BF16)
    vals = dot(table, back_out, 0, 0)
    vals0, vals1 = vals[:tok], vals[tok:]
    mixed_out = (
        tokens.astype(F32) + (combine[:, 0:1] * vals0 + combine[:, 1:2] * vals1)
    ).astype(BF16)
    d_combine = jnp.stack(
        [jnp.sum(grad_f * vals0, axis=1), jnp.sum(grad_f * vals1, axis=1)], axis=1
    )
    backs = dot(table, back_rows, 0, 0)
    d_tokens = (grad_f + (backs[:tok] + backs[tok:])).astype(BF16)
    pooled_own = lax.psum(jnp.sum(mixed_out.astype(F32), axis=0), "core") / PATCHES
    spread_out = jnp.broadcast_to(pooled_own.reshape(1, 10, 128), (CHIPS, 10, 128))
    pooled = lax.all_to_all(spread_out, CHIP, 0, 0, tiled=True).reshape(IMAGES, D)
    own_labels = jnp.broadcast_to(labels.reshape(1, 16), (16, 16))
    all_labels = lax.all_to_all(own_labels, "dp", 0, 0, tiled=True).reshape(IMAGES, 4)
    flat = all_labels.reshape(IMAGES * 4)
    entry = jnp.arange(IMAGES * 4, dtype=jnp.int32)
    same = flat[:, None] == flat[None, :]
    sooner = entry[:, None] > entry[None, :]
    same_image = (entry[:, None] // 4) == (entry[None, :] // 4)
    fresh = ~jnp.any(same & sooner & same_image, axis=1)
    first = ~jnp.any(same & sooner, axis=1)
    entry_count = jnp.sum((same & fresh[None, :]).astype(F32), axis=1)
    distinct = jnp.sum(first.astype(F32))
    effective_total = (CLASSES - distinct) * effective_of(jnp.zeros((), F32)) + jnp.sum(
        jnp.where(first, effective_of(entry_count), 0.0)
    )
    class_cols = head_w.shape[1]
    class_ids = ex_index * class_cols + jnp.arange(class_cols, dtype=jnp.int32)
    targets = jnp.any(all_labels[:, :, None] == class_ids[None, None, :], axis=1).astype(F32)
    class_weight = effective_of(jnp.sum(targets, axis=0)) * CLASSES / effective_total
    normed_bf = normalize(pooled).astype(BF16)
    logits = dot(normed_bf, head_w, 1, 0)
    focal_terms, focal_back = jax.vjp(
        lambda logit_vals: weighted_focal(logit_vals, targets, class_weight), logits
    )
    d_logits = focal_back(jnp.ones_like(focal_terms))[0].astype(BF16)
    own_logits = lax.dynamic_slice_in_dim(d_logits, dp_index * 4, 4, 0)
    own_loss = jnp.sum(lax.dynamic_slice_in_dim(focal_terms, dp_index * 4, 4, 0), axis=1)
    normed_part = dot(own_logits, head_w, 1, 1)
    message = jnp.concatenate(
        [normed_part.reshape(40, 128), jnp.broadcast_to(own_loss[:, None], (4, 128)), jnp.zeros((4, 128), F32)], axis=0
    )
    parts = lax.all_to_all(
        jnp.broadcast_to(message[None], (8, 48, 128)), EX, 0, 0, tiled=True
    )
    total = jnp.sum(parts, axis=0)
    d_normed = total[:40].reshape(4, D)
    image_loss = total[40:44, 0]
    own_pooled = lax.dynamic_slice_in_dim(pooled, dp_index * 4, 4, 0)
    _, norm_back = jax.vjp(normalize, own_pooled)
    d_pooled = norm_back(d_normed)[0]
    own_cols = lax.dynamic_slice_in_dim(normed_bf, dp_index * 80, 80, 1)
    d_head = dot(own_cols, d_logits, 0, 0).astype(BF16)
    return (mixed_out, d_tokens, d_combine, d_w_in, d_w_out, image_loss, d_pooled, d_head)


def solution(mesh):
    grid = Mesh(mesh.devices.reshape(16, 2, 2, 2), ALL)
    rows = P(ALL, None)
    in_specs = (rows, rows, rows, P(None, ALL), rows, rows, P(None, EX), P("dp", None))
    out_specs = (
        rows,
        rows,
        rows,
        P(None, ALL),
        rows,
        P("dp"),
        P("dp", None),
        P("dp", EX),
    )
    return jax.shard_map(shards, mesh=grid, in_specs=in_specs, out_specs=out_specs, check_vma=False)
```

time: 692 us -> 283 us (0.41)
  blocking collectives: 325 us -> 38.9 us
  waiting for transfers between devices: 124 us -> 62.9 us
  local copies, waits for them, and re-layouts: 106 us -> 51 us
  starting transfers between devices: 16.6 us -> 35.2 us
  between operations: 14.8 us -> 2.53 us
  other arithmetic: 30.6 us -> 22.2 us
    psum x3 -> x1, blocking collectives: 236 us -> 2.47 us  [shards(): lax.psum(jnp.sum(mixed_out.astype(F32), axis=0), 'core') / PATCHES]
    all_to_all x1, blocking collectives: 89.6 us -> 36.4 us  [chip_swap(): lax.all_to_all(packed, CHIP, 0, 0, tiled=True).reshape(CHIPS * CAP, D)]
    all_to_all x2 -> x6, waiting for transfers between devices: 103 us -> 57.5 us  [the longest x3 45.7 us: chip_swap(): lax.all_to_all(packed, CHIP, 0, 0, tiled=True).reshape(CHIPS * CAP, D)]
    slice x2 -> x4, local copies, waits for them, and re-layouts: 40.5 us -> 0.96 us  [the longest x1 0.64 us: shards(): image_loss = total[40:44, 0]]
    unnamed x2 -> x0, waiting for transfers between devices: 21.2 us -> none
    reduce_sum x10 -> x8, other arithmetic: 23.1 us -> 3.76 us  [the longest x1 2.4 us: shards(): jnp.sum(grad_f * vals0, axis=1)]
    another operation x5 -> x0, local copies, waits for them, and re-layouts: 18.4 us -> none  [the longest x1 6.99 us: shards(): grad_rows = arrived[1].reshape(n_devices * capacity, D)]
    all_to_all x2 -> x6, starting transfers between devices: 16.5 us -> 33.9 us  [the longest x3 17 us: chip_swap(): lax.all_to_all(packed, CHIP, 0, 0, tiled=True).reshape(CHIPS * CAP, D)]
  transfers between devices with their start and end apart: 3 -> 10, of which waited for: 2 -> 7; matrix products, arithmetic and copies ran while one was open for 9% -> 24% of each run, Pallas kernels for 0% -> 0%
where the time goes in v1:
time: 283 us; the launch traced here: 278 us
  matrix products  65.4 us (23%)
  waiting for transfers between devices  62.9 us (22%)
  local copies, waits for them, and re-layouts  51 us (18%)
  blocking collectives  38.9 us (14%)
  starting transfers between devices  35.2 us (12%)
  other arithmetic  22.2 us (8%)
    dot_general x14, matrix products, dot(): lax.dot_general(a, b, (((ca,), (cb,)), ((), ())), preferred_element_type=...  65.4 us
    all_to_all x3, waiting for transfers between devices, chip_swap(): lax.all_to_all(packed, CHIP, 0, 0, tiled=True).reshape(CHIPS * CAP, D)  45.7 us
    all_to_all x1, blocking collectives, chip_swap(): lax.all_to_all(packed, CHIP, 0, 0, tiled=True).reshape(CHIPS * CAP, D)  36.4 us
    reshape x4, local copies, waits for them, and re-layouts, chip_swap(): lax.all_to_all(packed, CHIP, 0, 0, tiled=True).reshape(CHIPS * CAP, D)  18.9 us
    all_to_all x3, starting transfers between devices, chip_swap(): lax.all_to_all(packed, CHIP, 0, 0, tiled=True).reshape(CHIPS * CAP, D)  17 us
    reshape x4, local copies, waits for them, and re-layouts, chip_swap(): packed = rows.reshape(CHIPS, CAP // 2, 2, D)  15.3 us
    unnamed x30, local copies, waits for them, and re-layouts  9.84 us
    all_to_all x1, starting transfers between devices, shards(): lax.all_to_all(spread_out, CHIP, 0, 0, tiled=True).reshape(IMAGES, D)  9.65 us
  transfers between devices with their start and end apart: 10, of which 7 were waited for; matrix products, arithmetic and copies ran while one was open for 24% of the time, Pallas kernels for 0%

profile of v1, /device:TPU:0, one launch (start us, length us, event | category | flops | bytes accessed | tf_op | source)
XLA Modules:
  0.0 278.2 jit_solution(14977638610493692671)
XLA Ops:
  2.6 2.7 convolution_convert_fusion.4
  5.3 4.5 %reshape.231 = bf16[64,5,2,1280]{3,2,1,0:T(2,128)(2,1)} reshape(bf16[640,1280]{1,0:T(8,128)(2,1)} %convolution_convert_fusion.4) | data formatting | bytes 3276800 | tf_op jit(solution)/shard_map/reshape | solution.py:29
  9.9 36.4 %all_to_all.36 = bf16[64,5,2,1280]{3,2,1,0:T(2,128)(2,1)} all-to-all(bf16[64,5,2,1280]{3,2,1,0:T(2,128)(2,1)} %reshape.231), channel_id=1, replica_groups=mesh['dp'=16,'yh'=2,'yl'=2,'core'=2] {'dp','yh','yl'}, dimensions={0} | all-to-all | bytes 3276800 | tf_op jit(solution)/shard_map/all_to_all | solution.py:30
  46.3 4.7 %reshape.232 = bf16[640,1280]{1,0:T(8,128)(2,1)} reshape(bf16[64,5,2,1280]{3,2,1,0:T(2,128)(2,1)} %all_to_all.36) | data formatting | bytes 3276800 | tf_op jit(solution)/shard_map/reshape | solution.py:30
  51.2 1.7 constant_dynamic-update-slice_fusion.1
  52.9 2.0 collective-permute-done
  55.0 1.7 copy-done.3
  56.7 4.5 %fusion.63 = f32[1280,1280]{1,0:T(8,128)S(1)} fusion(bf16[1280,1280]{1,0:T(8,128)(2,1)S(1)} %constant_dynamic-update-slice_fusion, bf16[1280,1280]{1,0:T(8,128)(2,1)S(1)} %copy-done.10), kind=kOutput, calls=%fused_computation.155 | convolution fusion | flops 4194304000 | bytes 13107200 | tf_op jit(solution)/shard_map/dot_general | solution.py:25
  61.3 5.7 %fusion.62 = f32[1280,1280]{1,0:T(8,128)S(1)} fusion(bf16[1280,1280]{1,0:T(8,128)(2,1)S(1)} %copy-done, f32[1280,1280]{1,0:T(8,128)S(1)} %fusion.63), kind=kOutput, calls=%fused_computation.154 | convolution fusion | flops 4209049600 | bytes 16384000 | tf_op jit(solution)/shard_map/dot_general | solution.py:25
  67.4 3.4 %collective-permute-done.1 = bf16[640,1280]{1,0:T(8,128)(2,1)S(1)} collective-permute-done((bf16[640,1280]{1,0:T(8,128)(2,1)S(1)}, bf16[640,1280]{1,0:T(8,128)(2,1)S(1)}, u32[]{:S(2)}, u32[]{:S(2)}) %collective-permute-start.1) | collective-permute-done | bytes 1638432 | tf_op jit(solution)/shard_map/ppermute | solution.py:39
  70.7 1.6 fusion.8
  72.3 4.6 %reshape.233 = bf16[64,5,2,1280]{3,2,1,0:T(2,128)(2,1)} reshape(bf16[640,1280]{1,0:T(8,128)(2,1)} %fusion.8) | data formatting | bytes 3276800 | tf_op jit(solution)/shard_map/reshape | solution.py:29
  76.9 5.9 %all-to-all-start.1 = ((bf16[64,5,2,1280]{3,2,1,0:T(2,128)(2,1)}), bf16[64,5,2,1280]{3,2,1,0:T(2,128)(2,1)}, u32[]{:S(2)}, u32[]{:S(2)}) async-start(bf16[64,5,2,1280]{3,2,1,0:T(2,128)(2,1)} %reshape.233), calls=%async_computation.1 | async-start | bytes 3276800 | tf_op jit(solution)/shard_map/all_to_all | solution.py:30
  83.0 24.8 %all-to-all-done.1 = bf16[64,5,2,1280]{3,2,1,0:T(2,128)(2,1)} async-done(((bf16[64,5,2,1280]{3,2,1,0:T(2,128)(2,1)}), bf16[64,5,2,1280]{3,2,1,0:T(2,128)(2,1)}, u32[]{:S(2)}, u32[]{:S(2)}) %all-to-all-start.1) | async-done | bytes 1638432 | tf_op jit(solution)/shard_map/all_to_all | solution.py:30
  108.4 3.8 %all-to-all-start.4 = ((s32[16,1,16]{2,1,0:T(1,128)}), s32[16,1,16]{2,1,0:T(1,128)S(1)}, u32[]{:S(2)}, u32[]{:S(2)}) async-start(s32[16,1,16]{2,1,0:T(1,128)} %broadcast_in_dim.27), calls=%async_computation.4 | async-start | bytes 16384 | tf_op jit(solution)/shard_map/all_to_all | solution.py:112
  112.2 4.7 %reshape.234 = bf16[640,1280]{1,0:T(8,128)(2,1)} reshape(bf16[64,5,2,1280]{3,2,1,0:T(2,128)(2,1)} %all-to-all-done.1) | data formatting | bytes 3276800 | tf_op jit(solution)/shard_map/reshape | solution.py:30
  116.9 2.3 fusion.12
  119.2 2.4 fusion.19
  121.6 2.5 psum.7
  125.0 9.6 %all-to-all-start.5 = ((f32[64,10,128]{2,1,0:T(8,128)}), f32[64,10,128]{2,1,0:T(8,128)}, u32[]{:S(2)}, u32[]{:S(2)}) async-start(f32[64,10,128]{2,1,0:T(8,128)} %broadcast_in_dim.30), calls=%async_computation.5 | async-start | bytes 1048576 | tf_op jit(solution)/shard_map/all_to_all | solution.py:110
  134.6 2.9 %convolution_convert_fusion.3 = bf16[640,1280]{1,0:T(8,128)(2,1)} fusion(bf16[128,1280]{1,0:T(8,128)(2,1)} %get-tuple-element.35, bf16[128,1280]{1,0:T(8,128)(2,1)} %get-tuple-element.36, s32[256]{0:T(256)S(1)} %pad_add_fusion, s32[640]{0:T(1024)S(1)} %iota_subtract_fusion), kind=kOutput, calls=%fused_computation.19 | convolution fusion | flops 421724160 | bytes 2297344 | tf_op jit(solution)/shard_map/dot_general | solution.py:25
  137.5 4.6 %reshape.235 = bf16[64,5,2,1280]{3,2,1,0:T(2,128)(2,1)} reshape(bf16[640,1280]{1,0:T(8,128)(2,1)} %convolution_convert_fusion.3) | data formatting | bytes 3276800 | tf_op jit(solution)/shard_map/reshape | solution.py:29
  142.1 6.0 %all-to-all-done.5 = f32[64,10,128]{2,1,0:T(8,128)} async-done(((f32[64,10,128]{2,1,0:T(8,128)}), f32[64,10,128]{2,1,0:T(8,128)}, u32[]{:S(2)}, u32[]{:S(2)}) %all-to-all-start.5) | async-done | bytes 327712 | tf_op jit(solution)/shard_map/all_to_all | solution.py:110
  148.1 5.5 %all-to-all-start.2 = ((bf16[64,5,2,1280]{3,2,1,0:T(2,128)(2,1)}), bf16[64,5,2,1280]{3,2,1,0:T(2,128)(2,1)}, u32[]{:S(2)}, u32[]{:S(2)}) async-start(bf16[64,5,2,1280]{3,2,1,0:T(2,128)(2,1)} %reshape.235), calls=%async_computation.2 | async-start | bytes 3276800 | tf_op jit(solution)/shard_map/all_to_all | solution.py:30
  158.5 1.6 reduce_sum.186
  160.1 2.0 multiply_reduce_fusion
  162.1 15.2 %all-to-all-done.2 = bf16[64,5,2,1280]{3,2,1,0:T(2,128)(2,1)} async-done(((bf16[64,5,2,1280]{3,2,1,0:T(2,128)(2,1)}), bf16[64,5,2,1280]{3,2,1,0:T(2,128)(2,1)}, u32[]{:S(2)}, u32[]{:S(2)}) %all-to-all-start.2) | async-done | bytes 1638432 | tf_op jit(solution)/shard_map/all_to_all | solution.py:30
  177.3 4.7 %reshape.236 = bf16[640,1280]{1,0:T(8,128)(2,1)} reshape(bf16[64,5,2,1280]{3,2,1,0:T(2,128)(2,1)} %all-to-all-done.2) | data formatting | bytes 3276800 | tf_op jit(solution)/shard_map/reshape | solution.py:30
  182.4 1.9 multiply_convert_fusion.1
  184.3 4.7 %multiply_multiply_fusion.2 = (f32[64,2176]{1,0:T(8,128)S(1)}, bf16[64,2176]{1,0:T(8,128)(2,1)S(1)}, f32[64,2176]{1,0:T(8,128)S(1)}) fusion(f32[2176]{0:T(1024)S(1)} %multiply_divide_fusion, pred[64,2176]{1,0:T(8,128)(4,1)S(1)} %compare_reduce_fusion, bf16[64,1280]{1,0:T(8,128)(2,1)S(1)} %get-tuple-element.26, bf16[1280,2176]{1,0:T(8,128)(2,1)} %param.15), kind=kOutput, calls=%fused_computation.66 | convolution fusion | flops 362921984 | bytes 7275008 | tf_op jit(solution)/shard_map/dot_general | solution.py:25
  189.8 4.1 %fusion.44 = f32[4,1280]{1,0:T(4,128)S(1)} fusion(bf16[1280,2176]{1,0:T(8,128)(2,1)} %param.15, bf16[64,2176]{1,0:T(8,128)(2,1)S(1)} %get-tuple-element.33, s32[]{:T(128)S(6)} %select_n.72), kind=kOutput, calls=%fused_computation.97 | convolution fusion | flops 22282240 | bytes 5608452 | tf_op jit(solution)/shard_map/dot_general | solution.py:25
  193.9 2.1 convolution_convert_fusion.2
  197.5 1.5 constant_dynamic-update-slice_fusion.2
  199.1 1.7 copy-done.4
  200.8 10.5 %fusion.6 = bf16[1280,1280]{1,0:T(8,128)(2,1)S(1)} fusion(f32[1280,1280]{1,0:T(8,128)} %copy-done.12, bf16[1280,1280]{1,0:T(8,128)(2,1)S(1)} %constant_dynamic-update-slice_fusion.2, bf16[1280,1280]{1,0:T(8,128)(2,1)S(1)} %copy-done), kind=kOutput, calls=%fused_computation.10 | convolution fusion | flops 4227072000 | bytes 16384000 | tf_op jit(solution)/shard_map/dot_general | solution.py:25
  211.3 4.4 %fusion.64 = f32[1280,1280]{1,0:T(8,128)S(1)} fusion(bf16[1280,1280]{1,0:T(8,128)(2,1)S(1)} %fusion.6, bf16[1280,1280]{1,0:T(8,128)(2,1)S(1)} %copy-done.11), kind=kOutput, calls=%fused_computation.156 | convolution fusion | flops 4194304000 | bytes 13107200 | tf_op jit(solution)/shard_map/dot_general | solution.py:25
  215.8 2.7 copy-done.2
  220.0 3.4 %all-to-all-start.6 = ((f32[8,48,128]{2,1,0:T(8,128)}), f32[8,48,128]{2,1,0:T(8,128)S(1)}, u32[]{:S(2)}, u32[]{:S(2)}) async-start(f32[8,48,128]{2,1,0:T(8,128)} %broadcast_in_dim.33), calls=%async_computation.6 | async-start | bytes 393216 | tf_op jit(solution)/shard_map/all_to_all | solution.py:141
  224.3 5.8 %all-to-all-done.6 = f32[8,48,128]{2,1,0:T(8,128)S(1)} async-done(((f32[8,48,128]{2,1,0:T(8,128)}), f32[8,48,128]{2,1,0:T(8,128)S(1)}, u32[]{:S(2)}, u32[]{:S(2)}) %all-to-all-start.6) | async-done | bytes 196640 | tf_op jit(solution)/shard_map/all_to_all | solution.py:141
  234.9 2.3 fusion.7
  237.1 1.6 reshape.237
  238.7 5.7 %all-to-all-start.3 = ((bf16[64,5,2,1280]{3,2,1,0:T(2,128)(2,1)}), bf16[64,5,2,1280]{3,2,1,0:T(2,128)(2,1)}, u32[]{:S(2)}, u32[]{:S(2)}) async-start(bf16[64,5,2,1280]{3,2,1,0:T(2,128)(2,1)} %reshape.237), calls=%async_computation.3 | async-start | bytes 3276800 | tf_op jit(solution)/shard_map/all_to_all | solution.py:30
  244.4 9.2 %convolution_convert_fusion.1 = bf16[1280,1280]{1,0:T(8,128)(2,1)} fusion(bf16[1280,1280]{1,0:T(8,128)(2,1)} %copy-done.3, bf16[1280,1280]{1,0:T(8,128)(2,1)} %copy-done.13), kind=kOutput, calls=%fused_computation.3 | convolution fusion | flops 4195942400 | bytes 9830400 | tf_op jit(solution)/shard_map/dot_general | solution.py:25
  253.6 9.8 %convolution_convert_fusion = bf16[1280,1280]{1,0:T(8,128)(2,1)} fusion(bf16[1280,1280]{1,0:T(8,128)(2,1)S(1)} %copy-done.5, f32[1280,1280]{1,0:T(8,128)} %copy-done.12), kind=kOutput, calls=%fused_computation.2 | convolution fusion | flops 4210688000 | bytes 13107200 | tf_op jit(solution)/shard_map/dot_general | solution.py:25
  263.5 5.6 %all-to-all-done.3 = bf16[64,5,2,1280]{3,2,1,0:T(2,128)(2,1)} async-done(((bf16[64,5,2,1280]{3,2,1,0:T(2,128)(2,1)}), bf16[64,5,2,1280]{3,2,1,0:T(2,128)(2,1)}, u32[]{:S(2)}, u32[]{:S(2)}) %all-to-all-start.3) | async-done | bytes 1638432 | tf_op jit(solution)/shard_map/all_to_all | solution.py:30
  269.1 4.9 %reshape.238 = bf16[640,1280]{1,0:T(8,128)(2,1)} reshape(bf16[64,5,2,1280]{3,2,1,0:T(2,128)(2,1)} %all-to-all-done.3) | data formatting | bytes 3276800 | tf_op jit(solution)/shard_map/reshape | solution.py:30
  274.0 2.3 fusion.9
  276.2 1.8 fusion.18
  (87 shorter events, 17.7 us)
Async XLA Ops:
  0.6 60.6 %copy-start = (bf16[1280,1280]{1,0:T(8,128)(2,1)S(1)}, bf16[1280,1280]{1,0:T(8,128)(2,1)}, u32[]{:S(2)}) copy-start(bf16[1280,1280]{1,0:T(8,128)(2,1)} %param.13) | copy-start | bytes 9830404
  51.0 5.7 %copy-start.10 = (bf16[1280,1280]{1,0:T(8,128)(2,1)S(1)}, bf16[1280,1280]{1,0:T(8,128)(2,1)}, u32[]{:S(2)}) copy-start(bf16[1280,1280]{1,0:T(8,128)(2,1)} %param.12) | copy-start | bytes 9830404
  51.0 3.9 %collective-permute-start = (bf16[640,1280]{1,0:T(8,128)(2,1)}, bf16[640,1280]{1,0:T(8,128)(2,1)S(1)}, u32[]{:S(2)}, u32[]{:S(2)}) collective-permute-start(bf16[640,1280]{1,0:T(8,128)(2,1)} %reshape.232), channel_id=1, source_target_pairs={{0,1},{1,0},{2,3},{3,2},{4,5},{5,4},{6,7},{7,6},{8,9},{9,8},{10,11... | collective-permute-start | bytes 4915208 | tf_op jit(solution)/shard_map/ppermute | solution.py:34
  55.0 1.7 copy-start.3
  61.2 5.7 %copy-start.12 = (f32[1280,1280]{1,0:T(8,128)}, f32[1280,1280]{1,0:T(8,128)S(1)}, u32[]{:S(2)}) copy-start(f32[1280,1280]{1,0:T(8,128)S(1)} %fusion.63) | copy-start | bytes 19660804
  67.1 3.6 %collective-permute-start.1 = (bf16[640,1280]{1,0:T(8,128)(2,1)S(1)}, bf16[640,1280]{1,0:T(8,128)(2,1)S(1)}, u32[]{:S(2)}, u32[]{:S(2)}) collective-permute-start(bf16[640,1280]{1,0:T(8,128)(2,1)S(1)} %slice.115), channel_id=1, source_target_pairs={{0,1},{1,0},{2,3},{3,2},{4,5},{5,4},{6,7},{7,6},{8,9},{9,8},{10,11... | collective-permute-start | bytes 4915208 | tf_op jit(solution)/shard_map/ppermute | solution.py:39
  72.3 10.5 %copy-start.8 = (s32[4,4]{1,0:T(4,128)S(1)}, s32[4,4]{1,0:T(4,128)}, u32[]{:S(2)}) copy-start(s32[4,4]{1,0:T(4,128)} %param.16) | copy-start | bytes 196
  72.3 10.6 %copy-start.9 = (f32[128,2]{0,1:T(2,128)S(1)}, f32[128,2]{0,1:T(2,128)}, u32[]{:S(2)}) copy-start(f32[128,2]{0,1:T(2,128)} %param.11) | copy-start | bytes 3076
  76.9 30.9 %all-to-all-start.1 = ((bf16[64,5,2,1280]{3,2,1,0:T(2,128)(2,1)}), bf16[64,5,2,1280]{3,2,1,0:T(2,128)(2,1)}, u32[]{:S(2)}, u32[]{:S(2)}) async-start(bf16[64,5,2,1280]{3,2,1,0:T(2,128)(2,1)} %reshape.233), calls=%async_computation.1 | async-start | bytes 3276800 | tf_op jit(solution)/shard_map/all_to_all | solution.py:30
  108.4 15.7 %all-to-all-start.4 = ((s32[16,1,16]{2,1,0:T(1,128)}), s32[16,1,16]{2,1,0:T(1,128)S(1)}, u32[]{:S(2)}, u32[]{:S(2)}) async-start(s32[16,1,16]{2,1,0:T(1,128)} %broadcast_in_dim.27), calls=%async_computation.4 | async-start | bytes 16384 | tf_op jit(solution)/shard_map/all_to_all | solution.py:112
  125.0 23.1 %all-to-all-start.5 = ((f32[64,10,128]{2,1,0:T(8,128)}), f32[64,10,128]{2,1,0:T(8,128)}, u32[]{:S(2)}, u32[]{:S(2)}) async-start(f32[64,10,128]{2,1,0:T(8,128)} %broadcast_in_dim.30), calls=%async_computation.5 | async-start | bytes 1048576 | tf_op jit(solution)/shard_map/all_to_all | solution.py:110
  148.1 29.3 %all-to-all-start.2 = ((bf16[64,5,2,1280]{3,2,1,0:T(2,128)(2,1)}), bf16[64,5,2,1280]{3,2,1,0:T(2,128)(2,1)}, u32[]{:S(2)}, u32[]{:S(2)}) async-start(bf16[64,5,2,1280]{3,2,1,0:T(2,128)(2,1)} %reshape.235), calls=%async_computation.2 | async-start | bytes 3276800 | tf_op jit(solution)/shard_map/all_to_all | solution.py:30
  182.0 15.5 %collective-permute-start.2 = (bf16[640,1280]{1,0:T(8,128)(2,1)}, bf16[640,1280]{1,0:T(8,128)(2,1)}, u32[]{:S(2)}, u32[]{:S(2)}) collective-permute-start(bf16[640,1280]{1,0:T(8,128)(2,1)} %reshape.236), channel_id=1, source_target_pairs={{0,1},{1,0},{2,3},{3,2},{4,5},{5,4},{6,7},{7,6},{8,9},{9,8},{10,11... | collective-permute-start | bytes 4915208 | tf_op jit(solution)/shard_map/ppermute | solution.py:34
  184.3 4.7 %copy-start.7 = (bf16[64,1280]{1,0:T(8,128)(2,1)}, bf16[64,1280]{1,0:T(8,128)(2,1)S(1)}, u32[]{:S(2)}) copy-start(bf16[64,1280]{1,0:T(8,128)(2,1)S(1)} %get-tuple-element.26) | copy-start | bytes 491524
  189.0 0.7 copy-start.6
  199.1 1.7 copy-start.4
  200.8 10.5 %copy-start.11 = (bf16[1280,1280]{1,0:T(8,128)(2,1)S(1)}, bf16[1280,1280]{1,0:T(8,128)(2,1)}, u32[]{:S(2)}) copy-start(bf16[1280,1280]{1,0:T(8,128)(2,1)} %param.12) | copy-start | bytes 9830404
  211.3 4.5 %copy-start.13 = (bf16[1280,1280]{1,0:T(8,128)(2,1)}, bf16[1280,1280]{1,0:T(8,128)(2,1)S(1)}, u32[]{:S(2)}) copy-start(bf16[1280,1280]{1,0:T(8,128)(2,1)S(1)} %fusion.6) | copy-start | bytes 9830404
  215.8 2.7 copy-start.2
  218.6 16.2 %collective-permute-start.3 = (bf16[640,1280]{1,0:T(8,128)(2,1)S(1)}, bf16[640,1280]{1,0:T(8,128)(2,1)S(1)}, u32[]{:S(2)}, u32[]{:S(2)}) collective-permute-start(bf16[640,1280]{1,0:T(8,128)(2,1)S(1)} %slice.114), channel_id=1, source_target_pairs={{0,1},{1,0},{2,3},{3,2},{4,5},{5,4},{6,7},{7,6},{8,9},{9,8},{10,11... | collective-permute-start | bytes 4915208 | tf_op jit(solution)/shard_map/ppermute | solution.py:39
  220.0 10.2 %all-to-all-start.6 = ((f32[8,48,128]{2,1,0:T(8,128)}), f32[8,48,128]{2,1,0:T(8,128)S(1)}, u32[]{:S(2)}, u32[]{:S(2)}) async-start(f32[8,48,128]{2,1,0:T(8,128)} %broadcast_in_dim.33), calls=%async_computation.6 | async-start | bytes 393216 | tf_op jit(solution)/shard_map/all_to_all | solution.py:141
  238.7 30.4 %all-to-all-start.3 = ((bf16[64,5,2,1280]{3,2,1,0:T(2,128)(2,1)}), bf16[64,5,2,1280]{3,2,1,0:T(2,128)(2,1)}, u32[]{:S(2)}, u32[]{:S(2)}) async-start(bf16[64,5,2,1280]{3,2,1,0:T(2,128)(2,1)} %reshape.237), calls=%async_computation.3 | async-start | bytes 3276800 | tf_op jit(solution)/shard_map/all_to_all | solution.py:30
  244.4 9.3 %copy-start.5 = (bf16[1280,1280]{1,0:T(8,128)(2,1)S(1)}, bf16[1280,1280]{1,0:T(8,128)(2,1)}, u32[]{:S(2)}) copy-start(bf16[1280,1280]{1,0:T(8,128)(2,1)} %copy-done.4) | copy-start | bytes 9830404
  269.1 8.9 %copy-start.1 = (bf16[1280,1280]{1,0:T(8,128)(2,1)S(1)}, bf16[1280,1280]{1,0:T(8,128)(2,1)}, u32[]{:S(2)}) copy-start(bf16[1280,1280]{1,0:T(8,128)(2,1)} %param.13) | copy-start | bytes 9830404

commit v2 on v1

v2 whole, which is shorter than its diff:
```python
import jax
import jax.numpy as jnp
from jax import lax
from jax.experimental import pallas as pl
from jax.experimental.pallas import tpu as pltpu
from jax.sharding import Mesh, PartitionSpec as P

D = 1280
EXPERTS = 32
PATCHES = 256
CLASSES = 17408
CAP = 10
CHIPS = 64
IMAGES = 64
TOK = 128
HALF = CHIPS * CAP
ROWS = 2 * HALF
COLS = CLASSES // 8
BETA = 0.99
EPS = 1e-06

CHIP = ("dp", "yh", "yl")
Y = ("yh", "yl")
EX = ("yh", "yl", "core")
ALL = ("dp", "yh", "yl", "core")
SWAP = [(0, 1), (1, 0)]
F32 = jnp.float32
BF16 = jnp.bfloat16
I32 = jnp.int32
PACKED = (HALF // 2, 2, D)
ROOT_2_PI = 0.7978845608028654
CUBIC = 0.044715


def dot(a, b, ca, cb):
    return lax.dot_general(a, b, (((ca,), (cb,)), ((), ())), preferred_element_type=F32)


def shape(dims, dtype):
    return jax.ShapeDtypeStruct(dims, dtype)


VMEM = pl.BlockSpec(memory_space=pltpu.VMEM)
SMEM = pl.BlockSpec(memory_space=pltpu.SMEM)
ANY = pl.BlockSpec(memory_space=pl.ANY)


TINY = pl.CostEstimate(flops=1, transcendentals=0, bytes_accessed=1)


def run(body, outs, *args, specs=None, scratch=(), name=None):
    return pl.pallas_call(
        body,
        out_shape=outs,
        in_specs=specs or [VMEM] * len(args),
        out_specs=jax.tree.map(lambda _: VMEM, outs),
        scratch_shapes=list(scratch),
        name=name,
        cost_estimate=TINY,
        compiler_params=pltpu.CompilerParams(vmem_limit_bytes=56 << 20),
    )(*args)


def pack_rows(ref, value):
    ref[...] = value.astype(BF16).reshape(PACKED)


def x_body(routes_ref, tokens_ref, table_ref, send_ref):
    ids = lax.broadcasted_iota(I32, (TOK, EXPERTS), 1)
    r0, r1 = routes_ref[:, 0:1], routes_ref[:, 1:2]
    hit0, hit1 = r0 == ids, r1 == ids
    hits = jnp.where(hit0, 1.0, jnp.where(hit1, 1.0, 0.0)).astype(BF16)
    t_row = lax.broadcasted_iota(I32, (TOK, TOK), 0)
    t_col = lax.broadcasted_iota(I32, (TOK, TOK), 1)
    before = jnp.where(t_row > t_col, 1.0, 0.0).astype(BF16)
    earlier = dot(before, hits, 1, 0)
    col = lax.broadcasted_iota(I32, (TOK, HALF), 1)
    both = jnp.zeros((TOK, HALF), F32)
    for k, (route, hit) in enumerate(((r0, hit0), (r1, hit1))):
        pos = jnp.sum(jnp.where(hit, earlier, 0.0), axis=1, keepdims=True)
        row = route * (2 * CAP) + pos.astype(I32)
        table = jnp.where(col == row, 1.0, jnp.where(col == row + CAP, 1.0, 0.0))
        table_ref[k] = table.astype(BF16)
        both = both + table
    pack_rows(send_ref, dot(both.astype(BF16), tokens_ref[...], 0, 0))


def g_body(table_ref, grad_ref, combine_ref, send_ref):
    grad = grad_ref[...].astype(F32)
    rows = dot(table_ref[0], (combine_ref[:, 0:1] * grad).astype(BF16), 0, 0)
    rows = rows + dot(table_ref[1], (combine_ref[:, 1:2] * grad).astype(BF16), 0, 0)
    pack_rows(send_ref, rows)


CHUNK = 320


def fetch(pairs, sems):
    copies = [pltpu.make_async_copy(s, d, sems.at[i]) for i, (s, d) in enumerate(pairs)]
    for copy in copies:
        copy.start()
    return copies


def forward_body(x_own, x_other, w1_hbm, w2_hbm, xs, hidden, slope, own, other, w1, w2, sems):
    first, second = fetch(((w1_hbm, w1), (w2_hbm, w2)), sems)
    xs[:HALF] = x_own[...].reshape(HALF, D)
    xs[HALF:] = x_other[...].reshape(HALF, D)
    first.wait()
    second.wait()

    def step(i, carry):
        for base in (0, HALF):
            rows = pl.ds(pl.multiple_of(base + i * CHUNK, CHUNK), CHUNK)
            h = dot(xs[rows, :], w1[...], 1, 0)
            square = h * h
            bend = jnp.tanh(ROOT_2_PI * h * (1.0 + CUBIC * square))
            half = 0.5 * (1.0 + bend)
            act = (h * half).astype(BF16)
            hidden[rows, :] = act
            slope[rows, :] = (
                half
                + 0.5 * h * (1.0 - bend * bend) * (ROOT_2_PI * (1.0 + 3.0 * CUBIC * square))
            ).astype(BF16)
            part = dot(act, w2[...], 1, 0)
            out_rows = pl.ds(pl.multiple_of(i * CHUNK, CHUNK), CHUNK)
            if base == 0:
                own[out_rows, :] = part
            else:
                other[out_rows, :] = part.astype(BF16)
        return carry

    lax.fori_loop(0, HALF // CHUNK, step, 0)


def backward_body(g_own, g_other, slope, w1_hbm, w2_hbm, gs, d_pre, own, other, w1, w2, sems):
    second, first = fetch(((w2_hbm, w2), (w1_hbm, w1)), sems)
    gs[:HALF] = g_own[...].reshape(HALF, D)
    gs[HALF:] = g_other[...].reshape(HALF, D)
    second.wait()
    first.wait()

    def step(i, carry):
        for base in (0, HALF):
            rows = pl.ds(pl.multiple_of(base + i * CHUNK, CHUNK), CHUNK)
            d_h = dot(gs[rows, :], w2[...], 1, 1)
            act = (d_h * slope[rows, :].astype(F32)).astype(BF16)
            d_pre[rows, :] = act
            part = dot(act, w1[...], 1, 1)
            out_rows = pl.ds(pl.multiple_of(i * CHUNK, CHUNK), CHUNK)
            if base == 0:
                own[out_rows, :] = part
            else:
                other[out_rows, :] = part.astype(BF16)
        return carry

    lax.fori_loop(0, HALF // CHUNK, step, 0)


WEIGHTS = (
    pltpu.VMEM((D, D), BF16),
    pltpu.VMEM((D, D), BF16),
    pltpu.SemaphoreType.DMA((2,)),
)
SQUARE = (ROWS, D)


def add_body(own_ref, other_ref, send_ref):
    pack_rows(send_ref, own_ref[...] + other_ref[...].astype(F32))


def add_cores(own, other, name):
    there = lax.ppermute(other, "core", SWAP)
    return run(add_body, shape(PACKED, BF16), own, there, name=name)


def mixed_body(table_ref, in_ref, tokens_ref, grad_ref, combine_ref, mixed_ref, dc_ref, sum_ref):
    rows = in_ref[...].reshape(HALF, D)
    vals0 = dot(table_ref[0], rows, 1, 0)
    vals1 = dot(table_ref[1], rows, 1, 0)
    grad = grad_ref[...].astype(F32)
    dc_ref[:, 0:1] = jnp.sum(grad * vals0, axis=1, keepdims=True)
    dc_ref[:, 1:2] = jnp.sum(grad * vals1, axis=1, keepdims=True)
    mixed = (
        tokens_ref[...].astype(F32)
        + (combine_ref[:, 0:1] * vals0 + combine_ref[:, 1:2] * vals1)
    ).astype(BF16)
    mixed_ref[...] = mixed
    sum_ref[...] = jnp.sum(mixed.astype(F32), axis=0, keepdims=True)


def tokens_body(table_ref, in_ref, grad_ref, out_ref):
    rows = in_ref[...].reshape(HALF, D)
    table = table_ref[0].astype(F32) + table_ref[1].astype(F32)
    out_ref[...] = (grad_ref[...].astype(F32) + dot(table.astype(BF16), rows, 1, 0)).astype(BF16)


def in_order(here, parts, j):
    pick = parts[0]
    for shift in (1, 2, 3):
        pick = jnp.where((here + shift) % 4 == j, parts[shift], pick)
    return pick


def y_parts(mine):
    return [mine] + [
        lax.ppermute(mine, Y, [((i + shift) % 4, i) for i in range(4)]) for shift in (1, 2, 3)
    ]


def dp_gather(mine):
    for step in (1, 2, 4, 8):
        there = lax.ppermute(mine, "dp", [((i + step) % 16, i) for i in range(16)])
        mine = jnp.concatenate([mine, there], axis=0)
    return mine


def centered(pooled):
    away = pooled - jnp.mean(pooled, axis=1, keepdims=True)
    return away, lax.rsqrt(jnp.mean(away * away, axis=1, keepdims=True) + EPS)


def head_body(here_ref, p0, p1, p2, p3, target_ref, weight_ref, w_ref, pooled_ref, part_ref, send_ref):
    here = here_ref[0]
    parts = [p[...] for p in (p0, p1, p2, p3)]
    for j in range(4):
        pooled_ref[j : j + 1, :] = in_order(here, parts, j) * (1.0 / PATCHES)
    away, scale = centered(pooled_ref[...])
    normed = (away * scale).astype(BF16)
    logits = dot(normed, w_ref[...], 1, 0)
    hit = target_ref[...] > 0.5
    signed = jnp.where(hit, -logits, logits)
    small = jnp.exp(-jnp.abs(signed))
    nll = jnp.maximum(signed, 0.0) + jnp.log1p(small)
    inverse = 1.0 / (1.0 + small)
    miss = jnp.where(signed >= 0.0, 1.0, small) * inverse
    keep = jnp.where(signed >= 0.0, small, 1.0) * inverse
    weight = weight_ref[...]
    loss = jnp.sum(weight * (miss * miss) * nll, axis=1, keepdims=True)
    slope = weight * (2.0 * miss * keep * nll + miss * miss) * miss
    d_logits = jnp.where(hit, -slope, slope).astype(BF16)
    part_ref[:, :D] = dot(d_logits, w_ref[...], 1, 1)
    part_ref[:, D:] = jnp.broadcast_to(loss, (4, 128))
    zeros = jnp.zeros((4, 48), BF16)
    for d in range(16):
        send_ref[d, :, :COLS] = d_logits
        send_ref[d, :, COLS : COLS + 128] = jnp.concatenate(
            [normed[:, 80 * d : 80 * d + 80], zeros], axis=1
        )


def pooled_body(here_ref, m0, m1, m2, m3, pooled_ref, d_ref, loss_ref):
    here = here_ref[0]
    parts = [m[...] for m in (m0, m1, m2, m3)]
    total = in_order(here, parts, 0)
    for j in (1, 2, 3):
        total = total + in_order(here, parts, j)
    away, scale = centered(pooled_ref[...])
    normed = away * scale
    d_normed = total[:, :D]
    mean = jnp.mean(d_normed, axis=1, keepdims=True)
    along = jnp.mean(d_normed * normed, axis=1, keepdims=True)
    d_ref[...] = scale * (d_normed - mean - normed * along)
    loss_ref[...] = total[:, D:]


def effective_of(counts):
    return (1.0 - BETA) / (1.0 - jnp.power(BETA, counts + 1.0))


def label_terms(labels, flat):
    entry = jnp.arange(IMAGES * 4, dtype=I32)
    same = flat[:, None] == flat[None, :]
    sooner = entry[:, None] > entry[None, :]
    same_image = (entry[:, None] // 4) == (entry[None, :] // 4)
    fresh = ~jnp.any(same & sooner & same_image, axis=1)
    first = ~jnp.any(same & sooner, axis=1)
    entry_count = jnp.sum((same & fresh[None, :]).astype(F32), axis=1)
    distinct = jnp.sum(first.astype(F32))
    effective_total = (CLASSES - distinct) * effective_of(jnp.zeros((), F32)) + jnp.sum(
        jnp.where(first, effective_of(entry_count), 0.0)
    )
    class_ids = lax.axis_index(EX) * COLS + jnp.arange(COLS, dtype=I32)
    targets = jnp.any(labels[:, :, None] == class_ids[None, None, :], axis=1).astype(F32)
    counts = jnp.sum(((flat[:, None] == class_ids[None, :]) & fresh[:, None]).astype(F32), axis=0)
    return targets, (effective_of(counts) * CLASSES / effective_total).reshape(1, COLS)


def chip_swap(packed, after=None):
    packed = packed.reshape(CHIPS, CAP // 2, 2, D)
    if after is not None:
        packed, _ = lax.optimization_barrier((packed, after))
    return lax.all_to_all(packed, CHIP, 0, 0, tiled=True).reshape(PACKED)


def shards(tokens, routes, combine, w_in, w_out, out_grad, head_w, labels):
    here = lax.axis_index(Y).astype(I32).reshape(1)
    table, x_send = run(
        x_body,
        (shape((2, TOK, HALF), BF16), shape(PACKED, BF16)),
        routes,
        tokens,
        name="dispatch_x",
    )
    x_in = chip_swap(x_send)
    g_send = run(g_body, shape(PACKED, BF16), table, out_grad, combine, name="dispatch_g")
    all_labels = dp_gather(labels).reshape(IMAGES * 4)
    x_in, g_send, all_labels = lax.optimization_barrier((x_in, g_send, all_labels))
    targets, class_weight = label_terms(labels, all_labels)
    g_in = chip_swap(g_send)
    x_other = lax.ppermute(x_in, "core", SWAP)
    halves = (shape((HALF, D), F32), shape((HALF, D), BF16))
    whole = (shape(SQUARE, BF16), shape(SQUARE, BF16))
    xs, hidden, slope, own, other = run(
        forward_body,
        (*whole, shape(SQUARE, BF16), *halves),
        x_in,
        x_other,
        w_in,
        w_out,
        specs=[VMEM, VMEM, ANY, ANY],
        scratch=WEIGHTS,
        name="forward",
    )
    g_in, own, other, targets, class_weight = lax.optimization_barrier(
        (g_in, own, other, targets, class_weight)
    )
    out_send = add_cores(own, other, "add_out")
    out_in = chip_swap(out_send)
    g_other = lax.ppermute(g_in, "core", SWAP)
    gs, d_pre, own, other = run(
        backward_body,
        (*whole, *halves),
        g_in,
        g_other,
        slope,
        w_in,
        w_out,
        specs=[VMEM, VMEM, VMEM, ANY, ANY],
        scratch=WEIGHTS,
        name="backward",
    )
    out_in, own, other = lax.optimization_barrier((out_in, own, other))
    rows_send = add_cores(own, other, "add_rows")
    rows_in = chip_swap(rows_send)
    mixed_out, d_combine, token_sum = run(
        mixed_body,
        (shape((TOK, D), BF16), shape((TOK, 2), F32), shape((1, D), F32)),
        table,
        out_in,
        tokens,
        out_grad,
        combine,
        name="mixed",
    )
    sums = y_parts(lax.psum(token_sum, "core"))
    pooled, part, dp_send = run(
        head_body,
        (shape((4, D), F32), shape((4, D + 128), F32), shape((16, 4, COLS + 128), BF16)),
        here,
        *sums,
        targets,
        class_weight,
        head_w,
        specs=[SMEM] + [VMEM] * 7,
        name="head",
    )
    messages = y_parts(lax.psum(part, "core"))
    d_pooled, losses = run(
        pooled_body,
        (shape((4, D), F32), shape((4, 128), F32)),
        here,
        *messages,
        pooled,
        specs=[SMEM] + [VMEM] * 5,
        name="d_pooled",
    )
    dp_send, rows_in = lax.optimization_barrier((dp_send, rows_in))
    dp_in = lax.all_to_all(dp_send, "dp", 0, 0, tiled=True).reshape(IMAGES, COLS + 128)
    d_tokens = run(tokens_body, shape((TOK, D), BF16), table, rows_in, out_grad, name="d_tokens")
    d_w_out = dot(hidden, gs, 0, 0).astype(BF16)
    d_w_in = dot(xs, d_pre, 0, 0).astype(BF16)
    d_head = dot(dp_in[:, COLS : COLS + 80], dp_in[:, :COLS], 0, 0).astype(BF16)
    return (mixed_out, d_tokens, d_combine, d_w_in, d_w_out, losses[:, 0], d_pooled, d_head)


def solution(mesh):
    grid = Mesh(mesh.devices.reshape(16, 2, 2, 2), ALL)
    rows = P(ALL, None)
    in_specs = (rows, rows, rows, P(None, ALL), rows, rows, P(None, EX), P("dp", None))
    out_specs = (
        rows,
        rows,
        rows,
        P(None, ALL),
        rows,
        P("dp"),
        P("dp", None),
        P("dp", EX),
    )
    return jax.shard_map(shards, mesh=grid, in_specs=in_specs, out_specs=out_specs, check_vma=False)
```

time: 283 us -> 207 us (0.73); the launches traced: 278 us -> 206 us
  Pallas kernels: 0 us -> 63.5 us
  matrix products: 65.4 us -> 19.2 us
  local copies, waits for them, and re-layouts: 51 us -> 8.79 us
  blocking collectives: 38.9 us -> 6.6 us
  starting transfers between devices: 35.2 us -> 65.3 us
  waiting for transfers between devices: 62.9 us -> 37.6 us
  other arithmetic: 22.2 us -> 2.56 us
    pallas_call x0 -> x10, Pallas kernels: none -> 63.5 us  [run(): pl.pallas_call(body, out_shape=outs, in_specs=specs or [VMEM] * len(args)...]
    all_to_all x6 -> x5, waiting for transfers between devices: 57.5 us -> 11.2 us  [the longest x4 11.2 us: chip_swap(): return lax.all_to_all(packed, CHIP, 0, 0, tiled=True).reshape(PACKED)]
    dot_general x14 -> x3, matrix products: 65.4 us -> 19.2 us  [dot(): lax.dot_general(a, b, (((ca,), (cb,)), ((), ())), preferred_element_type=...]
    all_to_all x1 -> x0, blocking collectives: 36.4 us -> none  [chip_swap(): lax.all_to_all(packed, CHIP, 0, 0, tiled=True).reshape(CHIPS * CAP, D)]
    reshape x10 -> x2, local copies, waits for them, and re-layouts: 34.3 us -> 0.18 us  [the longest x1 0.1 us: shards(): all_labels = dp_gather(labels).reshape(IMAGES * 4)]
    ppermute x4 -> x14, starting transfers between devices: 1.33 us -> 23.4 us  [the longest x4 13.7 us: dp_gather(): there = lax.ppermute(mine, 'dp', [((i + step) % 16, i) for i in range(16)])]
    ppermute x4 -> x14, waiting for transfers between devices: 5.38 us -> 26.4 us  [the longest x4 17.1 us: dp_gather(): there = lax.ppermute(mine, 'dp', [((i + step) % 16, i) for i in range(16)])]
    reduce_sum x13 -> x3, other arithmetic: 10.2 us -> 1.26 us  [the longest x1 0.62 us: label_terms(): jnp.sum(jnp.where(first, effective_of(entry_count), 0.0))]
  transfers between devices with their start and end apart: 10 -> 19, of which waited for: 7 -> 7; matrix products, arithmetic and copies ran while one was open for 24% -> 12% of each run, Pallas kernels for 0% -> 27%
where the time goes in v2:
time: 207 us; the launch traced here: 206 us
  starting transfers between devices  65.3 us (32%)
  Pallas kernels  63.5 us (31%)
  waiting for transfers between devices  37.6 us (18%)
  matrix products  19.2 us (9%)
  local copies, waits for them, and re-layouts  8.79 us (4%)
  blocking collectives  6.6 us (3%)
  other arithmetic  2.56 us (1%)
  between operations  2.22 us (1%)
    pallas_call x10, Pallas kernels, run(): pl.pallas_call(body, out_shape=outs, in_specs=specs or [VMEM] * len(args)...  63.5 us
    all_to_all x4, starting transfers between devices, chip_swap(): return lax.all_to_all(packed, CHIP, 0, 0, tiled=True).reshape(PACKED)  34.3 us
    dot_general x3, matrix products, dot(): lax.dot_general(a, b, (((ca,), (cb,)), ((), ())), preferred_element_type=...  19.2 us
    ppermute x4, waiting for transfers between devices, dp_gather(): there = lax.ppermute(mine, 'dp', [((i + step) % 16, i) for i in range(16)])  17.1 us
    ppermute x4, starting transfers between devices, dp_gather(): there = lax.ppermute(mine, 'dp', [((i + step) % 16, i) for i in range(16)])  13.7 us
    all_to_all x4, waiting for transfers between devices, chip_swap(): return lax.all_to_all(packed, CHIP, 0, 0, tiled=True).reshape(PACKED)  11.2 us
    ppermute x2, waiting for transfers between devices, add_cores(): there = lax.ppermute(other, 'core', SWAP)  9.22 us
    ppermute x6, starting transfers between devices, y_parts(): lax.ppermute(mine, Y, [((i + shift) % 4, i) for i in range(4)])  9.16 us
  transfers between devices with their start and end apart: 19, of which 7 were waited for; matrix products, arithmetic and copies ran while one was open for 12% of the time, Pallas kernels for 27%

profile of v2, /device:TPU:0, one launch (start us, length us, event | category | flops | bytes accessed | tf_op | source)
XLA Modules:
  0.0 205.9 jit_solution(18150653873575938300)
XLA Ops:
  0.7 1.4 copy.34.routes_ref
  2.1 3.4 %dispatch_x.1 = (bf16[2,128,640]{2,1,0:T(8,128)(2,1)}, bf16[320,2,1280]{2,1,0:T(2,128)(2,1)}) custom-call(s32[128,2]{1,0:T(8,128)} %copy.34.routes_ref, bf16[128,1280]{1,0:T(8,128)(2,1)} %tokens_ref.3), custom_call_target="tpu_custom_call" | custom-call | flops 1 | bytes 1 | tf_op jit(solution)/shard_map/dispatch_x/pallas_call | solution.py:52
  5.5 11.5 %all-to-all-start = ((bf16[64,5,2,1280]{3,2,1,0:T(2,128)(2,1)}), bf16[64,5,2,1280]{3,2,1,0:T(2,128)(2,1)S(1)}, u32[]{:S(2)}, u32[]{:S(2)}) async-start(bf16[64,5,2,1280]{3,2,1,0:T(2,128)(2,1)} %bitcast.22), calls=%async_computation | async-start | bytes 3276800 | tf_op jit(solution)/shard_map/all_to_all | solution.py:293
  17.1 5.2 %collective-permute-start = (s32[4,4]{0,1:T(4,128)S(1)}, s32[4,4]{0,1:T(4,128)S(1)}, u32[]{:S(2)}, u32[]{:S(2)}) collective-permute-start(s32[4,4]{0,1:T(4,128)S(1)} %copy.40), channel_id=1, source_target_pairs={{8,0},{16,8},{24,16},{32,24},{40,32},{48,40},{56,48},{64,56},{72,6... | collective-permute-start | bytes 200 | tf_op jit(solution)/shard_map/ppermute | solution.py:213
  22.3 13.8 %collective-permute-done = s32[4,4]{0,1:T(4,128)S(1)} collective-permute-done((s32[4,4]{0,1:T(4,128)S(1)}, s32[4,4]{0,1:T(4,128)S(1)}, u32[]{:S(2)}, u32[]{:S(2)}) %collective-permute-start) | collective-permute-done | bytes 96 | tf_op jit(solution)/shard_map/ppermute | solution.py:213
  36.2 5.1 %collective-permute-start.1 = (s32[8,4]{0,1:T(4,128)S(1)}, s32[8,4]{0,1:T(4,128)S(1)}, u32[]{:S(2)}, u32[]{:S(2)}) collective-permute-start(s32[8,4]{0,1:T(4,128)S(1)} %pad_add_fusion), channel_id=1, source_target_pairs={{16,0},{24,8},{32,16},{40,24},{48,32},{56,40},{64,48},{72,56},{80,... | collective-permute-start | bytes 392 | tf_op jit(solution)/shard_map/ppermute | solution.py:213
  41.3 1.3 collective-permute-done.1
  42.7 1.6 collective-permute-start.2
  44.3 2.0 collective-permute-done.2
  46.3 1.8 collective-permute-start.3
  48.2 0.7 copy.35.combine_ref
  48.9 3.5 %dispatch_g.1 = bf16[320,2,1280]{2,1,0:T(2,128)(2,1)} custom-call(bf16[2,128,640]{2,1,0:T(8,128)(2,1)} %get-tuple-element.40.table_ref, bf16[128,1280]{1,0:T(8,128)(2,1)} %grad_ref.5, f32[128,2]{1,0:T(8,128)} %copy.35.combine_ref), custom_call_target="tpu_custom_call" | custom-call | flops 1 | bytes 1 | tf_op jit(solution)/shard_map/dispatch_g/pallas_call | solution.py:52
  52.8 11.1 %all-to-all-start.1 = ((bf16[64,5,2,1280]{3,2,1,0:T(2,128)(2,1)}), bf16[64,5,2,1280]{3,2,1,0:T(2,128)(2,1)S(1)}, u32[]{:S(2)}, u32[]{:S(2)}) async-start(bf16[64,5,2,1280]{3,2,1,0:T(2,128)(2,1)} %bitcast.17), calls=%async_computation.1 | async-start | bytes 3276800 | tf_op jit(solution)/shard_map/all_to_all | solution.py:293
  64.1 0.6 convert_element_type.21.target_ref
  65.2 0.6 fusion.4
  67.6 0.6 reshape.185.weight_ref
  68.2 17.4 %forward.1 = (bf16[1280,1280]{1,0:T(8,128)(2,1)}, bf16[1280,1280]{1,0:T(8,128)(2,1)}, bf16[1280,1280]{1,0:T(8,128)(2,1)}, f32[640,1280]{1,0:T(8,128)}, bf16[640,1280]{1,0:T(8,128)(2,1)}) custom-call(bf16[320,2,1280]{2,1,0:T(2,128)(2,1)} %bitcast.14, bf16[320,2,1280]{2,1,0:T(2,128)(2,1)} %collective-permute-done.4.x_other, bf16[1280,1280]{1,0:T(8,128)(2,1)} %w1_hbm.3, ...), custom_call_target="tpu_custom_call" | custom-call | flops 1 | bytes 1 | tf_op jit(solution)/shard_map/forward/pallas_call | solution.py:52
  85.6 3.6 %all-to-all-done.1 = bf16[64,5,2,1280]{3,2,1,0:T(2,128)(2,1)S(1)} async-done(((bf16[64,5,2,1280]{3,2,1,0:T(2,128)(2,1)}), bf16[64,5,2,1280]{3,2,1,0:T(2,128)(2,1)S(1)}, u32[]{:S(2)}, u32[]{:S(2)}) %all-to-all-start.1) | async-done | bytes 1638432 | tf_op jit(solution)/shard_map/all_to_all | solution.py:293
  89.7 5.5 %collective-permute-done.5.other_ref = bf16[640,1280]{1,0:T(8,128)(2,1)S(1)} collective-permute-done((bf16[640,1280]{1,0:T(8,128)(2,1)}, bf16[640,1280]{1,0:T(8,128)(2,1)S(1)}, u32[]{:S(2)}, u32[]{:S(2)}) %collective-permute-start.5) | collective-permute-done | bytes 1638432 | tf_op jit(solution)/shard_map/ppermute | solution.py:173
  95.2 1.2 copy-done.4
  96.4 4.1 %add_out.1 = bf16[320,2,1280]{2,1,0:T(2,128)(2,1)} custom-call(f32[640,1280]{1,0:T(8,128)} %get-tuple-element.47.own_ref, bf16[640,1280]{1,0:T(8,128)(2,1)} %copy-done.4), custom_call_target="tpu_custom_call" | custom-call | flops 1 | bytes 1 | tf_op jit(solution)/shard_map/add_out/pallas_call | solution.py:52
  100.5 6.0 %all-to-all-start.2 = ((bf16[64,5,2,1280]{3,2,1,0:T(2,128)(2,1)}), bf16[64,5,2,1280]{3,2,1,0:T(2,128)(2,1)S(1)}, u32[]{:S(2)}, u32[]{:S(2)}) async-start(bf16[64,5,2,1280]{3,2,1,0:T(2,128)(2,1)} %bitcast.21), calls=%async_computation.2 | async-start | bytes 3276800 | tf_op jit(solution)/shard_map/all_to_all | solution.py:293
  106.5 17.2 %backward.1 = (bf16[1280,1280]{1,0:T(8,128)(2,1)}, bf16[1280,1280]{1,0:T(8,128)(2,1)}, f32[640,1280]{1,0:T(8,128)}, bf16[640,1280]{1,0:T(8,128)(2,1)}) custom-call(bf16[320,2,1280]{2,1,0:T(2,128)(2,1)} %bitcast.16, bf16[320,2,1280]{2,1,0:T(2,128)(2,1)} %collective-permute-done.6.g_other, bf16[1280,1280]{1,0:T(8,128)(2,1)} %get-tuple-element.50.slope, ...), custom_call_target="tpu_custom_call" | custom-call | flops 1 | bytes 1 | tf_op jit(solution)/shard_map/backward/pallas_call | solution.py:52
  123.8 7.7 %all-to-all-done.2 = bf16[64,5,2,1280]{3,2,1,0:T(2,128)(2,1)S(1)} async-done(((bf16[64,5,2,1280]{3,2,1,0:T(2,128)(2,1)}), bf16[64,5,2,1280]{3,2,1,0:T(2,128)(2,1)S(1)}, u32[]{:S(2)}, u32[]{:S(2)}) %all-to-all-start.2) | async-done | bytes 1638432 | tf_op jit(solution)/shard_map/all_to_all | solution.py:293
  131.4 3.7 %collective-permute-done.10.other_ref = bf16[640,1280]{1,0:T(8,128)(2,1)S(1)} collective-permute-done((bf16[640,1280]{1,0:T(8,128)(2,1)}, bf16[640,1280]{1,0:T(8,128)(2,1)S(1)}, u32[]{:S(2)}, u32[]{:S(2)}) %collective-permute-start.10) | collective-permute-done | bytes 1638432 | tf_op jit(solution)/shard_map/ppermute | solution.py:173
  135.2 1.2 copy-done.5
  136.4 4.1 %add_rows.1 = bf16[320,2,1280]{2,1,0:T(2,128)(2,1)} custom-call(f32[640,1280]{1,0:T(8,128)} %get-tuple-element.59.own_ref, bf16[640,1280]{1,0:T(8,128)(2,1)} %copy-done.5), custom_call_target="tpu_custom_call" | custom-call | flops 1 | bytes 1 | tf_op jit(solution)/shard_map/add_rows/pallas_call | solution.py:52
  140.4 5.7 %all-to-all-start.3 = ((bf16[64,5,2,1280]{3,2,1,0:T(2,128)(2,1)}), bf16[64,5,2,1280]{3,2,1,0:T(2,128)(2,1)S(1)}, u32[]{:S(2)}, u32[]{:S(2)}) async-start(bf16[64,5,2,1280]{3,2,1,0:T(2,128)(2,1)} %bitcast.19), calls=%async_computation.3 | async-start | bytes 3276800 | tf_op jit(solution)/shard_map/all_to_all | solution.py:293
  146.2 3.3 %mixed.1 = (bf16[128,1280]{1,0:T(8,128)(2,1)}, f32[128,2]{1,0:T(8,128)}, f32[1,1280]{1,0:T(1,128)}) custom-call(bf16[2,128,640]{2,1,0:T(8,128)(2,1)} %get-tuple-element.40.table_ref, bf16[320,2,1280]{2,1,0:T(2,128)(2,1)} %bitcast.20, bf16[128,1280]{1,0:T(8,128)(2,1)} %tokens_ref.3, bf16[128,1280]{1,0:T(8,128)(2,1)} %grad_ref.5, f32[128,2]{1,0:T(8,128)} %copy.35.combine_ref), custom_call_target="tpu_custom_call" | custom-call | flops 1 | bytes 1 | tf_op jit(solution)/shard_map/mixed/pallas_call | solution.py:52
  149.5 2.6 %psum.14.p0 = f32[1,1280]{1,0:T(1,128)S(1)} all-reduce(f32[1,1280]{1,0:T(1,128)} %get-tuple-element.55), channel_id=1, replica_groups=mesh['dp'=16,'yh'=2,'yl'=2,'core'=2] {'core'}, use_global_device_ids=true, to_apply=%region_7.8 | all-reduce | flops 1280 | bytes 10240 | tf_op jit(solution)/shard_map/psum | solution.py:356
  152.1 1.6 collective-permute-start.9
  153.7 2.7 %collective-permute-start.8 = (f32[1,1280]{1,0:T(1,128)S(1)}, f32[1,1280]{1,0:T(1,128)S(1)}, u32[]{:S(2)}, u32[]{:S(2)}) collective-permute-start(f32[1,1280]{1,0:T(1,128)S(1)} %psum.14.p0), channel_id=1, source_target_pairs={{4,0},{6,2},{0,4},{2,6},{5,1},{7,3},{1,5},{3,7},{12,8},{14,10},{8,... | collective-permute-start | bytes 15368 | tf_op jit(solution)/shard_map/ppermute | solution.py:207
  156.4 1.5 collective-permute-start.7
  157.8 9.1 %convolution_convert_fusion = bf16[1280,1280]{1,0:T(8,128)(2,1)} fusion(bf16[1280,1280]{1,0:T(8,128)(2,1)} %get-tuple-element.65, bf16[1280,1280]{1,0:T(8,128)(2,1)} %get-tuple-element.66), kind=kOutput, calls=%fused_computation | convolution fusion | flops 4195942400 | bytes 9830400 | tf_op jit(solution)/shard_map/dot_general | solution.py:36
  167.0 0.5 copy-done.13
  167.6 5.9 %head.1 = (f32[4,1280]{1,0:T(4,128)}, f32[4,1408]{1,0:T(4,128)}, bf16[16,4,2304]{2,1,0:T(4,128)(2,1)}) custom-call(s32[1]{0:T(128)} %bitcast.6.here_ref, f32[1,1280]{1,0:T(1,128)} %copy-done.11, f32[1,1280]{1,0:T(1,128)} %copy-done.15, f32[1,1280]{1,0:T(1,128)} %copy-done.14, f32[1,1280]{1,0:T(1,128)} %copy-done.13, ...), custom_call_target="tpu_custom_call" | custom-call | flops 1 | bytes 1 | tf_op jit(solution)/shard_map/head/pallas_call | solution.py:52
  173.5 4.0 %psum.15.m0 = f32[4,1408]{1,0:T(4,128)S(1)} all-reduce(f32[4,1408]{1,0:T(4,128)} %get-tuple-element.67), channel_id=1, replica_groups=mesh['dp'=16,'yh'=2,'yl'=2,'core'=2] {'core'}, use_global_device_ids=true, to_apply=%region_8.9 | all-reduce | flops 5632 | bytes 45056 | tf_op jit(solution)/shard_map/psum | solution.py:368
  177.5 0.6 collective-permute-start.13
  178.1 0.9 collective-permute-start.12
  179.0 1.9 collective-permute-start.11
  180.9 7.6 %all-to-all-start.4 = ((bf16[16,4,2304]{2,1,0:T(4,128)(2,1)}), bf16[16,4,2304]{2,1,0:T(4,128)(2,1)S(1)}, u32[]{:S(2)}, u32[]{:S(2)}) async-start(bf16[16,4,2304]{2,1,0:T(4,128)(2,1)} %get-tuple-element.71), calls=%async_computation.4 | async-start | bytes 589824 | tf_op jit(solution)/shard_map/all_to_all | solution.py:379
  188.5 9.1 %convolution_convert_fusion.1 = bf16[1280,1280]{1,0:T(8,128)(2,1)} fusion(bf16[1280,1280]{1,0:T(8,128)(2,1)} %get-tuple-element.63, bf16[1280,1280]{1,0:T(8,128)(2,1)} %get-tuple-element.64), kind=kOutput, calls=%fused_computation.1 | convolution fusion | flops 4195942400 | bytes 9830400 | tf_op jit(solution)/shard_map/dot_general | solution.py:36
  197.7 0.6 copy.43
  198.4 0.6 copy-done.8
  199.0 1.7 d_pooled.1
  200.7 1.3 slice_reduce_fusion
  202.0 2.8 %d_tokens.1 = bf16[128,1280]{1,0:T(8,128)(2,1)} custom-call(bf16[2,128,640]{2,1,0:T(8,128)(2,1)} %get-tuple-element.40.table_ref, bf16[320,2,1280]{2,1,0:T(2,128)(2,1)} %bitcast.18, bf16[128,1280]{1,0:T(8,128)(2,1)} %grad_ref.5), custom_call_target="tpu_custom_call" | custom-call | flops 1 | bytes 1 | tf_op jit(solution)/shard_map/d_tokens/pallas_call | solution.py:52
  204.8 1.0 convolution_convert_fusion.2
  (62 shorter events, 2.6 us)
Async XLA Ops:
  0.6 16.4 %copy-start.12 = (s32[4,4]{1,0:T(4,128)S(1)}, s32[4,4]{1,0:T(4,128)}, u32[]{:S(2)}) copy-start(s32[4,4]{1,0:T(4,128)} %param.15) | copy-start | bytes 196
  0.6 47.5 %copy-start.16 = (f32[128,2]{0,1:T(2,128)S(1)}, f32[128,2]{0,1:T(2,128)}, u32[]{:S(2)}) copy-start(f32[128,2]{0,1:T(2,128)} %param.10) | copy-start | bytes 3076
  5.5 47.2 %all-to-all-start = ((bf16[64,5,2,1280]{3,2,1,0:T(2,128)(2,1)}), bf16[64,5,2,1280]{3,2,1,0:T(2,128)(2,1)S(1)}, u32[]{:S(2)}, u32[]{:S(2)}) async-start(bf16[64,5,2,1280]{3,2,1,0:T(2,128)(2,1)} %bitcast.22), calls=%async_computation | async-start | bytes 3276800 | tf_op jit(solution)/shard_map/all_to_all | solution.py:293
  17.1 19.0 %collective-permute-start = (s32[4,4]{0,1:T(4,128)S(1)}, s32[4,4]{0,1:T(4,128)S(1)}, u32[]{:S(2)}, u32[]{:S(2)}) collective-permute-start(s32[4,4]{0,1:T(4,128)S(1)} %copy.40), channel_id=1, source_target_pairs={{8,0},{16,8},{24,16},{32,24},{40,32},{48,40},{56,48},{64,56},{72,6... | collective-permute-start | bytes 200 | tf_op jit(solution)/shard_map/ppermute | solution.py:213
  36.2 6.4 %collective-permute-start.1 = (s32[8,4]{0,1:T(4,128)S(1)}, s32[8,4]{0,1:T(4,128)S(1)}, u32[]{:S(2)}, u32[]{:S(2)}) collective-permute-start(s32[8,4]{0,1:T(4,128)S(1)} %pad_add_fusion), channel_id=1, source_target_pairs={{16,0},{24,8},{32,16},{40,24},{48,32},{56,40},{64,48},{72,56},{80,... | collective-permute-start | bytes 392 | tf_op jit(solution)/shard_map/ppermute | solution.py:213
  42.7 3.6 %collective-permute-start.2 = (s32[16,4]{0,1:T(4,128)S(1)}, s32[16,4]{0,1:T(4,128)S(1)}, u32[]{:S(2)}, u32[]{:S(2)}) collective-permute-start(s32[16,4]{0,1:T(4,128)S(1)} %pad_add_fusion.1), channel_id=1, source_target_pairs={{32,0},{40,8},{48,16},{56,24},{64,32},{72,40},{80,48},{88,56},{96,... | collective-permute-start | bytes 776 | tf_op jit(solution)/shard_map/ppermute | solution.py:213
  46.3 6.1 %collective-permute-start.3 = (s32[32,4]{0,1:T(4,128)S(1)}, s32[32,4]{0,1:T(4,128)S(1)}, u32[]{:S(2)}, u32[]{:S(2)}) collective-permute-start(s32[32,4]{0,1:T(4,128)S(1)} %pad_add_fusion.2), channel_id=1, source_target_pairs={{64,0},{72,8},{80,16},{88,24},{96,32},{104,40},{112,48},{120,56},{... | collective-permute-start | bytes 1544 | tf_op jit(solution)/shard_map/ppermute | solution.py:213
  52.7 15.5 %copy-start = (bf16[64,5,2,1280]{3,2,1,0:T(2,128)(2,1)}, bf16[64,5,2,1280]{3,2,1,0:T(2,128)(2,1)S(1)}, u32[]{:S(2)}) copy-start(bf16[64,5,2,1280]{3,2,1,0:T(2,128)(2,1)S(1)} %all-to-all-done) | copy-start | bytes 4915204
  52.7 15.4 %collective-permute-start.4 = (bf16[320,2,1280]{2,1,0:T(2,128)(2,1)S(1)}, bf16[320,2,1280]{2,1,0:T(2,128)(2,1)}, u32[]{:S(2)}, u32[]{:S(2)}) collective-permute-start(bf16[320,2,1280]{2,1,0:T(2,128)(2,1)S(1)} %bitcast.13), channel_id=1, source_target_pairs={{0,1},{1,0},{2,3},{3,2},{4,5},{5,4},{6,7},{7,6},{8,9},{9,8},{10,11... | collective-permute-start | bytes 4915208 | tf_op jit(solution)/shard_map/ppermute | solution.py:311
  52.8 36.4 %all-to-all-start.1 = ((bf16[64,5,2,1280]{3,2,1,0:T(2,128)(2,1)}), bf16[64,5,2,1280]{3,2,1,0:T(2,128)(2,1)S(1)}, u32[]{:S(2)}, u32[]{:S(2)}) async-start(bf16[64,5,2,1280]{3,2,1,0:T(2,128)(2,1)} %bitcast.17), calls=%async_computation.1 | async-start | bytes 3276800 | tf_op jit(solution)/shard_map/all_to_all | solution.py:293
  89.2 11.3 %copy-start.1 = (bf16[64,5,2,1280]{3,2,1,0:T(2,128)(2,1)}, bf16[64,5,2,1280]{3,2,1,0:T(2,128)(2,1)S(1)}, u32[]{:S(2)}) copy-start(bf16[64,5,2,1280]{3,2,1,0:T(2,128)(2,1)S(1)} %all-to-all-done.1) | copy-start | bytes 4915204
  89.2 6.0 %collective-permute-start.5 = (bf16[640,1280]{1,0:T(8,128)(2,1)}, bf16[640,1280]{1,0:T(8,128)(2,1)S(1)}, u32[]{:S(2)}, u32[]{:S(2)}) collective-permute-start(bf16[640,1280]{1,0:T(8,128)(2,1)} %get-tuple-element.48), channel_id=1, source_target_pairs={{0,1},{1,0},{2,3},{3,2},{4,5},{5,4},{6,7},{7,6},{8,9},{9,8},{10,11... | collective-permute-start | bytes 4915208 | tf_op jit(solution)/shard_map/ppermute | solution.py:173
  89.2 17.3 %collective-permute-start.6 = (bf16[320,2,1280]{2,1,0:T(2,128)(2,1)S(1)}, bf16[320,2,1280]{2,1,0:T(2,128)(2,1)}, u32[]{:S(2)}, u32[]{:S(2)}) collective-permute-start(bf16[320,2,1280]{2,1,0:T(2,128)(2,1)S(1)} %bitcast.15), channel_id=1, source_target_pairs={{0,1},{1,0},{2,3},{3,2},{4,5},{5,4},{6,7},{7,6},{8,9},{9,8},{10,11... | collective-permute-start | bytes 4915208 | tf_op jit(solution)/shard_map/ppermute | solution.py:330
  95.2 1.2 copy-start.4
  100.5 30.9 %all-to-all-start.2 = ((bf16[64,5,2,1280]{3,2,1,0:T(2,128)(2,1)}), bf16[64,5,2,1280]{3,2,1,0:T(2,128)(2,1)S(1)}, u32[]{:S(2)}, u32[]{:S(2)}) async-start(bf16[64,5,2,1280]{3,2,1,0:T(2,128)(2,1)} %bitcast.21), calls=%async_computation.2 | async-start | bytes 3276800 | tf_op jit(solution)/shard_map/all_to_all | solution.py:293
  131.4 9.0 %copy-start.3 = (bf16[64,5,2,1280]{3,2,1,0:T(2,128)(2,1)}, bf16[64,5,2,1280]{3,2,1,0:T(2,128)(2,1)S(1)}, u32[]{:S(2)}) copy-start(bf16[64,5,2,1280]{3,2,1,0:T(2,128)(2,1)S(1)} %all-to-all-done.2) | copy-start | bytes 4915204
  131.4 3.7 %collective-permute-start.10 = (bf16[640,1280]{1,0:T(8,128)(2,1)}, bf16[640,1280]{1,0:T(8,128)(2,1)S(1)}, u32[]{:S(2)}, u32[]{:S(2)}) collective-permute-start(bf16[640,1280]{1,0:T(8,128)(2,1)} %get-tuple-element.60), channel_id=1, source_target_pairs={{0,1},{1,0},{2,3},{3,2},{4,5},{5,4},{6,7},{7,6},{8,9},{9,8},{10,11... | collective-permute-start | bytes 4915208 | tf_op jit(solution)/shard_map/ppermute | solution.py:173
  135.2 1.2 copy-start.5
  140.4 40.4 %all-to-all-start.3 = ((bf16[64,5,2,1280]{3,2,1,0:T(2,128)(2,1)}), bf16[64,5,2,1280]{3,2,1,0:T(2,128)(2,1)S(1)}, u32[]{:S(2)}, u32[]{:S(2)}) async-start(bf16[64,5,2,1280]{3,2,1,0:T(2,128)(2,1)} %bitcast.19), calls=%async_computation.3 | async-start | bytes 3276800 | tf_op jit(solution)/shard_map/all_to_all | solution.py:293
  152.1 14.9 %copy-start.11 = (f32[1,1280]{1,0:T(1,128)}, f32[1,1280]{1,0:T(1,128)S(1)}, u32[]{:S(2)}) copy-start(f32[1,1280]{1,0:T(1,128)S(1)} %psum.14.p0) | copy-start | bytes 15364
  152.1 14.9 %collective-permute-start.9 = (f32[1,1280]{1,0:T(1,128)S(1)}, f32[1,1280]{1,0:T(1,128)S(1)}, u32[]{:S(2)}, u32[]{:S(2)}) collective-permute-start(f32[1,1280]{1,0:T(1,128)S(1)} %psum.14.p0), channel_id=1, source_target_pairs={{6,0},{0,2},{2,4},{4,6},{7,1},{1,3},{3,5},{5,7},{14,8},{8,10},{10,... | collective-permute-start | bytes 15368 | tf_op jit(solution)/shard_map/ppermute | solution.py:207
  153.7 13.3 %collective-permute-start.8 = (f32[1,1280]{1,0:T(1,128)S(1)}, f32[1,1280]{1,0:T(1,128)S(1)}, u32[]{:S(2)}, u32[]{:S(2)}) collective-permute-start(f32[1,1280]{1,0:T(1,128)S(1)} %psum.14.p0), channel_id=1, source_target_pairs={{4,0},{6,2},{0,4},{2,6},{5,1},{7,3},{1,5},{3,7},{12,8},{14,10},{8,... | collective-permute-start | bytes 15368 | tf_op jit(solution)/shard_map/ppermute | solution.py:207
  156.4 10.6 %collective-permute-start.7 = (f32[1,1280]{1,0:T(1,128)S(1)}, f32[1,1280]{1,0:T(1,128)S(1)}, u32[]{:S(2)}, u32[]{:S(2)}) collective-permute-start(f32[1,1280]{1,0:T(1,128)S(1)} %psum.14.p0), channel_id=1, source_target_pairs={{2,0},{4,2},{6,4},{0,6},{3,1},{5,3},{7,5},{1,7},{10,8},{12,10},{14... | collective-permute-start | bytes 15368 | tf_op jit(solution)/shard_map/ppermute | solution.py:207
  166.9 0.6 copy-start.13
  166.9 0.6 copy-start.14
  167.0 0.6 copy-start.15
  177.5 20.2 %copy-start.6 = (f32[4,1408]{1,0:T(4,128)}, f32[4,1408]{1,0:T(4,128)S(1)}, u32[]{:S(2)}) copy-start(f32[4,1408]{1,0:T(4,128)S(1)} %psum.15.m0) | copy-start | bytes 67588
  177.5 20.8 %collective-permute-start.13 = (f32[4,1408]{1,0:T(4,128)S(1)}, f32[4,1408]{1,0:T(4,128)S(1)}, u32[]{:S(2)}, u32[]{:S(2)}) collective-permute-start(f32[4,1408]{1,0:T(4,128)S(1)} %psum.15.m0), channel_id=1, source_target_pairs={{6,0},{0,2},{2,4},{4,6},{7,1},{1,3},{3,5},{5,7},{14,8},{8,10},{10,... | collective-permute-start | bytes 67592 | tf_op jit(solution)/shard_map/ppermute | solution.py:207
  178.1 20.2 %collective-permute-start.12 = (f32[4,1408]{1,0:T(4,128)S(1)}, f32[4,1408]{1,0:T(4,128)S(1)}, u32[]{:S(2)}, u32[]{:S(2)}) collective-permute-start(f32[4,1408]{1,0:T(4,128)S(1)} %psum.15.m0), channel_id=1, source_target_pairs={{4,0},{6,2},{0,4},{2,6},{5,1},{7,3},{1,5},{3,7},{12,8},{14,10},{8,... | collective-permute-start | bytes 67592 | tf_op jit(solution)/shard_map/ppermute | solution.py:207
  179.0 19.3 %collective-permute-start.11 = (f32[4,1408]{1,0:T(4,128)S(1)}, f32[4,1408]{1,0:T(4,128)S(1)}, u32[]{:S(2)}, u32[]{:S(2)}) collective-permute-start(f32[4,1408]{1,0:T(4,128)S(1)} %psum.15.m0), channel_id=1, source_target_pairs={{2,0},{4,2},{6,4},{0,6},{3,1},{5,3},{7,5},{1,7},{10,8},{12,10},{14... | collective-permute-start | bytes 67592 | tf_op jit(solution)/shard_map/ppermute | solution.py:207
  180.9 16.8 %copy-start.2 = (bf16[64,5,2,1280]{3,2,1,0:T(2,128)(2,1)}, bf16[64,5,2,1280]{3,2,1,0:T(2,128)(2,1)S(1)}, u32[]{:S(2)}) copy-start(bf16[64,5,2,1280]{3,2,1,0:T(2,128)(2,1)S(1)} %all-to-all-done.3) | copy-start | bytes 4915204
  180.9 23.9 %all-to-all-start.4 = ((bf16[16,4,2304]{2,1,0:T(4,128)(2,1)}), bf16[16,4,2304]{2,1,0:T(4,128)(2,1)S(1)}, u32[]{:S(2)}, u32[]{:S(2)}) async-start(bf16[16,4,2304]{2,1,0:T(4,128)(2,1)} %get-tuple-element.71), calls=%async_computation.4 | async-start | bytes 589824 | tf_op jit(solution)/shard_map/all_to_all | solution.py:379
  188.5 9.1 %copy-start.7 = (f32[128,2]{1,0:T(8,128)S(1)}, f32[128,2]{1,0:T(8,128)}, u32[]{:S(2)}) copy-start(f32[128,2]{1,0:T(8,128)} %get-tuple-element.98) | copy-start | bytes 3076
  198.3 0.6 copy-start.8
  198.3 0.6 copy-start.9
  198.4 0.6 copy-start.10

commit v3 on v2

v3 whole, which is shorter than its diff:
```python
import math

import jax
import jax.numpy as jnp
from jax import lax
from jax.experimental import pallas as pl
from jax.experimental.pallas import tpu as pltpu
from jax.sharding import Mesh, PartitionSpec as P

D = 1280
EXPERTS = 32
PATCHES = 256
CLASSES = 17408
CAP = 10
CHIPS = 64
IMAGES = 64
TOK = 128
HALF = CHIPS * CAP
ROWS = 2 * HALF
COLS = CLASSES // 8
BETA = 0.99
LOG_BETA = math.log(BETA)
EPS = 1e-06

CHIP = ("dp", "yh", "yl")
Y = ("yh", "yl")
EX = ("yh", "yl", "core")
ALL = ("dp", "yh", "yl", "core")
SWAP = [(0, 1), (1, 0)]
F32 = jnp.float32
BF16 = jnp.bfloat16
I32 = jnp.int32
PACKED = (HALF // 2, 2, D)
WIDE = D + 128
PACKED_X = (HALF // 2, 2, WIDE)
ROOT_2_PI = 0.7978845608028654
CUBIC = 0.044715


def dot(a, b, ca, cb):
    return lax.dot_general(a, b, (((ca,), (cb,)), ((), ())), preferred_element_type=F32)


def shape(dims, dtype):
    return jax.ShapeDtypeStruct(dims, dtype)


VMEM = pl.BlockSpec(memory_space=pltpu.VMEM)
SMEM = pl.BlockSpec(memory_space=pltpu.SMEM)
ANY = pl.BlockSpec(memory_space=pl.ANY)


TINY = pl.CostEstimate(flops=1, transcendentals=0, bytes_accessed=1)


LONG = pl.CostEstimate(flops=1 << 34, transcendentals=0, bytes_accessed=1 << 26)


def run(body, outs, *args, specs=None, out_specs=None, scratch=(), name=None, cost=TINY):
    return pl.pallas_call(
        body,
        out_shape=outs,
        in_specs=specs or [VMEM] * len(args),
        out_specs=out_specs or jax.tree.map(lambda _: VMEM, outs),
        scratch_shapes=list(scratch),
        name=name,
        cost_estimate=cost,
        compiler_params=pltpu.CompilerParams(vmem_limit_bytes=56 << 20),
    )(*args)


def pack_rows(ref, value):
    ref[...] = value.astype(BF16).reshape(ref.shape)


def x_body(routes_ref, labels_ref, tokens_ref, table_ref, send_ref):
    ids = lax.broadcasted_iota(I32, (EXPERTS, TOK), 0)
    routes = (routes_ref[0:1, :], routes_ref[1:2, :])
    hit = [r == ids for r in routes]
    hits = jnp.where(hit[0], 1.0, jnp.where(hit[1], 1.0, 0.0)).astype(BF16)
    t_row = lax.broadcasted_iota(I32, (TOK, TOK), 0)
    t_col = lax.broadcasted_iota(I32, (TOK, TOK), 1)
    before = jnp.where(t_row < t_col, 1.0, 0.0).astype(BF16)
    earlier = dot(hits, before, 1, 0)
    slot = lax.broadcasted_iota(I32, (HALF, TOK), 0)
    both = jnp.zeros((HALF, TOK), F32)
    for k in range(2):
        pos = jnp.sum(jnp.where(hit[k], earlier, 0.0), axis=0, keepdims=True)
        row = routes[k] * (2 * CAP) + pos.astype(I32)
        table = jnp.where(slot == row, 1.0, jnp.where(slot == row + CAP, 1.0, 0.0))
        table_ref[k] = table.astype(BF16)
        both = both + table
    rows = dot(both.astype(BF16), tokens_ref[...], 1, 0)
    labels = labels_ref[...]
    high = lax.shift_right_logical(labels, 8)
    low = labels - high * 256
    digits = jnp.concatenate(
        [high.astype(F32), low.astype(F32), jnp.zeros((4, 120), F32)], axis=1
    ).astype(BF16)
    place = lax.broadcasted_iota(I32, (HALF, 4), 0)
    image = lax.broadcasted_iota(I32, (HALF, 4), 1)
    chip = lax.shift_right_logical(place * 6554, 16)
    spread = jnp.where(place - CAP * chip == image, 1.0, 0.0).astype(BF16)
    pack_rows(send_ref, jnp.concatenate([rows, dot(spread, digits, 1, 0)], axis=1))


def g_body(table_ref, grad_ref, combine_ref, send_ref):
    table0, table1 = table_ref[0].astype(F32), table_ref[1].astype(F32)
    scale = jnp.sum(
        table0 * combine_ref[0:1, :] + table1 * combine_ref[1:2, :], axis=1, keepdims=True
    )
    pack_rows(send_ref, scale * dot((table0 + table1).astype(BF16), grad_ref[...], 1, 0))


CHUNK = 320
STEPS = HALF // CHUNK


def chunk_rows(base, i):
    return pl.ds(pl.multiple_of(base + i * CHUNK, CHUNK), CHUNK)


def chunk_copies(i, square, own, other, sems):
    pairs = []
    for vmem, hbm in square:
        for base in (0, HALF):
            rows = chunk_rows(base, i)
            pairs.append((vmem.at[rows, :], hbm.at[rows, :]))
    for vmem, hbm in (own, other):
        rows = chunk_rows(0, i)
        pairs.append((vmem.at[rows, :], hbm.at[rows, :]))
    return [pltpu.make_async_copy(s, d, sems.at[i, n]) for n, (s, d) in enumerate(pairs)]


def load(pairs, sems):
    copies = [pltpu.make_async_copy(s, d, sems.at[n]) for n, (s, d) in enumerate(pairs)]
    for copy in copies:
        copy.start()
    return copies


def forward_body(
    own_in, other_in, w1_in, w2_in, xs_out, hidden_out, slope_out, own_out, other_out,
    own_x, other_x, w1, w2, xs, hidden, slope, own, other, in_sems, xs_sem, out_sems,
):
    copies = load(((own_in, own_x), (other_in, other_x), (w1_in, w1), (w2_in, w2)), in_sems)
    copies[0].wait()
    xs[:HALF] = own_x[:, :, :D].reshape(HALF, D)
    copies[1].wait()
    xs[HALF:] = other_x[:, :, :D].reshape(HALF, D)
    keep = pltpu.make_async_copy(xs, xs_out, xs_sem)
    keep.start()
    copies[2].wait()
    copies[3].wait()

    def outputs(i):
        square = ((hidden, hidden_out), (slope, slope_out))
        return chunk_copies(i, square, (own, own_out), (other, other_out), out_sems)

    def step(i, carry):
        for base in (0, HALF):
            rows = chunk_rows(base, i)
            h = dot(xs[rows, :], w1[...], 1, 0)
            square = h * h
            bend = jnp.tanh(ROOT_2_PI * h * (1.0 + CUBIC * square))
            half = 0.5 * (1.0 + bend)
            act = (h * half).astype(BF16)
            hidden[rows, :] = act
            slope[rows, :] = (
                half
                + 0.5 * h * (1.0 - bend * bend) * (ROOT_2_PI * (1.0 + 3.0 * CUBIC * square))
            ).astype(BF16)
            part = dot(act, w2[...], 1, 0)
            if base == 0:
                own[chunk_rows(0, i), :] = part
            else:
                other[chunk_rows(0, i), :] = part.astype(BF16)
        for copy in outputs(i):
            copy.start()
        return carry

    lax.fori_loop(0, STEPS, step, 0)
    keep.wait()
    for i in range(STEPS):
        for copy in outputs(i):
            copy.wait()


def backward_body(
    own_in, other_in, slope_in, w1_in, w2_in, gs_out, d_pre_out, own_out, other_out,
    own_g, other_g, slope, w1, w2, gs, d_pre, own, other, in_sems, gs_sem, out_sems,
):
    pairs = ((own_in, own_g), (other_in, other_g), (w2_in, w2), (slope_in, slope), (w1_in, w1))
    copies = load(pairs, in_sems)
    copies[0].wait()
    gs[:HALF] = own_g[...].reshape(HALF, D)
    copies[1].wait()
    gs[HALF:] = other_g[...].reshape(HALF, D)
    keep = pltpu.make_async_copy(gs, gs_out, gs_sem)
    keep.start()
    for copy in copies[2:]:
        copy.wait()

    def outputs(i):
        square = ((d_pre, d_pre_out),)
        return chunk_copies(i, square, (own, own_out), (other, other_out), out_sems)

    def step(i, carry):
        for base in (0, HALF):
            rows = chunk_rows(base, i)
            d_h = dot(gs[rows, :], w2[...], 1, 1)
            act = (d_h * slope[rows, :].astype(F32)).astype(BF16)
            d_pre[rows, :] = act
            part = dot(act, w1[...], 1, 1)
            if base == 0:
                own[chunk_rows(0, i), :] = part
            else:
                other[chunk_rows(0, i), :] = part.astype(BF16)
        for copy in outputs(i):
            copy.start()
        return carry

    lax.fori_loop(0, STEPS, step, 0)
    keep.wait()
    for i in range(STEPS):
        for copy in outputs(i):
            copy.wait()


SQUARE = (ROWS, D)


def expert_kernel(body, ins, kept, received, name):
    outs = (*[shape(SQUARE, BF16)] * kept, shape((HALF, D), F32), shape((HALF, D), BF16))
    scratch = [pltpu.VMEM(received, BF16)] * 2
    scratch += [pltpu.VMEM((D, D), BF16)] * (len(ins) - 2)
    scratch += [pltpu.VMEM(SQUARE, BF16)] * (kept if len(ins) == 4 else 2)
    scratch += [pltpu.VMEM((HALF, D), F32), pltpu.VMEM((HALF, D), BF16)]
    scratch += [
        pltpu.SemaphoreType.DMA((len(ins),)),
        pltpu.SemaphoreType.DMA,
        pltpu.SemaphoreType.DMA((STEPS, 6)),
    ]
    return run(
        body,
        outs,
        *ins,
        specs=[ANY] * len(ins),
        out_specs=tuple([ANY] * len(outs)),
        scratch=scratch,
        name=name,
    )


GRAD_COLS = 256


def weight_grad_body(left_ref, right_ref, out_ref):
    def step(i, carry):
        cols = pl.ds(pl.multiple_of(i * GRAD_COLS, GRAD_COLS), GRAD_COLS)
        out_ref[cols, :] = dot(left_ref[:, cols], right_ref[...], 0, 0).astype(BF16)
        return carry

    lax.fori_loop(0, D // GRAD_COLS, step, 0)


def add_body(own_ref, other_ref, send_ref):
    pack_rows(send_ref, own_ref[...] + other_ref[...].astype(F32))


def across(row):
    return jnp.sum(jnp.where(eye(), row, 0.0), axis=1, keepdims=True)


def along(column):
    return jnp.sum(jnp.where(eye(), column, 0.0), axis=0, keepdims=True)


def eye():
    return lax.broadcasted_iota(I32, (TOK, TOK), 0) == lax.broadcasted_iota(I32, (TOK, TOK), 1)


def mixed_body(table_ref, in_ref, tokens_ref, grad_ref, combine_ref, mixed_ref, dc_ref, sum_ref):
    rows = in_ref[...].reshape(HALF, D)
    vals0 = dot(table_ref[0], rows, 0, 0)
    vals1 = dot(table_ref[1], rows, 0, 0)
    grad = grad_ref[...].astype(F32)
    dc_ref[0:1, :] = along(jnp.sum(grad * vals0, axis=1, keepdims=True))
    dc_ref[1:2, :] = along(jnp.sum(grad * vals1, axis=1, keepdims=True))
    mixed = (
        tokens_ref[...].astype(F32)
        + (across(combine_ref[0:1, :]) * vals0 + across(combine_ref[1:2, :]) * vals1)
    ).astype(BF16)
    mixed_ref[...] = mixed
    sum_ref[...] = jnp.sum(mixed.astype(F32), axis=0, keepdims=True)


def tokens_body(table_ref, in_ref, grad_ref, out_ref):
    rows = in_ref[...].reshape(HALF, D)
    table = (table_ref[0].astype(F32) + table_ref[1].astype(F32)).astype(BF16)
    out_ref[...] = (grad_ref[...].astype(F32) + dot(table, rows, 0, 0)).astype(BF16)


def in_order(here, parts, j):
    pick = parts[0]
    for shift in (1, 2, 3):
        pick = jnp.where((here + shift) % 4 == j, parts[shift], pick)
    return pick


def y_parts(mine):
    return [mine] + [
        lax.ppermute(mine, Y, [((i + shift) % 4, i) for i in range(4)]) for shift in (1, 2, 3)
    ]


def centered(pooled):
    away = pooled - jnp.mean(pooled, axis=1, keepdims=True)
    return away, lax.rsqrt(jnp.mean(away * away, axis=1, keepdims=True) + EPS)


def head_body(here_ref, p0, p1, p2, p3, target_ref, weight_ref, w_ref, pooled_ref, part_ref, send_ref):
    here = here_ref[0]
    parts = [p[...] for p in (p0, p1, p2, p3)]
    for j in range(4):
        pooled_ref[j : j + 1, :] = in_order(here, parts, j) * (1.0 / PATCHES)
    away, scale = centered(pooled_ref[...])
    normed = (away * scale).astype(BF16)
    logits = dot(normed, w_ref[...], 1, 0)
    hit = target_ref[...] > 0.5
    signed = jnp.where(hit, -logits, logits)
    small = jnp.exp(-jnp.abs(signed))
    nll = jnp.maximum(signed, 0.0) + jnp.log1p(small)
    inverse = 1.0 / (1.0 + small)
    miss = jnp.where(signed >= 0.0, 1.0, small) * inverse
    keep = jnp.where(signed >= 0.0, small, 1.0) * inverse
    weight = weight_ref[...]
    loss = jnp.sum(weight * (miss * miss) * nll, axis=1, keepdims=True)
    slope = weight * (2.0 * miss * keep * nll + miss * miss) * miss
    d_logits = jnp.where(hit, -slope, slope).astype(BF16)
    part_ref[:, :D] = dot(d_logits, w_ref[...], 1, 1)
    part_ref[:, D:] = jnp.broadcast_to(loss, (4, 128))
    zeros = jnp.zeros((4, 48), BF16)
    for d in range(16):
        send_ref[d, :, :COLS] = d_logits
        send_ref[d, :, COLS : COLS + 128] = jnp.concatenate(
            [normed[:, 80 * d : 80 * d + 80], zeros], axis=1
        )


def pooled_body(here_ref, m0, m1, m2, m3, pooled_ref, d_ref, loss_ref):
    here = here_ref[0]
    parts = [m[...] for m in (m0, m1, m2, m3)]
    total = in_order(here, parts, 0)
    for j in (1, 2, 3):
        total = total + in_order(here, parts, j)
    away, scale = centered(pooled_ref[...])
    normed = away * scale
    d_normed = total[:, :D]
    mean = jnp.mean(d_normed, axis=1, keepdims=True)
    along = jnp.mean(d_normed * normed, axis=1, keepdims=True)
    d_ref[...] = scale * (d_normed - mean - normed * along)
    loss_ref[...] = total[:, D:]


def effective_of(counts):
    return (1.0 - BETA) / (1.0 - jnp.exp((counts + 1.0) * LOG_BETA))


def label_body(first_ref, digits_ref, labels_ref, target_ref, weight_ref):
    ids = (lax.broadcasted_iota(I32, (1, COLS), 1) + first_ref[0]).astype(F32)
    own = labels_ref[...].astype(F32)
    target = own[:, 0:1] == ids
    for n in range(1, 4):
        target = target | (own[:, n : n + 1] == ids)
    target_ref[...] = jnp.where(target, 1.0, 0.0)
    digits = digits_ref[...].astype(F32)
    labels = digits[:, 0:4] * 256.0 + digits[:, 4:8]
    padded = jnp.concatenate([labels, jnp.zeros((IMAGES, 124), F32)], axis=1)
    turned = jnp.concatenate([padded, jnp.zeros((128 - IMAGES, 128), F32)], axis=0).T
    columns = [labels[:, n : n + 1] for n in range(4)]
    rows = [turned[n : n + 1, :IMAGES] for n in range(4)]

    def fresh_of(entries):
        out = [jnp.ones_like(entries[0])]
        for n in range(1, 4):
            keep = out[0]
            for m in range(n):
                keep = jnp.where(entries[m] == entries[n], 0.0, keep)
            out.append(keep)
        return out

    fresh, fresh_row = fresh_of(columns), fresh_of(rows)
    counts = jnp.zeros((IMAGES, COLS), F32)
    excess = jnp.zeros((IMAGES, 1), F32)
    base = effective_of(jnp.zeros((IMAGES, 1), F32))
    for n in range(4):
        counts = counts + jnp.where(columns[n] == ids, fresh[n], 0.0)
        same = jnp.zeros((IMAGES, IMAGES), F32)
        for m in range(4):
            same = same + jnp.where(columns[n] == rows[m], fresh_row[m], 0.0)
        count = jnp.sum(same, axis=1, keepdims=True)
        excess = excess + fresh[n] * (effective_of(count) - base) / count
    total = CLASSES * base[0:1, :] + jnp.sum(excess, axis=0, keepdims=True)
    weight_ref[...] = effective_of(jnp.sum(counts, axis=0, keepdims=True)) * (CLASSES / total)


def chip_swap(packed):
    dims = packed.shape
    blocks = packed.reshape(CHIPS, CAP // 2, 2, dims[-1])
    return lax.all_to_all(blocks, CHIP, 0, 0, tiled=True).reshape(dims)


def core_swap(rows):
    return lax.ppermute(rows, "core", SWAP)


def shards(tokens, routes, combine, w_in, w_out, out_grad, head_w, labels):
    here = lax.axis_index(Y).astype(I32).reshape(1)
    first_class = (lax.axis_index(EX) * COLS).astype(I32).reshape(1)
    combine = combine.T
    table, x_send = run(
        x_body,
        (shape((2, HALF, TOK), BF16), shape(PACKED_X, BF16)),
        routes.T,
        labels,
        tokens,
        name="dispatch_x",
    )
    x_in = chip_swap(x_send)
    g_send = run(g_body, shape(PACKED, BF16), table, out_grad, combine, name="dispatch_g")
    x_in, g_send = lax.optimization_barrier((x_in, g_send))
    g_in = chip_swap(g_send)
    xs, hidden, slope, own, other = expert_kernel(
        forward_body, (x_in, core_swap(x_in), w_in, w_out), 3, PACKED_X, "forward"
    )
    other = core_swap(other)
    digits = x_in.reshape(IMAGES // 4, 4, CAP, WIDE)[:, 0, :4, D : D + 128].reshape(IMAGES, 128)
    g_in, digits = lax.optimization_barrier((g_in, digits))
    targets, class_weight = run(
        label_body,
        (shape((4, COLS), F32), shape((1, COLS), F32)),
        first_class,
        digits,
        labels,
        specs=[SMEM, VMEM, VMEM],
        name="labels",
        cost=LONG,
    )
    own, class_weight = lax.optimization_barrier((own, class_weight))
    out_in = chip_swap(run(add_body, shape(PACKED, BF16), own, other, name="add_out"))
    gs, d_pre, own, other = expert_kernel(
        backward_body, (g_in, core_swap(g_in), slope, w_in, w_out), 2, PACKED, "backward"
    )
    other = core_swap(other)
    d_w_out = run(weight_grad_body, shape((D, D), BF16), hidden, gs, name="d_w_out")
    out_in, d_w_out = lax.optimization_barrier((out_in, d_w_out))
    mixed_out, d_combine, token_sum = run(
        mixed_body,
        (shape((TOK, D), BF16), shape((2, TOK), F32), shape((1, D), F32)),
        table,
        out_in,
        tokens,
        out_grad,
        combine,
        name="mixed",
        cost=LONG,
    )
    own, token_sum = lax.optimization_barrier((own, token_sum))
    rows_in = chip_swap(run(add_body, shape(PACKED, BF16), own, other, name="add_rows"))
    sums = y_parts(lax.psum(token_sum, "core"))
    pooled, part, dp_send = run(
        head_body,
        (shape((4, D), F32), shape((4, D + 128), F32), shape((16, 4, COLS + 128), BF16)),
        here,
        *sums,
        targets,
        class_weight,
        head_w,
        specs=[SMEM] + [VMEM] * 7,
        name="head",
    )
    messages = y_parts(lax.psum(part, "core"))
    d_pooled, losses = run(
        pooled_body,
        (shape((4, D), F32), shape((4, 128), F32)),
        here,
        *messages,
        pooled,
        specs=[SMEM] + [VMEM] * 5,
        name="d_pooled",
    )
    dp_send, rows_in, xs, d_pooled = lax.optimization_barrier((dp_send, rows_in, xs, d_pooled))
    dp_in = lax.all_to_all(dp_send, "dp", 0, 0, tiled=True).reshape(IMAGES, COLS + 128)
    d_tokens = run(tokens_body, shape((TOK, D), BF16), table, rows_in, out_grad, name="d_tokens")
    d_w_in = run(weight_grad_body, shape((D, D), BF16), xs, d_pre, name="d_w_in")
    d_head = dot(dp_in[:, COLS : COLS + 80], dp_in[:, :COLS], 0, 0).astype(BF16)
    return (mixed_out, d_tokens, d_combine.T, d_w_in, d_w_out, losses[:, 0], d_pooled, d_head)


def solution(mesh):
    grid = Mesh(mesh.devices.reshape(16, 2, 2, 2), ALL)
    rows = P(ALL, None)
    in_specs = (rows, rows, rows, P(None, ALL), rows, rows, P(None, EX), P("dp", None))
    out_specs = (
        rows,
        rows,
        rows,
        P(None, ALL),
        rows,
        P("dp"),
        P("dp", None),
        P("dp", EX),
    )
    return jax.shard_map(shards, mesh=grid, in_specs=in_specs, out_specs=out_specs, check_vma=False)
```

time: 207 us -> 200 us (0.966)
  Pallas kernels: 63.5 us -> 83.4 us
  matrix products: 19.2 us -> 1.02 us
  starting transfers between devices: 65.3 us -> 59 us
  local copies, waits for them, and re-layouts: 8.79 us -> 11.8 us
  other arithmetic: 2.56 us -> 0 us
    ppermute x8 -> x4, waiting for transfers between devices: 26.4 us -> 0.01 us  [core_swap(): return lax.ppermute(rows, 'core', SWAP)]
    pallas_call x10 -> x13, Pallas kernels: 63.5 us -> 83.4 us  [run(): pl.pallas_call(body, out_shape=outs, in_specs=specs or [VMEM] * len(args)...]
    dot_general x3 -> x1, matrix products: 19.2 us -> 1.02 us  [dot(): lax.dot_general(a, b, (((ca,), (cb,)), ((), ())), preferred_element_type=...]
    ppermute x8 -> x4, starting transfers between devices: 14.3 us -> 0.39 us  [core_swap(): return lax.ppermute(rows, 'core', SWAP)]
    all_to_all x4, waiting for transfers between devices: 11.2 us -> 24.7 us  [chip_swap(): return lax.all_to_all(blocks, CHIP, 0, 0, tiled=True).reshape(dims)]
    ppermute x6, waiting for transfers between devices: 0.02 us -> 11.5 us  [y_parts(): lax.ppermute(mine, Y, [((i + shift) % 4, i) for i in range(4)])]
    reshape x1, local copies, waits for them, and re-layouts: 0.1 us -> 5.5 us  [shards(): x_in.reshape(IMAGES // 4, 4, CAP, WIDE)[:, 0, :4, D:D + 128]]
    all_to_all x1, starting transfers between devices: 7.64 us -> 11.1 us  [shards(): lax.all_to_all(dp_send, 'dp', 0, 0, tiled=True).reshape(IMAGES, COLS + 128)]
  transfers between devices with their start and end apart: 19 -> 15, of which waited for: 7 -> 7; matrix products, arithmetic and copies ran while one was open for 12% -> 4% of each run, Pallas kernels for 27% -> 38%
where the time goes in v3:
time: 200 us; the launch traced here: 199 us
  Pallas kernels  83.4 us (42%)
  starting transfers between devices  59 us (30%)
  waiting for transfers between devices  36.2 us (18%)
  local copies, waits for them, and re-layouts  11.8 us (6%)
  blocking collectives  6.5 us (3%)
    pallas_call x13, Pallas kernels, run(): pl.pallas_call(body, out_shape=outs, in_specs=specs or [VMEM] * len(args)...  83.4 us
    all_to_all x4, starting transfers between devices, chip_swap(): return lax.all_to_all(blocks, CHIP, 0, 0, tiled=True).reshape(dims)  37.6 us
    all_to_all x4, waiting for transfers between devices, chip_swap(): return lax.all_to_all(blocks, CHIP, 0, 0, tiled=True).reshape(dims)  24.7 us
    ppermute x6, waiting for transfers between devices, y_parts(): lax.ppermute(mine, Y, [((i + shift) % 4, i) for i in range(4)])  11.5 us
    all_to_all x1, starting transfers between devices, shards(): lax.all_to_all(dp_send, 'dp', 0, 0, tiled=True).reshape(IMAGES, COLS + 128)  11.1 us
    ppermute x6, starting transfers between devices, y_parts(): lax.ppermute(mine, Y, [((i + shift) % 4, i) for i in range(4)])  9.92 us
    reshape x1, local copies, waits for them, and re-layouts, shards(): x_in.reshape(IMAGES // 4, 4, CAP, WIDE)[:, 0, :4, D:D + 128]  5.5 us
    psum x1, blocking collectives, shards(): messages = y_parts(lax.psum(part, 'core'))  4.01 us
  transfers between devices with their start and end apart: 15, of which 7 were waited for; matrix products, arithmetic and copies ran while one was open for 4% of the time, Pallas kernels for 38%

profile of v3, /device:TPU:0, one launch (start us, length us, event | category | flops | bytes accessed | tf_op | source)
XLA Modules:
  0.0 198.7 jit_solution(1877058195276469588)
XLA Ops:
  0.6 3.1 %dispatch_x.1 = (bf16[2,640,128]{2,1,0:T(8,128)(2,1)}, bf16[320,2,1408]{2,1,0:T(2,128)(2,1)}) custom-call(s32[2,128]{1,0:T(2,128)} %bitcast.25, s32[4,4]{1,0:T(4,128)} %labels_ref.3, bf16[128,1280]{1,0:T(8,128)(2,1)} %tokens_ref.3), custom_call_target="tpu_custom_call" | custom-call | flops 1 | bytes 1 | tf_op jit(solution)/shard_map/dispatch_x/pallas_call | solution.py:60
  3.7 11.5 %all-to-all-start = ((bf16[64,5,2,1408]{3,2,1,0:T(2,128)(2,1)}), bf16[64,5,2,1408]{3,2,1,0:T(2,128)(2,1)S(1)}, u32[]{:S(2)}, u32[]{:S(2)}) async-start(bf16[64,5,2,1408]{3,2,1,0:T(2,128)(2,1)} %bitcast.23), calls=%async_computation | async-start | bytes 3604480 | tf_op jit(solution)/shard_map/all_to_all | solution.py:411
  15.2 3.0 %dispatch_g.1 = bf16[320,2,1280]{2,1,0:T(2,128)(2,1)} custom-call(bf16[2,640,128]{2,1,0:T(8,128)(2,1)} %get-tuple-element.43.table_ref, bf16[128,1280]{1,0:T(8,128)(2,1)} %grad_ref.5, f32[2,128]{1,0:T(2,128)} %bitcast.26), custom_call_target="tpu_custom_call" | custom-call | flops 1 | bytes 1 | tf_op jit(solution)/shard_map/dispatch_g/pallas_call | solution.py:60
  18.2 23.6 %all-to-all-done = bf16[64,5,2,1408]{3,2,1,0:T(2,128)(2,1)S(1)} async-done(((bf16[64,5,2,1408]{3,2,1,0:T(2,128)(2,1)}), bf16[64,5,2,1408]{3,2,1,0:T(2,128)(2,1)S(1)}, u32[]{:S(2)}, u32[]{:S(2)}) %all-to-all-start) | async-done | bytes 1802272 | tf_op jit(solution)/shard_map/all_to_all | solution.py:411
  41.8 0.0 collective-permute-start
  41.8 5.8 %all-to-all-start.1 = ((bf16[64,5,2,1280]{3,2,1,0:T(2,128)(2,1)}), bf16[64,5,2,1280]{3,2,1,0:T(2,128)(2,1)S(1)}, u32[]{:S(2)}, u32[]{:S(2)}) async-start(bf16[64,5,2,1280]{3,2,1,0:T(2,128)(2,1)} %bitcast.21), calls=%async_computation.1 | async-start | bytes 3276800 | tf_op jit(solution)/shard_map/all_to_all | solution.py:411
  47.6 17.1 %forward.1 = (bf16[1280,1280]{1,0:T(8,128)(2,1)}, bf16[1280,1280]{1,0:T(8,128)(2,1)}, bf16[1280,1280]{1,0:T(8,128)(2,1)}, f32[640,1280]{1,0:T(8,128)}, bf16[640,1280]{1,0:T(8,128)(2,1)}) custom-call(bf16[320,2,1408]{2,1,0:T(2,128)(2,1)} %bitcast.15, bf16[320,2,1408]{2,1,0:T(2,128)(2,1)} %collective-permute-done.other_in, bf16[1280,1280]{1,0:T(8,128)(2,1)} %w1_in.3, ...), custom_call_target="tpu_custom_call" | custom-call | flops 1 | bytes 1 | tf_op jit(solution)/shard_map/forward/pallas_call | solution.py:60
  64.8 0.3 collective-permute-start.1
  65.1 5.5 %reshape.57 = bf16[16,4,10,1408]{3,2,1,0:T(8,128)(2,1)} reshape(bf16[320,2,1408]{2,1,0:T(2,128)(2,1)} %bitcast.16) | data formatting | bytes 3604480 | tf_op jit(solution)/shard_map/reshape | solution.py:438
  70.6 1.4 slice.16
  72.0 1.2 all-to-all-done.1
  73.1 0.0 collective-permute-start.2
  73.1 2.1 %labels.1 = (f32[4,2176]{1,0:T(4,128)}, f32[1,2176]{1,0:T(1,128)}) custom-call(s32[1]{0:T(128)} %bitcast.4.first_ref, bf16[64,128]{1,0:T(8,128)(2,1)} %bitcast.24, s32[4,4]{1,0:T(4,128)} %labels_ref.3), custom_call_target="tpu_custom_call" | custom-call | flops 17179869184 | bytes 67108864 | tf_op jit(solution)/shard_map/labels/pallas_call | solution.py:60
  75.3 0.0 collective-permute-done.1.other_ref
  75.3 4.1 %add_out.1 = bf16[320,2,1280]{2,1,0:T(2,128)(2,1)} custom-call(f32[640,1280]{1,0:T(8,128)} %get-tuple-element.50.own_ref, bf16[640,1280]{1,0:T(8,128)(2,1)} %collective-permute-done.1.other_ref), custom_call_target="tpu_custom_call" | custom-call | flops 1 | bytes 1 | tf_op jit(solution)/shard_map/add_out/pallas_call | solution.py:60
  79.4 9.9 %all-to-all-start.2 = ((bf16[64,5,2,1280]{3,2,1,0:T(2,128)(2,1)}), bf16[64,5,2,1280]{3,2,1,0:T(2,128)(2,1)}, u32[]{:S(2)}, u32[]{:S(2)}) async-start(bf16[64,5,2,1280]{3,2,1,0:T(2,128)(2,1)} %bitcast.22), calls=%async_computation.2 | async-start | bytes 3276800 | tf_op jit(solution)/shard_map/all_to_all | solution.py:411
  89.3 1.2 copy-done.3
  90.5 16.3 %backward.1 = (bf16[1280,1280]{1,0:T(8,128)(2,1)}, bf16[1280,1280]{1,0:T(8,128)(2,1)}, f32[640,1280]{1,0:T(8,128)}, bf16[640,1280]{1,0:T(8,128)(2,1)}) custom-call(bf16[320,2,1280]{2,1,0:T(2,128)(2,1)} %bitcast.18, bf16[320,2,1280]{2,1,0:T(2,128)(2,1)} %copy-done.3, bf16[1280,1280]{1,0:T(8,128)(2,1)} %get-tuple-element.54.slope_in, ...), custom_call_target="tpu_custom_call" | custom-call | flops 1 | bytes 1 | tf_op jit(solution)/shard_map/backward/pallas_call | solution.py:60
  106.8 0.1 collective-permute-start.6
  106.9 10.0 %d_w_out.1 = bf16[1280,1280]{1,0:T(8,128)(2,1)} custom-call(bf16[1280,1280]{1,0:T(8,128)(2,1)} %get-tuple-element.52.left_ref, bf16[1280,1280]{1,0:T(8,128)(2,1)} %get-tuple-element.55.right_ref), custom_call_target="tpu_custom_call" | custom-call | flops 1 | bytes 1 | tf_op jit(solution)/shard_map/d_w_out/pallas_call | solution.py:60
  116.9 3.2 %mixed.1 = (bf16[128,1280]{1,0:T(8,128)(2,1)}, f32[2,128]{1,0:T(2,128)}, f32[1,1280]{1,0:T(1,128)}) custom-call(bf16[2,640,128]{2,1,0:T(8,128)(2,1)} %get-tuple-element.43.table_ref, bf16[320,2,1280]{2,1,0:T(2,128)(2,1)} %bitcast.9.in_ref, bf16[128,1280]{1,0:T(8,128)(2,1)} %tokens_ref.3, bf16[128,1280]{1,0:T(8,128)(2,1)} %grad_ref.5, f32[2,128]{1,0:T(2,128)} %bitcast.27), custom_call_target="tpu_custom_call" | custom-call | flops 17179869184 | bytes 67108864 | tf_op jit(solution)/shard_map/mixed/pallas_call | solution.py:60
  120.1 1.2 copy-done.4
  121.3 4.1 %add_rows.1 = bf16[320,2,1280]{2,1,0:T(2,128)(2,1)} custom-call(f32[640,1280]{1,0:T(8,128)} %get-tuple-element.64.own_ref, bf16[640,1280]{1,0:T(8,128)(2,1)} %copy-done.4), custom_call_target="tpu_custom_call" | custom-call | flops 1 | bytes 1 | tf_op jit(solution)/shard_map/add_rows/pallas_call | solution.py:60
  125.3 10.4 %all-to-all-start.3 = ((bf16[64,5,2,1280]{3,2,1,0:T(2,128)(2,1)}), bf16[64,5,2,1280]{3,2,1,0:T(2,128)(2,1)S(1)}, u32[]{:S(2)}, u32[]{:S(2)}) async-start(bf16[64,5,2,1280]{3,2,1,0:T(2,128)(2,1)} %bitcast.20), calls=%async_computation.3 | async-start | bytes 3276800 | tf_op jit(solution)/shard_map/all_to_all | solution.py:411
  135.8 2.5 %psum.14.p0 = f32[1,1280]{1,0:T(1,128)S(1)} all-reduce(f32[1,1280]{1,0:T(1,128)S(1)} %copy-done.13), channel_id=1, replica_groups=mesh['dp'=16,'yh'=2,'yl'=2,'core'=2] {'core'}, use_global_device_ids=true, to_apply=%region_0.0 | all-reduce | flops 1280 | bytes 10240 | tf_op jit(solution)/shard_map/psum | solution.py:471
  138.3 1.6 collective-permute-start.5
  139.9 2.7 %collective-permute-start.4 = (f32[1,1280]{1,0:T(1,128)S(1)}, f32[1,1280]{1,0:T(1,128)S(1)}, u32[]{:S(2)}, u32[]{:S(2)}) collective-permute-start(f32[1,1280]{1,0:T(1,128)S(1)} %psum.14.p0), channel_id=1, source_target_pairs={{4,0},{6,2},{0,4},{2,6},{5,1},{7,3},{1,5},{3,7},{12,8},{14,10},{8,... | collective-permute-start | bytes 15368 | tf_op jit(solution)/shard_map/ppermute | solution.py:313
  142.6 1.5 collective-permute-start.3
  144.0 5.3 %collective-permute-done.5.p3 = f32[1,1280]{1,0:T(1,128)S(1)} collective-permute-done((f32[1,1280]{1,0:T(1,128)S(1)}, f32[1,1280]{1,0:T(1,128)S(1)}, u32[]{:S(2)}, u32[]{:S(2)}) %collective-permute-start.5) | collective-permute-done | bytes 5152 | tf_op jit(solution)/shard_map/ppermute | solution.py:313
  149.3 3.1 %collective-permute-done.4.p2 = f32[1,1280]{1,0:T(1,128)S(1)} collective-permute-done((f32[1,1280]{1,0:T(1,128)S(1)}, f32[1,1280]{1,0:T(1,128)S(1)}, u32[]{:S(2)}, u32[]{:S(2)}) %collective-permute-start.4) | collective-permute-done | bytes 5152 | tf_op jit(solution)/shard_map/ppermute | solution.py:313
  152.5 0.6 copy-done.11
  153.0 5.9 %head.1 = (f32[4,1280]{1,0:T(4,128)}, f32[4,1408]{1,0:T(4,128)}, bf16[16,4,2304]{2,1,0:T(4,128)(2,1)}) custom-call(s32[1]{0:T(128)} %bitcast.10.here_ref, f32[1,1280]{1,0:T(1,128)} %copy-done.9, f32[1,1280]{1,0:T(1,128)} %copy-done.12, f32[1,1280]{1,0:T(1,128)} %copy-done.11, f32[1,1280]{1,0:T(1,128)} %copy-done.10, f32[4,2176]{1,0:T(4,128)} %get-tuple-element.61.target_ref, ...), custom_call_target="tpu_custom_call" | custom-call | flops 1 | bytes 1 | tf_op jit(solution)/shard_map/head/pallas_call | solution.py:60
  158.9 4.0 %psum.15.m0 = f32[4,1408]{1,0:T(4,128)S(1)} all-reduce(f32[4,1408]{1,0:T(4,128)} %get-tuple-element.67), channel_id=1, replica_groups=mesh['dp'=16,'yh'=2,'yl'=2,'core'=2] {'core'}, use_global_device_ids=true, to_apply=%region_1.0 | all-reduce | flops 5632 | bytes 45056 | tf_op jit(solution)/shard_map/psum | solution.py:483
  162.9 0.0 copy-start.5
  162.9 0.8 collective-permute-start.9
  163.8 2.5 %collective-permute-start.8 = (f32[4,1408]{1,0:T(4,128)S(1)}, f32[4,1408]{1,0:T(4,128)S(1)}, u32[]{:S(2)}, u32[]{:S(2)}) collective-permute-start(f32[4,1408]{1,0:T(4,128)S(1)} %psum.15.m0), channel_id=1, source_target_pairs={{4,0},{6,2},{0,4},{2,6},{5,1},{7,3},{1,5},{3,7},{12,8},{14,10},{8,... | collective-permute-start | bytes 67592 | tf_op jit(solution)/shard_map/ppermute | solution.py:313
  166.3 0.8 collective-permute-start.7
  167.1 1.0 collective-permute-done.9.m3
  168.1 1.0 collective-permute-done.8.m2
  169.1 1.0 collective-permute-done.7.m1
  170.2 0.6 copy-done.8
  170.8 1.7 d_pooled.1
  172.5 11.1 %all-to-all-start.4 = ((bf16[16,4,2304]{2,1,0:T(4,128)(2,1)}), bf16[16,4,2304]{2,1,0:T(4,128)(2,1)S(1)}, u32[]{:S(2)}, u32[]{:S(2)}) async-start(bf16[16,4,2304]{2,1,0:T(4,128)(2,1)} %get-tuple-element.77), calls=%async_computation.4 | async-start | bytes 589824 | tf_op jit(solution)/shard_map/all_to_all | solution.py:494
  183.5 1.3 slice_reduce_fusion
  184.8 2.8 %d_tokens.1 = bf16[128,1280]{1,0:T(8,128)(2,1)} custom-call(bf16[2,640,128]{2,1,0:T(8,128)(2,1)} %get-tuple-element.43.table_ref, bf16[320,2,1280]{2,1,0:T(2,128)(2,1)} %bitcast.19, bf16[128,1280]{1,0:T(8,128)(2,1)} %grad_ref.5), custom_call_target="tpu_custom_call" | custom-call | flops 1 | bytes 1 | tf_op jit(solution)/shard_map/d_tokens/pallas_call | solution.py:60
  187.6 9.9 %d_w_in.1 = bf16[1280,1280]{1,0:T(8,128)(2,1)} custom-call(bf16[1280,1280]{1,0:T(8,128)(2,1)} %get-tuple-element.72.left_ref, bf16[1280,1280]{1,0:T(8,128)(2,1)} %get-tuple-element.73.right_ref), custom_call_target="tpu_custom_call" | custom-call | flops 1 | bytes 1 | tf_op jit(solution)/shard_map/d_w_in/pallas_call | solution.py:60
  197.6 0.1 reshape.63
  197.6 1.0 convolution_convert_fusion
  (30 shorter events, 0.1 us)
Async XLA Ops:
  3.7 38.0 %all-to-all-start = ((bf16[64,5,2,1408]{3,2,1,0:T(2,128)(2,1)}), bf16[64,5,2,1408]{3,2,1,0:T(2,128)(2,1)S(1)}, u32[]{:S(2)}, u32[]{:S(2)}) async-start(bf16[64,5,2,1408]{3,2,1,0:T(2,128)(2,1)} %bitcast.23), calls=%async_computation | async-start | bytes 3604480 | tf_op jit(solution)/shard_map/all_to_all | solution.py:411
  41.8 5.8 %copy-start = (bf16[64,5,2,1408]{3,2,1,0:T(2,128)(2,1)}, bf16[64,5,2,1408]{3,2,1,0:T(2,128)(2,1)S(1)}, u32[]{:S(2)}) copy-start(bf16[64,5,2,1408]{3,2,1,0:T(2,128)(2,1)S(1)} %all-to-all-done) | copy-start | bytes 5406724
  41.8 5.8 %collective-permute-start = (bf16[320,2,1408]{2,1,0:T(2,128)(2,1)S(1)}, bf16[320,2,1408]{2,1,0:T(2,128)(2,1)}, u32[]{:S(2)}, u32[]{:S(2)}) collective-permute-start(bf16[320,2,1408]{2,1,0:T(2,128)(2,1)S(1)} %bitcast.14), channel_id=1, source_target_pairs={{0,1},{1,0},{2,3},{3,2},{4,5},{5,4},{6,7},{7,6},{8,9},{9,8},{10,11... | collective-permute-start | bytes 5406728 | tf_op jit(solution)/shard_map/ppermute | solution.py:415
  41.8 31.3 %all-to-all-start.1 = ((bf16[64,5,2,1280]{3,2,1,0:T(2,128)(2,1)}), bf16[64,5,2,1280]{3,2,1,0:T(2,128)(2,1)S(1)}, u32[]{:S(2)}, u32[]{:S(2)}) async-start(bf16[64,5,2,1280]{3,2,1,0:T(2,128)(2,1)} %bitcast.21), calls=%async_computation.1 | async-start | bytes 3276800 | tf_op jit(solution)/shard_map/all_to_all | solution.py:411
  64.8 10.5 %collective-permute-start.1 = (bf16[640,1280]{1,0:T(8,128)(2,1)}, bf16[640,1280]{1,0:T(8,128)(2,1)}, u32[]{:S(2)}, u32[]{:S(2)}) collective-permute-start(bf16[640,1280]{1,0:T(8,128)(2,1)} %get-tuple-element.51), channel_id=1, source_target_pairs={{0,1},{1,0},{2,3},{3,2},{4,5},{5,4},{6,7},{7,6},{8,9},{9,8},{10,11... | collective-permute-start | bytes 4915208 | tf_op jit(solution)/shard_map/ppermute | solution.py:415
  73.1 2.1 %copy-start.1 = (bf16[64,5,2,1280]{3,2,1,0:T(2,128)(2,1)}, bf16[64,5,2,1280]{3,2,1,0:T(2,128)(2,1)S(1)}, u32[]{:S(2)}) copy-start(bf16[64,5,2,1280]{3,2,1,0:T(2,128)(2,1)S(1)} %all-to-all-done.1) | copy-start | bytes 4915204
  73.1 16.2 %collective-permute-start.2 = (bf16[320,2,1280]{2,1,0:T(2,128)(2,1)S(1)}, bf16[320,2,1280]{2,1,0:T(2,128)(2,1)S(1)}, u32[]{:S(2)}, u32[]{:S(2)}) collective-permute-start(bf16[320,2,1280]{2,1,0:T(2,128)(2,1)S(1)} %bitcast.17), channel_id=1, source_target_pairs={{0,1},{1,0},{2,3},{3,2},{4,5},{5,4},{6,7},{7,6},{8,9},{9,8},{10,11... | collective-permute-start | bytes 4915208 | tf_op jit(solution)/shard_map/ppermute | solution.py:415
  79.4 37.5 %all-to-all-start.2 = ((bf16[64,5,2,1280]{3,2,1,0:T(2,128)(2,1)}), bf16[64,5,2,1280]{3,2,1,0:T(2,128)(2,1)}, u32[]{:S(2)}, u32[]{:S(2)}) async-start(bf16[64,5,2,1280]{3,2,1,0:T(2,128)(2,1)} %bitcast.22), calls=%async_computation.2 | async-start | bytes 3276800 | tf_op jit(solution)/shard_map/all_to_all | solution.py:411
  89.3 1.2 copy-start.3
  106.8 13.3 %collective-permute-start.6 = (bf16[640,1280]{1,0:T(8,128)(2,1)}, bf16[640,1280]{1,0:T(8,128)(2,1)S(1)}, u32[]{:S(2)}, u32[]{:S(2)}) collective-permute-start(bf16[640,1280]{1,0:T(8,128)(2,1)} %get-tuple-element.65), channel_id=1, source_target_pairs={{0,1},{1,0},{2,3},{3,2},{4,5},{5,4},{6,7},{7,6},{8,9},{9,8},{10,11... | collective-permute-start | bytes 4915208 | tf_op jit(solution)/shard_map/ppermute | solution.py:415
  120.1 1.2 copy-start.4
  125.3 10.4 %copy-start.13 = (f32[1,1280]{1,0:T(1,128)S(1)}, f32[1,1280]{1,0:T(1,128)}, u32[]{:S(2)}) copy-start(f32[1,1280]{1,0:T(1,128)} %get-tuple-element.60) | copy-start | bytes 15364
  125.3 47.1 %all-to-all-start.3 = ((bf16[64,5,2,1280]{3,2,1,0:T(2,128)(2,1)}), bf16[64,5,2,1280]{3,2,1,0:T(2,128)(2,1)S(1)}, u32[]{:S(2)}, u32[]{:S(2)}) async-start(bf16[64,5,2,1280]{3,2,1,0:T(2,128)(2,1)} %bitcast.20), calls=%async_computation.3 | async-start | bytes 3276800 | tf_op jit(solution)/shard_map/all_to_all | solution.py:411
  138.3 14.2 %copy-start.9 = (f32[1,1280]{1,0:T(1,128)}, f32[1,1280]{1,0:T(1,128)S(1)}, u32[]{:S(2)}) copy-start(f32[1,1280]{1,0:T(1,128)S(1)} %psum.14.p0) | copy-start | bytes 15364
  138.3 11.0 %collective-permute-start.5 = (f32[1,1280]{1,0:T(1,128)S(1)}, f32[1,1280]{1,0:T(1,128)S(1)}, u32[]{:S(2)}, u32[]{:S(2)}) collective-permute-start(f32[1,1280]{1,0:T(1,128)S(1)} %psum.14.p0), channel_id=1, source_target_pairs={{6,0},{0,2},{2,4},{4,6},{7,1},{1,3},{3,5},{5,7},{14,8},{8,10},{10,... | collective-permute-start | bytes 15368 | tf_op jit(solution)/shard_map/ppermute | solution.py:313
  139.9 12.5 %collective-permute-start.4 = (f32[1,1280]{1,0:T(1,128)S(1)}, f32[1,1280]{1,0:T(1,128)S(1)}, u32[]{:S(2)}, u32[]{:S(2)}) collective-permute-start(f32[1,1280]{1,0:T(1,128)S(1)} %psum.14.p0), channel_id=1, source_target_pairs={{4,0},{6,2},{0,4},{2,6},{5,1},{7,3},{1,5},{3,7},{12,8},{14,10},{8,... | collective-permute-start | bytes 15368 | tf_op jit(solution)/shard_map/ppermute | solution.py:313
  142.6 9.9 %collective-permute-start.3 = (f32[1,1280]{1,0:T(1,128)S(1)}, f32[1,1280]{1,0:T(1,128)S(1)}, u32[]{:S(2)}, u32[]{:S(2)}) collective-permute-start(f32[1,1280]{1,0:T(1,128)S(1)} %psum.14.p0), channel_id=1, source_target_pairs={{2,0},{4,2},{6,4},{0,6},{3,1},{5,3},{7,5},{1,7},{10,8},{12,10},{14... | collective-permute-start | bytes 15368 | tf_op jit(solution)/shard_map/ppermute | solution.py:313
  149.3 3.2 %copy-start.10 = (f32[1,1280]{1,0:T(1,128)}, f32[1,1280]{1,0:T(1,128)S(1)}, u32[]{:S(2)}) copy-start(f32[1,1280]{1,0:T(1,128)S(1)} %collective-permute-done.5.p3) | copy-start | bytes 15364
  152.4 0.6 copy-start.11
  152.4 0.6 copy-start.12
  162.9 7.2 %copy-start.5 = (f32[4,1408]{1,0:T(4,128)}, f32[4,1408]{1,0:T(4,128)S(1)}, u32[]{:S(2)}) copy-start(f32[4,1408]{1,0:T(4,128)S(1)} %psum.15.m0) | copy-start | bytes 67588
  162.9 5.2 %collective-permute-start.9 = (f32[4,1408]{1,0:T(4,128)S(1)}, f32[4,1408]{1,0:T(4,128)S(1)}, u32[]{:S(2)}, u32[]{:S(2)}) collective-permute-start(f32[4,1408]{1,0:T(4,128)S(1)} %psum.15.m0), channel_id=1, source_target_pairs={{6,0},{0,2},{2,4},{4,6},{7,1},{1,3},{3,5},{5,7},{14,8},{8,10},{10,... | collective-permute-start | bytes 67592 | tf_op jit(solution)/shard_map/ppermute | solution.py:313
  163.8 5.3 %collective-permute-start.8 = (f32[4,1408]{1,0:T(4,128)S(1)}, f32[4,1408]{1,0:T(4,128)S(1)}, u32[]{:S(2)}, u32[]{:S(2)}) collective-permute-start(f32[4,1408]{1,0:T(4,128)S(1)} %psum.15.m0), channel_id=1, source_target_pairs={{4,0},{6,2},{0,4},{2,6},{5,1},{7,3},{1,5},{3,7},{12,8},{14,10},{8,... | collective-permute-start | bytes 67592 | tf_op jit(solution)/shard_map/ppermute | solution.py:313
  166.3 3.8 %collective-permute-start.7 = (f32[4,1408]{1,0:T(4,128)S(1)}, f32[4,1408]{1,0:T(4,128)S(1)}, u32[]{:S(2)}, u32[]{:S(2)}) collective-permute-start(f32[4,1408]{1,0:T(4,128)S(1)} %psum.15.m0), channel_id=1, source_target_pairs={{2,0},{4,2},{6,4},{0,6},{3,1},{5,3},{7,5},{1,7},{10,8},{12,10},{14... | collective-permute-start | bytes 67592 | tf_op jit(solution)/shard_map/ppermute | solution.py:313
  168.1 2.1 %copy-start.6 = (f32[4,1408]{1,0:T(4,128)}, f32[4,1408]{1,0:T(4,128)S(1)}, u32[]{:S(2)}) copy-start(f32[4,1408]{1,0:T(4,128)S(1)} %collective-permute-done.9.m3) | copy-start | bytes 67588
  169.1 1.1 copy-start.7
  170.1 0.6 copy-start.8
  172.4 12.4 %copy-start.2 = (bf16[64,5,2,1280]{3,2,1,0:T(2,128)(2,1)}, bf16[64,5,2,1280]{3,2,1,0:T(2,128)(2,1)S(1)}, u32[]{:S(2)}) copy-start(bf16[64,5,2,1280]{3,2,1,0:T(2,128)(2,1)S(1)} %all-to-all-done.3) | copy-start | bytes 4915204
  172.5 25.1 %all-to-all-start.4 = ((bf16[16,4,2304]{2,1,0:T(4,128)(2,1)}), bf16[16,4,2304]{2,1,0:T(4,128)(2,1)S(1)}, u32[]{:S(2)}, u32[]{:S(2)}) async-start(bf16[16,4,2304]{2,1,0:T(4,128)(2,1)} %get-tuple-element.77), calls=%async_computation.4 | async-start | bytes 589824 | tf_op jit(solution)/shard_map/all_to_all | solution.py:494

commit v4 on v3

--- a/solution.py
+++ b/solution.py
@@ -56,10 +56,11 @@
 LONG = pl.CostEstimate(flops=1 << 34, transcendentals=0, bytes_accessed=1 << 26)
 
 
-def run(body, outs, *args, specs=None, out_specs=None, scratch=(), name=None, cost=TINY):
+def run(body, outs, *args, grid=(), specs=None, out_specs=None, scratch=(), name=None, cost=TINY):
     return pl.pallas_call(
         body,
         out_shape=outs,
+        grid=grid,
         in_specs=specs or [VMEM] * len(args),
         out_specs=out_specs or jax.tree.map(lambda _: VMEM, outs),
         scratch_shapes=list(scratch),
@@ -112,27 +113,14 @@
     pack_rows(send_ref, scale * dot((table0 + table1).astype(BF16), grad_ref[...], 1, 0))
 
 
-CHUNK = 320
-STEPS = HALF // CHUNK
-
-
-def chunk_rows(base, i):
-    return pl.ds(pl.multiple_of(base + i * CHUNK, CHUNK), CHUNK)
-
-
-def chunk_copies(i, square, own, other, sems):
-    pairs = []
-    for vmem, hbm in square:
-        for base in (0, HALF):
-            rows = chunk_rows(base, i)
-            pairs.append((vmem.at[rows, :], hbm.at[rows, :]))
-    for vmem, hbm in (own, other):
-        rows = chunk_rows(0, i)
-        pairs.append((vmem.at[rows, :], hbm.at[rows, :]))
-    return [pltpu.make_async_copy(s, d, sems.at[i, n]) for n, (s, d) in enumerate(pairs)]
-
-
-def load(pairs, sems):
+HALVES = (slice(0, HALF), slice(HALF, ROWS))
+
+
+def chunks(part, size):
+    return [slice(n, n + size) for n in range(part.start, part.stop, size)]
+
+
+def start_all(pairs, sems):
     copies = [pltpu.make_async_copy(s, d, sems.at[n]) for n, (s, d) in enumerate(pairs)]
     for copy in copies:
         copy.start()
@@ -141,90 +129,78 @@
 
 def forward_body(
     own_in, other_in, w1_in, w2_in, xs_out, hidden_out, slope_out, own_out, other_out,
-    own_x, other_x, w1, w2, xs, hidden, slope, own, other, in_sems, xs_sem, out_sems,
+    own_x, other_x, w1, w2, xs, hidden, slope, own, other, in_sems, out_sems,
 ):
-    copies = load(((own_in, own_x), (other_in, other_x), (w1_in, w1), (w2_in, w2)), in_sems)
-    copies[0].wait()
-    xs[:HALF] = own_x[:, :, :D].reshape(HALF, D)
-    copies[1].wait()
-    xs[HALF:] = other_x[:, :, :D].reshape(HALF, D)
-    keep = pltpu.make_async_copy(xs, xs_out, xs_sem)
-    keep.start()
-    copies[2].wait()
-    copies[3].wait()
-
-    def outputs(i):
-        square = ((hidden, hidden_out), (slope, slope_out))
-        return chunk_copies(i, square, (own, own_out), (other, other_out), out_sems)
-
-    def step(i, carry):
-        for base in (0, HALF):
-            rows = chunk_rows(base, i)
+    pairs = ((own_in, own_x), (w1_in, w1), (other_in, other_x), (w2_in, w2))
+    copies = start_all(pairs, in_sems)
+    saved = []
+    for n, half in enumerate(HALVES):
+        copies[2 * n].wait()
+        xs[half] = (own_x, other_x)[n][:, :, :D].reshape(HALF, D)
+        if n == 0:
+            copies[1].wait()
+        for rows in chunks(half, 160):
             h = dot(xs[rows, :], w1[...], 1, 0)
             square = h * h
-            bend = jnp.tanh(ROOT_2_PI * h * (1.0 + CUBIC * square))
-            half = 0.5 * (1.0 + bend)
-            act = (h * half).astype(BF16)
-            hidden[rows, :] = act
-            slope[rows, :] = (
-                half
-                + 0.5 * h * (1.0 - bend * bend) * (ROOT_2_PI * (1.0 + 3.0 * CUBIC * square))
-            ).astype(BF16)
-            part = dot(act, w2[...], 1, 0)
-            if base == 0:
-                own[chunk_rows(0, i), :] = part
+            bend = jnp.tanh(h * (ROOT_2_PI + (ROOT_2_PI * CUBIC) * square))
+            act = 0.5 + 0.5 * bend
+            hidden[rows, :] = (h * act).astype(BF16)
+            tilt = (1.0 - bend * bend) * (0.5 * ROOT_2_PI + (1.5 * ROOT_2_PI * CUBIC) * square)
+            slope[rows, :] = (act + h * tilt).astype(BF16)
+        saved += start_all(
+            [(v.at[half], o.at[half]) for v, o in ((xs, xs_out), (hidden, hidden_out), (slope, slope_out))],
+            out_sems.at[n],
+        )
+        if n == 0:
+            copies[3].wait()
+        for rows in chunks(half, 160):
+            part = dot(hidden[rows, :], w2[...], 1, 0)
+            there = slice(rows.start - half.start, rows.stop - half.start)
+            if n == 0:
+                own[there, :] = part
             else:
-                other[chunk_rows(0, i), :] = part.astype(BF16)
-        for copy in outputs(i):
-            copy.start()
-        return carry
-
-    lax.fori_loop(0, STEPS, step, 0)
-    keep.wait()
-    for i in range(STEPS):
-        for copy in outputs(i):
-            copy.wait()
+                other[there, :] = part.astype(BF16)
+        saved += start_all([((own, other)[n], (own_out, other_out)[n])], out_sems.at[2 + n])
+    for copy in saved:
+        copy.wait()
 
 
 def backward_body(
     own_in, other_in, slope_in, w1_in, w2_in, gs_out, d_pre_out, own_out, other_out,
-    own_g, other_g, slope, w1, w2, gs, d_pre, own, other, in_sems, gs_sem, out_sems,
+    own_g, other_g, slope, w1, w2, gs, d_pre, own, other, in_sems, out_sems,
 ):
-    pairs = ((own_in, own_g), (other_in, other_g), (w2_in, w2), (slope_in, slope), (w1_in, w1))
-    copies = load(pairs, in_sems)
-    copies[0].wait()
-    gs[:HALF] = own_g[...].reshape(HALF, D)
-    copies[1].wait()
-    gs[HALF:] = other_g[...].reshape(HALF, D)
-    keep = pltpu.make_async_copy(gs, gs_out, gs_sem)
-    keep.start()
-    for copy in copies[2:]:
+    first, last = HALVES
+    pairs = (
+        (own_in, own_g), (w2_in, w2), (slope_in.at[first], slope.at[first]), (w1_in, w1),
+        (other_in, other_g), (slope_in.at[last], slope.at[last]),
+    )
+    copies = start_all(pairs, in_sems)
+    saved = []
+    for n, half in enumerate(HALVES):
+        copies[4 * n].wait()
+        gs[half] = (own_g, other_g)[n][...].reshape(HALF, D)
+        if n == 0:
+            copies[1].wait()
+        copies[(2, 5)[n]].wait()
+        for rows in chunks(half, 320):
+            d_h = dot(gs[rows, :], w2[...], 1, 1)
+            d_pre[rows, :] = (d_h * slope[rows, :].astype(F32)).astype(BF16)
+        saved += start_all(
+            [(v.at[half], o.at[half]) for v, o in ((gs, gs_out), (d_pre, d_pre_out))],
+            out_sems.at[n],
+        )
+        if n == 0:
+            copies[3].wait()
+        for rows in chunks(half, 320):
+            part = dot(d_pre[rows, :], w1[...], 1, 1)
+            there = slice(rows.start - half.start, rows.stop - half.start)
+            if n == 0:
+                own[there, :] = part
+            else:
+                other[there, :] = part.astype(BF16)
+        saved += start_all([((own, other)[n], (own_out, other_out)[n])], out_sems.at[2 + n])
+    for copy in saved:
         copy.wait()
-
-    def outputs(i):
-        square = ((d_pre, d_pre_out),)
-        return chunk_copies(i, square, (own, own_out), (other, other_out), out_sems)
-
-    def step(i, carry):
-        for base in (0, HALF):
-            rows = chunk_rows(base, i)
-            d_h = dot(gs[rows, :], w2[...], 1, 1)
-            act = (d_h * slope[rows, :].astype(F32)).astype(BF16)
-            d_pre[rows, :] = act
-            part = dot(act, w1[...], 1, 1)
-            if base == 0:
-                own[chunk_rows(0, i), :] = part
-            else:
-                other[chunk_rows(0, i), :] = part.astype(BF16)
-        for copy in outputs(i):
-            copy.start()
-        return carry
-
-    lax.fori_loop(0, STEPS, step, 0)
-    keep.wait()
-    for i in range(STEPS):
-        for copy in outputs(i):
-            copy.wait()
 
 
 SQUARE = (ROWS, D)
@@ -237,9 +213,8 @@
     scratch += [pltpu.VMEM(SQUARE, BF16)] * (kept if len(ins) == 4 else 2)
     scratch += [pltpu.VMEM((HALF, D), F32), pltpu.VMEM((HALF, D), BF16)]
     scratch += [
-        pltpu.SemaphoreType.DMA((len(ins),)),
-        pltpu.SemaphoreType.DMA,
-        pltpu.SemaphoreType.DMA((STEPS, 6)),
+        pltpu.SemaphoreType.DMA((6,)),
+        pltpu.SemaphoreType.DMA((4, 3)),
     ]
     return run(
         body,
@@ -252,20 +227,45 @@
     )
 
 
-GRAD_COLS = 256
+GRAD_COLS = 640
 
 
 def weight_grad_body(left_ref, right_ref, out_ref):
-    def step(i, carry):
-        cols = pl.ds(pl.multiple_of(i * GRAD_COLS, GRAD_COLS), GRAD_COLS)
-        out_ref[cols, :] = dot(left_ref[:, cols], right_ref[...], 0, 0).astype(BF16)
-        return carry
-
-    lax.fori_loop(0, D // GRAD_COLS, step, 0)
+    out_ref[...] = dot(left_ref[...], right_ref[...], 0, 0).astype(BF16)
+
+
+def weight_grad(left, right, name):
+    return run(
+        weight_grad_body,
+        shape((D, D), BF16),
+        left,
+        right,
+        grid=(D // GRAD_COLS,),
+        specs=[pl.BlockSpec((ROWS, GRAD_COLS), lambda i: (0, i)), pl.BlockSpec((ROWS, D), lambda i: (0, 0))],
+        out_specs=pl.BlockSpec((GRAD_COLS, D), lambda i: (i, 0)),
+        name=name,
+    )
 
 
 def add_body(own_ref, other_ref, send_ref):
     pack_rows(send_ref, own_ref[...] + other_ref[...].astype(F32))
+
+
+ADD_ROWS = 320
+
+
+def add_cores(own, other, name):
+    rows = pl.BlockSpec((ADD_ROWS, D), lambda i: (i, 0))
+    return run(
+        add_body,
+        shape(PACKED, BF16),
+        own,
+        other,
+        grid=(HALF // ADD_ROWS,),
+        specs=[rows, rows],
+        out_specs=pl.BlockSpec((ADD_ROWS // 2, 2, D), lambda i: (i, 0, 0)),
+        name=name,
+    )
 
 
 def across(row):
@@ -360,7 +360,10 @@
     mean = jnp.mean(d_normed, axis=1, keepdims=True)
     along = jnp.mean(d_normed * normed, axis=1, keepdims=True)
     d_ref[...] = scale * (d_normed - mean - normed * along)
-    loss_ref[...] = total[:, D:]
+    diagonal = lax.broadcasted_iota(I32, (4, 4), 0) == lax.broadcasted_iota(I32, (4, 4), 1)
+    loss_ref[...] = jnp.sum(
+        jnp.where(diagonal, total[:, D : D + 1], 0.0), axis=0, keepdims=True
+    )
 
 
 def effective_of(counts):
@@ -435,7 +438,7 @@
         forward_body, (x_in, core_swap(x_in), w_in, w_out), 3, PACKED_X, "forward"
     )
     other = core_swap(other)
-    digits = x_in.reshape(IMAGES // 4, 4, CAP, WIDE)[:, 0, :4, D : D + 128].reshape(IMAGES, 128)
+    digits = x_in.reshape(16, 2 * CAP, 2, WIDE)[:, :2, :, D:].reshape(IMAGES, 128)
     g_in, digits = lax.optimization_barrier((g_in, digits))
     targets, class_weight = run(
         label_body,
@@ -448,13 +451,11 @@
         cost=LONG,
     )
     own, class_weight = lax.optimization_barrier((own, class_weight))
-    out_in = chip_swap(run(add_body, shape(PACKED, BF16), own, other, name="add_out"))
+    out_in = chip_swap(add_cores(own, other, "add_out"))
     gs, d_pre, own, other = expert_kernel(
         backward_body, (g_in, core_swap(g_in), slope, w_in, w_out), 2, PACKED, "backward"
     )
     other = core_swap(other)
-    d_w_out = run(weight_grad_body, shape((D, D), BF16), hidden, gs, name="d_w_out")
-    out_in, d_w_out = lax.optimization_barrier((out_in, d_w_out))
     mixed_out, d_combine, token_sum = run(
         mixed_body,
         (shape((TOK, D), BF16), shape((2, TOK), F32), shape((1, D), F32)),
@@ -466,9 +467,11 @@
         name="mixed",
         cost=LONG,
     )
+    token_sum = lax.psum(token_sum, "core")
     own, token_sum = lax.optimization_barrier((own, token_sum))
-    rows_in = chip_swap(run(add_body, shape(PACKED, BF16), own, other, name="add_rows"))
-    sums = y_parts(lax.psum(token_sum, "core"))
+    rows_send = add_cores(own, other, "add_rows")
+    rows_send, *sums = lax.optimization_barrier((rows_send, *y_parts(token_sum)))
+    rows_in = chip_swap(rows_send)
     pooled, part, dp_send = run(
         head_body,
         (shape((4, D), F32), shape((4, D + 128), F32), shape((16, 4, COLS + 128), BF16)),
@@ -480,10 +483,13 @@
         specs=[SMEM] + [VMEM] * 7,
         name="head",
     )
+    hidden, part = lax.optimization_barrier((hidden, part))
+    d_w_out = weight_grad(hidden, gs, "d_w_out")
     messages = y_parts(lax.psum(part, "core"))
+    pooled, d_w_out = lax.optimization_barrier((pooled, d_w_out))
     d_pooled, losses = run(
         pooled_body,
-        (shape((4, D), F32), shape((4, 128), F32)),
+        (shape((4, D), F32), shape((1, 4), F32)),
         here,
         *messages,
         pooled,
@@ -493,9 +499,9 @@
     dp_send, rows_in, xs, d_pooled = lax.optimization_barrier((dp_send, rows_in, xs, d_pooled))
     dp_in = lax.all_to_all(dp_send, "dp", 0, 0, tiled=True).reshape(IMAGES, COLS + 128)
     d_tokens = run(tokens_body, shape((TOK, D), BF16), table, rows_in, out_grad, name="d_tokens")
-    d_w_in = run(weight_grad_body, shape((D, D), BF16), xs, d_pre, name="d_w_in")
+    d_w_in = weight_grad(xs, d_pre, "d_w_in")
     d_head = dot(dp_in[:, COLS : COLS + 80], dp_in[:, :COLS], 0, 0).astype(BF16)
-    return (mixed_out, d_tokens, d_combine.T, d_w_in, d_w_out, losses[:, 0], d_pooled, d_head)
+    return (mixed_out, d_tokens, d_combine.T, d_w_in, d_w_out, losses.reshape(4), d_pooled, d_head)
 
 
 def solution(mesh):

time: 200 us -> 179 us (0.90)
  starting transfers between devices: 59 us -> 47.3 us
  Pallas kernels: 83.4 us -> 73.7 us
  local copies, waits for them, and re-layouts: 11.8 us -> 4.97 us
  waiting for transfers between devices: 36.2 us -> 42.9 us
    all_to_all x4, waiting for transfers between devices: 24.7 us -> 42.9 us  [chip_swap(): return lax.all_to_all(blocks, CHIP, 0, 0, tiled=True).reshape(dims)]
    ppermute x6, waiting for transfers between devices: 11.5 us -> 0.02 us  [y_parts(): lax.ppermute(mine, Y, [((i + shift) % 4, i) for i in range(4)])]
    pallas_call x13, Pallas kernels: 83.4 us -> 73.7 us  [run(): pl.pallas_call(body, out_shape=outs, grid=grid, in_specs=specs or [VMEM]...]
    all_to_all x4, starting transfers between devices: 37.6 us -> 29.9 us  [chip_swap(): return lax.all_to_all(blocks, CHIP, 0, 0, tiled=True).reshape(dims)]
    reshape x1 -> x0, local copies, waits for them, and re-layouts: 5.5 us -> none  [shards(): x_in.reshape(IMAGES // 4, 4, CAP, WIDE)[:, 0, :4, D:D + 128]]
    all_to_all x1, starting transfers between devices: 11.1 us -> 6.94 us  [shards(): lax.all_to_all(dp_send, 'dp', 0, 0, tiled=True).reshape(IMAGES, COLS + 128)]
  transfers between devices with their start and end apart: 15 -> 15, of which waited for: 7 -> 3; matrix products, arithmetic and copies ran while one was open for 4% -> 1% of each run, Pallas kernels for 38% -> 40%
where the time goes in v4:
time: 179 us; the launch traced here: 177 us
  Pallas kernels  73.7 us (41%)
  starting transfers between devices  47.3 us (26%)
  waiting for transfers between devices  42.9 us (24%)
  blocking collectives  6.6 us (4%)
  local copies, waits for them, and re-layouts  4.97 us (3%)
    pallas_call x13, Pallas kernels, run(): pl.pallas_call(body, out_shape=outs, grid=grid, in_specs=specs or [VMEM]...  73.7 us
    all_to_all x4, waiting for transfers between devices, chip_swap(): return lax.all_to_all(blocks, CHIP, 0, 0, tiled=True).reshape(dims)  42.9 us
    all_to_all x4, starting transfers between devices, chip_swap(): return lax.all_to_all(blocks, CHIP, 0, 0, tiled=True).reshape(dims)  29.9 us
    ppermute x6, starting transfers between devices, y_parts(): lax.ppermute(mine, Y, [((i + shift) % 4, i) for i in range(4)])  9.86 us
    all_to_all x1, starting transfers between devices, shards(): lax.all_to_all(dp_send, 'dp', 0, 0, tiled=True).reshape(IMAGES, COLS + 128)  6.94 us
    psum x1, blocking collectives, shards(): messages = y_parts(lax.psum(part, 'core'))  4.01 us
  transfers between devices with their start and end apart: 15, of which 3 were waited for; matrix products, arithmetic and copies ran while one was open for 1% of the time, Pallas kernels for 40%

profile of v4, /device:TPU:0, one launch (start us, length us, event | category | flops | bytes accessed | tf_op | source)
XLA Modules:
  0.0 177.3 jit_solution(11785409224664289715)
XLA Ops:
  0.6 3.1 %dispatch_x.1 = (bf16[2,640,128]{2,1,0:T(8,128)(2,1)}, bf16[320,2,1408]{2,1,0:T(2,128)(2,1)}) custom-call(s32[2,128]{1,0:T(2,128)} %bitcast.27, s32[4,4]{1,0:T(4,128)} %labels_ref.3, bf16[128,1280]{1,0:T(8,128)(2,1)} %tokens_ref.3), custom_call_target="tpu_custom_call" | custom-call | flops 1 | bytes 1 | tf_op jit(solution)/shard_map/dispatch_x/pallas_call | solution.py:60
  3.7 11.5 %all-to-all-start = ((bf16[64,5,2,1408]{3,2,1,0:T(2,128)(2,1)}), bf16[64,5,2,1408]{3,2,1,0:T(2,128)(2,1)S(1)}, u32[]{:S(2)}, u32[]{:S(2)}) async-start(bf16[64,5,2,1408]{3,2,1,0:T(2,128)(2,1)} %bitcast.25), calls=%async_computation | async-start | bytes 3604480 | tf_op jit(solution)/shard_map/all_to_all | solution.py:414
  15.2 3.1 %dispatch_g.1 = bf16[320,2,1280]{2,1,0:T(2,128)(2,1)} custom-call(bf16[2,640,128]{2,1,0:T(8,128)(2,1)} %get-tuple-element.50.table_ref, bf16[128,1280]{1,0:T(8,128)(2,1)} %grad_ref.5, f32[2,128]{1,0:T(2,128)} %bitcast.28), custom_call_target="tpu_custom_call" | custom-call | flops 1 | bytes 1 | tf_op jit(solution)/shard_map/dispatch_g/pallas_call | solution.py:60
  18.3 23.5 %all-to-all-done = bf16[64,5,2,1408]{3,2,1,0:T(2,128)(2,1)S(1)} async-done(((bf16[64,5,2,1408]{3,2,1,0:T(2,128)(2,1)}), bf16[64,5,2,1408]{3,2,1,0:T(2,128)(2,1)S(1)}, u32[]{:S(2)}, u32[]{:S(2)}) %all-to-all-start) | async-done | bytes 1802272 | tf_op jit(solution)/shard_map/all_to_all | solution.py:414
  41.8 6.0 %all-to-all-start.1 = ((bf16[64,5,2,1280]{3,2,1,0:T(2,128)(2,1)}), bf16[64,5,2,1280]{3,2,1,0:T(2,128)(2,1)S(1)}, u32[]{:S(2)}, u32[]{:S(2)}) async-start(bf16[64,5,2,1280]{3,2,1,0:T(2,128)(2,1)} %bitcast.23), calls=%async_computation.1 | async-start | bytes 3276800 | tf_op jit(solution)/shard_map/all_to_all | solution.py:414
  47.8 0.0 collective-permute-done.other_in
  47.8 14.6 %forward.1 = (bf16[1280,1280]{1,0:T(8,128)(2,1)}, bf16[1280,1280]{1,0:T(8,128)(2,1)}, bf16[1280,1280]{1,0:T(8,128)(2,1)}, f32[640,1280]{1,0:T(8,128)}, bf16[640,1280]{1,0:T(8,128)(2,1)}) custom-call(bf16[320,2,1408]{2,1,0:T(2,128)(2,1)} %bitcast.17, bf16[320,2,1408]{2,1,0:T(2,128)(2,1)} %collective-permute-done.other_in, bf16[1280,1280]{1,0:T(8,128)(2,1)} %w1_in.3, ...), custom_call_target="tpu_custom_call" | custom-call | flops 1 | bytes 1 | tf_op jit(solution)/shard_map/forward/pallas_call | solution.py:60
  62.5 0.3 collective-permute-start.1
  62.8 1.3 slice.12
  64.1 9.0 %all-to-all-done.1 = bf16[64,5,2,1280]{3,2,1,0:T(2,128)(2,1)S(1)} async-done(((bf16[64,5,2,1280]{3,2,1,0:T(2,128)(2,1)}), bf16[64,5,2,1280]{3,2,1,0:T(2,128)(2,1)S(1)}, u32[]{:S(2)}, u32[]{:S(2)}) %all-to-all-start.1) | async-done | bytes 1638432 | tf_op jit(solution)/shard_map/all_to_all | solution.py:414
  73.1 0.0 collective-permute-start.2
  73.1 2.1 %labels.1 = (f32[4,2176]{1,0:T(4,128)}, f32[1,2176]{1,0:T(1,128)}) custom-call(s32[1]{0:T(128)} %bitcast.4.first_ref, bf16[64,128]{1,0:T(8,128)(2,1)} %bitcast.26, s32[4,4]{1,0:T(4,128)} %labels_ref.3), custom_call_target="tpu_custom_call" | custom-call | flops 17179869184 | bytes 67108864 | tf_op jit(solution)/shard_map/labels/pallas_call | solution.py:60
  75.3 0.0 collective-permute-done.1.other_ref
  75.3 3.5 %add_out.1 = bf16[320,2,1280]{2,1,0:T(2,128)(2,1)} custom-call(f32[640,1280]{1,0:T(8,128)} %get-tuple-element.57.own_ref, bf16[640,1280]{1,0:T(8,128)(2,1)} %collective-permute-done.1.other_ref), custom_call_target="tpu_custom_call" | custom-call | flops 1 | bytes 1 | tf_op jit(solution)/shard_map/add_out/pallas_call | solution.py:60
  78.8 6.0 %all-to-all-start.2 = ((bf16[64,5,2,1280]{3,2,1,0:T(2,128)(2,1)}), bf16[64,5,2,1280]{3,2,1,0:T(2,128)(2,1)}, u32[]{:S(2)}, u32[]{:S(2)}) async-start(bf16[64,5,2,1280]{3,2,1,0:T(2,128)(2,1)} %bitcast.24), calls=%async_computation.2 | async-start | bytes 3276800 | tf_op jit(solution)/shard_map/all_to_all | solution.py:414
  84.9 1.2 copy-done.3
  86.1 13.5 %backward.1 = (bf16[1280,1280]{1,0:T(8,128)(2,1)}, bf16[1280,1280]{1,0:T(8,128)(2,1)}, f32[640,1280]{1,0:T(8,128)}, bf16[640,1280]{1,0:T(8,128)(2,1)}) custom-call(bf16[320,2,1280]{2,1,0:T(2,128)(2,1)} %bitcast.20, bf16[320,2,1280]{2,1,0:T(2,128)(2,1)} %copy-done.3, bf16[1280,1280]{1,0:T(8,128)(2,1)} %get-tuple-element.61.slope_in, ...), custom_call_target="tpu_custom_call" | custom-call | flops 1 | bytes 1 | tf_op jit(solution)/shard_map/backward/pallas_call | solution.py:60
  99.5 0.3 collective-permute-start.3
  99.8 10.4 %all-to-all-done.2 = bf16[64,5,2,1280]{3,2,1,0:T(2,128)(2,1)} async-done(((bf16[64,5,2,1280]{3,2,1,0:T(2,128)(2,1)}), bf16[64,5,2,1280]{3,2,1,0:T(2,128)(2,1)}, u32[]{:S(2)}, u32[]{:S(2)}) %all-to-all-start.2) | async-done | bytes 1638432 | tf_op jit(solution)/shard_map/all_to_all | solution.py:414
  110.2 3.2 %mixed.1 = (bf16[128,1280]{1,0:T(8,128)(2,1)}, f32[2,128]{1,0:T(2,128)}, f32[1,1280]{1,0:T(1,128)}) custom-call(bf16[2,640,128]{2,1,0:T(8,128)(2,1)} %get-tuple-element.50.table_ref, bf16[320,2,1280]{2,1,0:T(2,128)(2,1)} %bitcast.10.in_ref, bf16[128,1280]{1,0:T(8,128)(2,1)} %tokens_ref.3, bf16[128,1280]{1,0:T(8,128)(2,1)} %grad_ref.5, f32[2,128]{1,0:T(2,128)} %bitcast.29), custom_call_target="tpu_custom_call" | custom-call | flops 17179869184 | bytes 67108864 | tf_op jit(solution)/shard_map/mixed/pallas_call | solution.py:60
  113.4 2.6 %psum.14.p0 = f32[1,1280]{1,0:T(1,128)S(1)} all-reduce(f32[1,1280]{1,0:T(1,128)} %get-tuple-element.63), channel_id=1, replica_groups=mesh['dp'=16,'yh'=2,'yl'=2,'core'=2] {'core'}, use_global_device_ids=true, to_apply=%region_0.0 | all-reduce | flops 1280 | bytes 10240 | tf_op jit(solution)/shard_map/psum | solution.py:470
  116.0 0.9 collective-permute-start.6
  116.9 1.4 collective-permute-start.5
  118.4 2.0 %collective-permute-start.4 = (f32[1,1280]{1,0:T(1,128)S(1)}, f32[1,1280]{1,0:T(1,128)S(1)}, u32[]{:S(2)}, u32[]{:S(2)}) collective-permute-start(f32[1,1280]{1,0:T(1,128)S(1)} %psum.14.p0), channel_id=1, source_target_pairs={{2,0},{4,2},{6,4},{0,6},{3,1},{5,3},{7,5},{1,7},{10,8},{12,10},{14... | collective-permute-start | bytes 15368 | tf_op jit(solution)/shard_map/ppermute | solution.py:313
  120.4 1.2 copy-done.4
  121.5 3.5 %add_rows.1 = bf16[320,2,1280]{2,1,0:T(2,128)(2,1)} custom-call(f32[640,1280]{1,0:T(8,128)} %get-tuple-element.64.own_ref, bf16[640,1280]{1,0:T(8,128)(2,1)} %copy-done.4), custom_call_target="tpu_custom_call" | custom-call | flops 1 | bytes 1 | tf_op jit(solution)/shard_map/add_rows/pallas_call | solution.py:60
  125.1 0.0 collective-permute-done.6.p3
  125.1 0.0 collective-permute-done.5.p2
  125.1 6.4 %all-to-all-start.3 = ((bf16[64,5,2,1280]{3,2,1,0:T(2,128)(2,1)}), bf16[64,5,2,1280]{3,2,1,0:T(2,128)(2,1)S(1)}, u32[]{:S(2)}, u32[]{:S(2)}) async-start(bf16[64,5,2,1280]{3,2,1,0:T(2,128)(2,1)} %bitcast.22), calls=%async_computation.3 | async-start | bytes 3276800 | tf_op jit(solution)/shard_map/all_to_all | solution.py:414
  131.5 5.9 %head.1 = (f32[4,1280]{1,0:T(4,128)}, f32[4,1408]{1,0:T(4,128)}, bf16[16,4,2304]{2,1,0:T(4,128)(2,1)}) custom-call(s32[1]{0:T(128)} %bitcast.11.here_ref, f32[1,1280]{1,0:T(1,128)} %copy-done.9, f32[1,1280]{1,0:T(1,128)} %copy-done.12, f32[1,1280]{1,0:T(1,128)} %copy-done.11, f32[1,1280]{1,0:T(1,128)} %copy-done.10, f32[4,2176]{1,0:T(4,128)} %get-tuple-element.71.target_ref, ...), custom_call_target="tpu_custom_call" | custom-call | flops 1 | bytes 1 | tf_op jit(solution)/shard_map/head/pallas_call | solution.py:60
  137.4 4.0 %psum.15.m0 = f32[4,1408]{1,0:T(4,128)S(1)} all-reduce(f32[4,1408]{1,0:T(4,128)} %get-tuple-element.78), channel_id=1, replica_groups=mesh['dp'=16,'yh'=2,'yl'=2,'core'=2] {'core'}, use_global_device_ids=true, to_apply=%region_1.0 | all-reduce | flops 5632 | bytes 45056 | tf_op jit(solution)/shard_map/psum | solution.py:488
  141.4 0.0 copy-start.5
  141.5 1.4 collective-permute-start.9
  142.8 2.7 %collective-permute-start.8 = (f32[4,1408]{1,0:T(4,128)S(1)}, f32[4,1408]{1,0:T(4,128)S(1)}, u32[]{:S(2)}, u32[]{:S(2)}) collective-permute-start(f32[4,1408]{1,0:T(4,128)S(1)} %psum.15.m0), channel_id=1, source_target_pairs={{4,0},{6,2},{0,4},{2,6},{5,1},{7,3},{1,5},{3,7},{12,8},{14,10},{8,... | collective-permute-start | bytes 67592 | tf_op jit(solution)/shard_map/ppermute | solution.py:313
  145.5 1.5 collective-permute-start.7
  147.0 8.3 %d_w_out.1 = bf16[1280,1280]{1,0:T(8,128)(2,1)} custom-call(bf16[1280,1280]{1,0:T(8,128)(2,1)} %get-tuple-element.80.left_ref, bf16[1280,1280]{1,0:T(8,128)(2,1)} %get-tuple-element.81.right_ref), custom_call_target="tpu_custom_call" | custom-call | flops 1 | bytes 1 | tf_op jit(solution)/shard_map/d_w_out/pallas_call | solution.py:60
  155.2 0.0 collective-permute-done.9.m3
  155.2 0.0 collective-permute-done.8.m2
  155.3 0.0 collective-permute-done.7.m1
  155.3 0.6 copy-done.6
  155.8 0.0 copy-done.7
  155.9 0.6 copy-done.8
  156.5 1.7 d_pooled.1
  158.2 6.9 %all-to-all-start.4 = ((bf16[16,4,2304]{2,1,0:T(4,128)(2,1)}), bf16[16,4,2304]{2,1,0:T(4,128)(2,1)S(1)}, u32[]{:S(2)}, u32[]{:S(2)}) async-start(bf16[16,4,2304]{2,1,0:T(4,128)(2,1)} %get-tuple-element.91), calls=%async_computation.4 | async-start | bytes 589824 | tf_op jit(solution)/shard_map/all_to_all | solution.py:500
  165.1 2.8 %d_tokens.1 = bf16[128,1280]{1,0:T(8,128)(2,1)} custom-call(bf16[2,640,128]{2,1,0:T(8,128)(2,1)} %get-tuple-element.50.table_ref, bf16[320,2,1280]{2,1,0:T(2,128)(2,1)} %bitcast.21, bf16[128,1280]{1,0:T(8,128)(2,1)} %grad_ref.5), custom_call_target="tpu_custom_call" | custom-call | flops 1 | bytes 1 | tf_op jit(solution)/shard_map/d_tokens/pallas_call | solution.py:60
  167.9 8.3 %d_w_in.1 = bf16[1280,1280]{1,0:T(8,128)(2,1)} custom-call(bf16[1280,1280]{1,0:T(8,128)(2,1)} %get-tuple-element.86.left_ref, bf16[1280,1280]{1,0:T(8,128)(2,1)} %get-tuple-element.87.right_ref), custom_call_target="tpu_custom_call" | custom-call | flops 1 | bytes 1 | tf_op jit(solution)/shard_map/d_w_in/pallas_call | solution.py:60
  176.2 0.1 reshape.71
  176.3 1.0 convolution_convert_fusion
  (26 shorter events, 0.1 us)
Async XLA Ops:
  3.7 38.0 %all-to-all-start = ((bf16[64,5,2,1408]{3,2,1,0:T(2,128)(2,1)}), bf16[64,5,2,1408]{3,2,1,0:T(2,128)(2,1)S(1)}, u32[]{:S(2)}, u32[]{:S(2)}) async-start(bf16[64,5,2,1408]{3,2,1,0:T(2,128)(2,1)} %bitcast.25), calls=%async_computation | async-start | bytes 3604480 | tf_op jit(solution)/shard_map/all_to_all | solution.py:414
  41.8 6.0 %copy-start = (bf16[64,5,2,1408]{3,2,1,0:T(2,128)(2,1)}, bf16[64,5,2,1408]{3,2,1,0:T(2,128)(2,1)S(1)}, u32[]{:S(2)}) copy-start(bf16[64,5,2,1408]{3,2,1,0:T(2,128)(2,1)S(1)} %all-to-all-done) | copy-start | bytes 5406724
  41.8 6.0 %collective-permute-start = (bf16[320,2,1408]{2,1,0:T(2,128)(2,1)S(1)}, bf16[320,2,1408]{2,1,0:T(2,128)(2,1)}, u32[]{:S(2)}, u32[]{:S(2)}) collective-permute-start(bf16[320,2,1408]{2,1,0:T(2,128)(2,1)S(1)} %bitcast.16), channel_id=1, source_target_pairs={{0,1},{1,0},{2,3},{3,2},{4,5},{5,4},{6,7},{7,6},{8,9},{9,8},{10,11... | collective-permute-start | bytes 5406728 | tf_op jit(solution)/shard_map/ppermute | solution.py:418
  41.8 31.3 %all-to-all-start.1 = ((bf16[64,5,2,1280]{3,2,1,0:T(2,128)(2,1)}), bf16[64,5,2,1280]{3,2,1,0:T(2,128)(2,1)S(1)}, u32[]{:S(2)}, u32[]{:S(2)}) async-start(bf16[64,5,2,1280]{3,2,1,0:T(2,128)(2,1)} %bitcast.23), calls=%async_computation.1 | async-start | bytes 3276800 | tf_op jit(solution)/shard_map/all_to_all | solution.py:414
  62.5 12.8 %collective-permute-start.1 = (bf16[640,1280]{1,0:T(8,128)(2,1)}, bf16[640,1280]{1,0:T(8,128)(2,1)}, u32[]{:S(2)}, u32[]{:S(2)}) collective-permute-start(bf16[640,1280]{1,0:T(8,128)(2,1)} %get-tuple-element.58), channel_id=1, source_target_pairs={{0,1},{1,0},{2,3},{3,2},{4,5},{5,4},{6,7},{7,6},{8,9},{9,8},{10,11... | collective-permute-start | bytes 4915208 | tf_op jit(solution)/shard_map/ppermute | solution.py:418
  73.1 2.1 %copy-start.1 = (bf16[64,5,2,1280]{3,2,1,0:T(2,128)(2,1)}, bf16[64,5,2,1280]{3,2,1,0:T(2,128)(2,1)S(1)}, u32[]{:S(2)}) copy-start(bf16[64,5,2,1280]{3,2,1,0:T(2,128)(2,1)S(1)} %all-to-all-done.1) | copy-start | bytes 4915204
  73.1 11.7 %collective-permute-start.2 = (bf16[320,2,1280]{2,1,0:T(2,128)(2,1)S(1)}, bf16[320,2,1280]{2,1,0:T(2,128)(2,1)S(1)}, u32[]{:S(2)}, u32[]{:S(2)}) collective-permute-start(bf16[320,2,1280]{2,1,0:T(2,128)(2,1)S(1)} %bitcast.19), channel_id=1, source_target_pairs={{0,1},{1,0},{2,3},{3,2},{4,5},{5,4},{6,7},{7,6},{8,9},{9,8},{10,11... | collective-permute-start | bytes 4915208 | tf_op jit(solution)/shard_map/ppermute | solution.py:418
  78.8 31.4 %all-to-all-start.2 = ((bf16[64,5,2,1280]{3,2,1,0:T(2,128)(2,1)}), bf16[64,5,2,1280]{3,2,1,0:T(2,128)(2,1)}, u32[]{:S(2)}, u32[]{:S(2)}) async-start(bf16[64,5,2,1280]{3,2,1,0:T(2,128)(2,1)} %bitcast.24), calls=%async_computation.2 | async-start | bytes 3276800 | tf_op jit(solution)/shard_map/all_to_all | solution.py:414
  84.9 1.2 copy-start.3
  99.5 20.8 %collective-permute-start.3 = (bf16[640,1280]{1,0:T(8,128)(2,1)}, bf16[640,1280]{1,0:T(8,128)(2,1)S(1)}, u32[]{:S(2)}, u32[]{:S(2)}) collective-permute-start(bf16[640,1280]{1,0:T(8,128)(2,1)} %get-tuple-element.65), channel_id=1, source_target_pairs={{0,1},{1,0},{2,3},{3,2},{4,5},{5,4},{6,7},{7,6},{8,9},{9,8},{10,11... | collective-permute-start | bytes 4915208 | tf_op jit(solution)/shard_map/ppermute | solution.py:418
  116.0 15.5 %copy-start.9 = (f32[1,1280]{1,0:T(1,128)}, f32[1,1280]{1,0:T(1,128)S(1)}, u32[]{:S(2)}) copy-start(f32[1,1280]{1,0:T(1,128)S(1)} %psum.14.p0) | copy-start | bytes 15364
  116.0 9.1 %collective-permute-start.6 = (f32[1,1280]{1,0:T(1,128)S(1)}, f32[1,1280]{1,0:T(1,128)S(1)}, u32[]{:S(2)}, u32[]{:S(2)}) collective-permute-start(f32[1,1280]{1,0:T(1,128)S(1)} %psum.14.p0), channel_id=1, source_target_pairs={{6,0},{0,2},{2,4},{4,6},{7,1},{1,3},{3,5},{5,7},{14,8},{8,10},{10,... | collective-permute-start | bytes 15368 | tf_op jit(solution)/shard_map/ppermute | solution.py:313
  116.9 8.1 %collective-permute-start.5 = (f32[1,1280]{1,0:T(1,128)S(1)}, f32[1,1280]{1,0:T(1,128)S(1)}, u32[]{:S(2)}, u32[]{:S(2)}) collective-permute-start(f32[1,1280]{1,0:T(1,128)S(1)} %psum.14.p0), channel_id=1, source_target_pairs={{4,0},{6,2},{0,4},{2,6},{5,1},{7,3},{1,5},{3,7},{12,8},{14,10},{8,... | collective-permute-start | bytes 15368 | tf_op jit(solution)/shard_map/ppermute | solution.py:313
  118.4 6.7 %collective-permute-start.4 = (f32[1,1280]{1,0:T(1,128)S(1)}, f32[1,1280]{1,0:T(1,128)S(1)}, u32[]{:S(2)}, u32[]{:S(2)}) collective-permute-start(f32[1,1280]{1,0:T(1,128)S(1)} %psum.14.p0), channel_id=1, source_target_pairs={{2,0},{4,2},{6,4},{0,6},{3,1},{5,3},{7,5},{1,7},{10,8},{12,10},{14... | collective-permute-start | bytes 15368 | tf_op jit(solution)/shard_map/ppermute | solution.py:313
  120.4 1.2 copy-start.4
  125.1 6.4 %copy-start.10 = (f32[1,1280]{1,0:T(1,128)}, f32[1,1280]{1,0:T(1,128)S(1)}, u32[]{:S(2)}) copy-start(f32[1,1280]{1,0:T(1,128)S(1)} %collective-permute-done.6.p3) | copy-start | bytes 15364
  125.1 6.4 %copy-start.11 = (f32[1,1280]{1,0:T(1,128)}, f32[1,1280]{1,0:T(1,128)S(1)}, u32[]{:S(2)}) copy-start(f32[1,1280]{1,0:T(1,128)S(1)} %collective-permute-done.5.p2) | copy-start | bytes 15364
  125.1 6.4 %copy-start.12 = (f32[1,1280]{1,0:T(1,128)}, f32[1,1280]{1,0:T(1,128)S(1)}, u32[]{:S(2)}) copy-start(f32[1,1280]{1,0:T(1,128)S(1)} %collective-permute-done.4.p1) | copy-start | bytes 15364
  125.1 33.0 %all-to-all-start.3 = ((bf16[64,5,2,1280]{3,2,1,0:T(2,128)(2,1)}), bf16[64,5,2,1280]{3,2,1,0:T(2,128)(2,1)S(1)}, u32[]{:S(2)}, u32[]{:S(2)}) async-start(bf16[64,5,2,1280]{3,2,1,0:T(2,128)(2,1)} %bitcast.22), calls=%async_computation.3 | async-start | bytes 3276800 | tf_op jit(solution)/shard_map/all_to_all | solution.py:414
  141.4 13.8 %copy-start.5 = (f32[4,1408]{1,0:T(4,128)}, f32[4,1408]{1,0:T(4,128)S(1)}, u32[]{:S(2)}) copy-start(f32[4,1408]{1,0:T(4,128)S(1)} %psum.15.m0) | copy-start | bytes 67588
  141.5 13.8 %collective-permute-start.9 = (f32[4,1408]{1,0:T(4,128)S(1)}, f32[4,1408]{1,0:T(4,128)S(1)}, u32[]{:S(2)}, u32[]{:S(2)}) collective-permute-start(f32[4,1408]{1,0:T(4,128)S(1)} %psum.15.m0), channel_id=1, source_target_pairs={{6,0},{0,2},{2,4},{4,6},{7,1},{1,3},{3,5},{5,7},{14,8},{8,10},{10,... | collective-permute-start | bytes 67592 | tf_op jit(solution)/shard_map/ppermute | solution.py:313
  142.8 12.4 %collective-permute-start.8 = (f32[4,1408]{1,0:T(4,128)S(1)}, f32[4,1408]{1,0:T(4,128)S(1)}, u32[]{:S(2)}, u32[]{:S(2)}) collective-permute-start(f32[4,1408]{1,0:T(4,128)S(1)} %psum.15.m0), channel_id=1, source_target_pairs={{4,0},{6,2},{0,4},{2,6},{5,1},{7,3},{1,5},{3,7},{12,8},{14,10},{8,... | collective-permute-start | bytes 67592 | tf_op jit(solution)/shard_map/ppermute | solution.py:313
  145.5 9.8 %collective-permute-start.7 = (f32[4,1408]{1,0:T(4,128)S(1)}, f32[4,1408]{1,0:T(4,128)S(1)}, u32[]{:S(2)}, u32[]{:S(2)}) collective-permute-start(f32[4,1408]{1,0:T(4,128)S(1)} %psum.15.m0), channel_id=1, source_target_pairs={{2,0},{4,2},{6,4},{0,6},{3,1},{5,3},{7,5},{1,7},{10,8},{12,10},{14... | collective-permute-start | bytes 67592 | tf_op jit(solution)/shard_map/ppermute | solution.py:313
  155.2 0.6 copy-start.6
  155.3 0.6 copy-start.7
  155.9 0.6 copy-start.8
  158.2 7.0 %copy-start.2 = (bf16[64,5,2,1280]{3,2,1,0:T(2,128)(2,1)}, bf16[64,5,2,1280]{3,2,1,0:T(2,128)(2,1)S(1)}, u32[]{:S(2)}) copy-start(bf16[64,5,2,1280]{3,2,1,0:T(2,128)(2,1)S(1)} %all-to-all-done.3) | copy-start | bytes 4915204
  158.2 18.0 %all-to-all-start.4 = ((bf16[16,4,2304]{2,1,0:T(4,128)(2,1)}), bf16[16,4,2304]{2,1,0:T(4,128)(2,1)S(1)}, u32[]{:S(2)}, u32[]{:S(2)}) async-start(bf16[16,4,2304]{2,1,0:T(4,128)(2,1)} %get-tuple-element.91), calls=%async_computation.4 | async-start | bytes 589824 | tf_op jit(solution)/shard_map/all_to_all | solution.py:500

commit v5 on v4

--- a/solution.py
+++ b/solution.py
@@ -56,7 +56,7 @@
 LONG = pl.CostEstimate(flops=1 << 34, transcendentals=0, bytes_accessed=1 << 26)
 
 
-def run(body, outs, *args, grid=(), specs=None, out_specs=None, scratch=(), name=None, cost=TINY):
+def run(body, outs, *args, grid=(), specs=None, out_specs=None, scratch=(), name=None, cost=TINY, limit=56):
     return pl.pallas_call(
         body,
         out_shape=outs,
@@ -66,12 +66,16 @@
         scratch_shapes=list(scratch),
         name=name,
         cost_estimate=cost,
-        compiler_params=pltpu.CompilerParams(vmem_limit_bytes=56 << 20),
+        compiler_params=pltpu.CompilerParams(vmem_limit_bytes=limit << 20),
     )(*args)
 
 
 def pack_rows(ref, value):
     ref[...] = value.astype(BF16).reshape(ref.shape)
+
+
+def in_vmem(value):
+    return pltpu.with_memory_space_constraint(value, pltpu.VMEM)
 
 
 def x_body(routes_ref, labels_ref, tokens_ref, table_ref, send_ref):
@@ -128,17 +132,15 @@
 
 
 def forward_body(
-    own_in, other_in, w1_in, w2_in, xs_out, hidden_out, slope_out, own_out, other_out,
-    own_x, other_x, w1, w2, xs, hidden, slope, own, other, in_sems, out_sems,
+    own_x, other_x, w1_in, w2_in, xs_out, hidden_out, slope_out, own_out, other_out,
+    w1, w2, xs, hidden, slope, own, other, in_sems, out_sems,
 ):
-    pairs = ((own_in, own_x), (w1_in, w1), (other_in, other_x), (w2_in, w2))
-    copies = start_all(pairs, in_sems)
+    copies = start_all(((w1_in, w1), (w2_in, w2)), in_sems)
     saved = []
     for n, half in enumerate(HALVES):
-        copies[2 * n].wait()
         xs[half] = (own_x, other_x)[n][:, :, :D].reshape(HALF, D)
         if n == 0:
-            copies[1].wait()
+            copies[0].wait()
         for rows in chunks(half, 160):
             h = dot(xs[rows, :], w1[...], 1, 0)
             square = h * h
@@ -152,7 +154,7 @@
             out_sems.at[n],
         )
         if n == 0:
-            copies[3].wait()
+            copies[1].wait()
         for rows in chunks(half, 160):
             part = dot(hidden[rows, :], w2[...], 1, 0)
             there = slice(rows.start - half.start, rows.stop - half.start)
@@ -166,22 +168,21 @@
 
 
 def backward_body(
-    own_in, other_in, slope_in, w1_in, w2_in, gs_out, d_pre_out, own_out, other_out,
-    own_g, other_g, slope, w1, w2, gs, d_pre, own, other, in_sems, out_sems,
+    own_g, other_g, slope_in, w1_in, w2_in, gs_out, d_pre_out, own_out, other_out,
+    slope, w1, w2, gs, d_pre, own, other, in_sems, out_sems,
 ):
     first, last = HALVES
     pairs = (
-        (own_in, own_g), (w2_in, w2), (slope_in.at[first], slope.at[first]), (w1_in, w1),
-        (other_in, other_g), (slope_in.at[last], slope.at[last]),
+        (w2_in, w2), (slope_in.at[first], slope.at[first]), (w1_in, w1),
+        (slope_in.at[last], slope.at[last]),
     )
     copies = start_all(pairs, in_sems)
     saved = []
     for n, half in enumerate(HALVES):
-        copies[4 * n].wait()
         gs[half] = (own_g, other_g)[n][...].reshape(HALF, D)
         if n == 0:
-            copies[1].wait()
-        copies[(2, 5)[n]].wait()
+            copies[0].wait()
+        copies[(1, 3)[n]].wait()
         for rows in chunks(half, 320):
             d_h = dot(gs[rows, :], w2[...], 1, 1)
             d_pre[rows, :] = (d_h * slope[rows, :].astype(F32)).astype(BF16)
@@ -190,7 +191,7 @@
             out_sems.at[n],
         )
         if n == 0:
-            copies[3].wait()
+            copies[2].wait()
         for rows in chunks(half, 320):
             part = dot(d_pre[rows, :], w1[...], 1, 1)
             there = slice(rows.start - half.start, rows.stop - half.start)
@@ -206,21 +207,22 @@
 SQUARE = (ROWS, D)
 
 
-def expert_kernel(body, ins, kept, received, name):
+def expert_kernel(body, ins, kept, name):
     outs = (*[shape(SQUARE, BF16)] * kept, shape((HALF, D), F32), shape((HALF, D), BF16))
-    scratch = [pltpu.VMEM(received, BF16)] * 2
-    scratch += [pltpu.VMEM((D, D), BF16)] * (len(ins) - 2)
+    scratch = [pltpu.VMEM((D, D), BF16)] * (len(ins) - 2)
     scratch += [pltpu.VMEM(SQUARE, BF16)] * (kept if len(ins) == 4 else 2)
     scratch += [pltpu.VMEM((HALF, D), F32), pltpu.VMEM((HALF, D), BF16)]
     scratch += [
-        pltpu.SemaphoreType.DMA((6,)),
+        pltpu.SemaphoreType.DMA((4,)),
         pltpu.SemaphoreType.DMA((4, 3)),
     ]
     return run(
         body,
         outs,
-        *ins,
-        specs=[ANY] * len(ins),
+        in_vmem(ins[0]),
+        in_vmem(ins[1]),
+        *ins[2:],
+        specs=[VMEM] * 2 + [ANY] * (len(ins) - 2),
         out_specs=tuple([ANY] * len(outs)),
         scratch=scratch,
         name=name,
@@ -247,24 +249,30 @@
     )
 
 
+def mark_body(in_ref, out_ref):
+    out_ref[0] = in_ref[0]
+
+
 def add_body(own_ref, other_ref, send_ref):
-    pack_rows(send_ref, own_ref[...] + other_ref[...].astype(F32))
+    rows = pl.ds(pl.multiple_of(pl.program_id(0) * ADD_ROWS, ADD_ROWS), ADD_ROWS)
+    pack_rows(send_ref, own_ref[...] + other_ref[rows, :].astype(F32))
 
 
 ADD_ROWS = 320
 
 
-def add_cores(own, other, name):
+def add_cores(own, other, name, cost=TINY):
     rows = pl.BlockSpec((ADD_ROWS, D), lambda i: (i, 0))
     return run(
         add_body,
         shape(PACKED, BF16),
         own,
-        other,
+        in_vmem(other),
         grid=(HALF // ADD_ROWS,),
-        specs=[rows, rows],
+        specs=[rows, VMEM],
         out_specs=pl.BlockSpec((ADD_ROWS // 2, 2, D), lambda i: (i, 0, 0)),
         name=name,
+        cost=cost,
     )
 
 
@@ -309,8 +317,9 @@
 
 
 def y_parts(mine):
-    return [mine] + [
-        lax.ppermute(mine, Y, [((i + shift) % 4, i) for i in range(4)]) for shift in (1, 2, 3)
+    return [in_vmem(mine)] + [
+        in_vmem(lax.ppermute(mine, Y, [((i + shift) % 4, i) for i in range(4)]))
+        for shift in (1, 2, 3)
     ]
 
 
@@ -435,11 +444,10 @@
     x_in, g_send = lax.optimization_barrier((x_in, g_send))
     g_in = chip_swap(g_send)
     xs, hidden, slope, own, other = expert_kernel(
-        forward_body, (x_in, core_swap(x_in), w_in, w_out), 3, PACKED_X, "forward"
+        forward_body, (x_in, core_swap(x_in), w_in, w_out), 3, "forward"
     )
     other = core_swap(other)
     digits = x_in.reshape(16, 2 * CAP, 2, WIDE)[:, :2, :, D:].reshape(IMAGES, 128)
-    g_in, digits = lax.optimization_barrier((g_in, digits))
     targets, class_weight = run(
         label_body,
         (shape((4, COLS), F32), shape((1, COLS), F32)),
@@ -448,19 +456,24 @@
         labels,
         specs=[SMEM, VMEM, VMEM],
         name="labels",
-        cost=LONG,
-    )
-    own, class_weight = lax.optimization_barrier((own, class_weight))
+    )
+    g_in, mark = lax.optimization_barrier((g_in, here))
+    mark = run(mark_body, shape((1,), I32), mark, specs=[SMEM], out_specs=SMEM, name="mark", cost=LONG)
+    own, mark = lax.optimization_barrier((own, mark))
     out_in = chip_swap(add_cores(own, other, "add_out"))
     gs, d_pre, own, other = expert_kernel(
-        backward_body, (g_in, core_swap(g_in), slope, w_in, w_out), 2, PACKED, "backward"
+        backward_body, (g_in, core_swap(g_in), slope, w_in, w_out), 2, "backward"
     )
     other = core_swap(other)
+    d_w_out = weight_grad(hidden, gs, "d_w_out")
+    out_in, d_w_out, targets, class_weight = lax.optimization_barrier(
+        (out_in, d_w_out, targets, class_weight)
+    )
     mixed_out, d_combine, token_sum = run(
         mixed_body,
         (shape((TOK, D), BF16), shape((2, TOK), F32), shape((1, D), F32)),
         table,
-        out_in,
+        in_vmem(out_in),
         tokens,
         out_grad,
         combine,
@@ -483,10 +496,10 @@
         specs=[SMEM] + [VMEM] * 7,
         name="head",
     )
-    hidden, part = lax.optimization_barrier((hidden, part))
-    d_w_out = weight_grad(hidden, gs, "d_w_out")
+    xs, part = lax.optimization_barrier((xs, part))
     messages = y_parts(lax.psum(part, "core"))
-    pooled, d_w_out = lax.optimization_barrier((pooled, d_w_out))
+    d_w_in = weight_grad(xs, d_pre, "d_w_in")
+    pooled, d_w_in = lax.optimization_barrier((pooled, d_w_in))
     d_pooled, losses = run(
         pooled_body,
         (shape((4, D), F32), shape((1, 4), F32)),
@@ -496,10 +509,9 @@
         specs=[SMEM] + [VMEM] * 5,
         name="d_pooled",
     )
-    dp_send, rows_in, xs, d_pooled = lax.optimization_barrier((dp_send, rows_in, xs, d_pooled))
+    dp_send, rows_in, d_pooled = lax.optimization_barrier((dp_send, rows_in, d_pooled))
     dp_in = lax.all_to_all(dp_send, "dp", 0, 0, tiled=True).reshape(IMAGES, COLS + 128)
-    d_tokens = run(tokens_body, shape((TOK, D), BF16), table, rows_in, out_grad, name="d_tokens")
-    d_w_in = weight_grad(xs, d_pre, "d_w_in")
+    d_tokens = run(tokens_body, shape((TOK, D), BF16), table, in_vmem(rows_in), out_grad, name="d_tokens")
     d_head = dot(dp_in[:, COLS : COLS + 80], dp_in[:, :COLS], 0, 0).astype(BF16)
     return (mixed_out, d_tokens, d_combine.T, d_w_in, d_w_out, losses.reshape(4), d_pooled, d_head)
 

time: 179 us -> 175 us (0.978)
  local copies, waits for them, and re-layouts: 4.97 us -> 0.69 us
  starting transfers between devices: 47.3 us -> 51.4 us
  waiting for transfers between devices: 42.9 us -> 39.7 us
    all_to_all x4, waiting for transfers between devices: 42.9 us -> 33.1 us  [chip_swap(): return lax.all_to_all(blocks, CHIP, 0, 0, tiled=True).reshape(dims)]
    all_to_all x1, waiting for transfers between devices: 0.01 us -> 6.56 us  [shards(): lax.all_to_all(dp_send, 'dp', 0, 0, tiled=True).reshape(IMAGES, COLS + 128)]
    unnamed x26 -> x0, local copies, waits for them, and re-layouts: 3.57 us -> none
    all_to_all x4, starting transfers between devices: 29.9 us -> 32.7 us  [chip_swap(): return lax.all_to_all(blocks, CHIP, 0, 0, tiled=True).reshape(dims)]
  transfers between devices with their start and end apart: 15 -> 15, of which waited for: 3 -> 3; matrix products, arithmetic and copies ran while one was open for 1% -> 0% of each run, Pallas kernels for 40% -> 41%
where the time goes in v5:
time: 175 us; the launch traced here: 174 us
  Pallas kernels  74.2 us (42%)
  starting transfers between devices  51.4 us (29%)
  waiting for transfers between devices  39.7 us (23%)
  blocking collectives  6.6 us (4%)
    pallas_call x13, Pallas kernels, run(): pl.pallas_call(body, out_shape=outs, grid=grid, in_specs=specs or [VMEM]...  74.2 us
    all_to_all x4, waiting for transfers between devices, chip_swap(): return lax.all_to_all(blocks, CHIP, 0, 0, tiled=True).reshape(dims)  33.1 us
    all_to_all x4, starting transfers between devices, chip_swap(): return lax.all_to_all(blocks, CHIP, 0, 0, tiled=True).reshape(dims)  32.7 us
    ppermute x6, starting transfers between devices, y_parts(): lax.ppermute(mine, Y, [((i + shift) % 4, i) for i in range(4)])  11.2 us
    all_to_all x1, starting transfers between devices, shards(): lax.all_to_all(dp_send, 'dp', 0, 0, tiled=True).reshape(IMAGES, COLS + 128)  6.92 us
    all_to_all x1, waiting for transfers between devices, shards(): lax.all_to_all(dp_send, 'dp', 0, 0, tiled=True).reshape(IMAGES, COLS + 128)  6.56 us
    psum x1, blocking collectives, shards(): messages = y_parts(lax.psum(part, 'core'))  4.01 us
  transfers between devices with their start and end apart: 15, of which 3 were waited for; matrix products, arithmetic and copies ran while one was open for 0% of the time, Pallas kernels for 41%

profile of v5, /device:TPU:0, one launch (start us, length us, event | category | flops | bytes accessed | tf_op | source)
XLA Modules:
  0.0 174.4 jit_solution(14630273292142278495)
XLA Ops:
  0.6 3.1 %dispatch_x.1 = (bf16[2,640,128]{2,1,0:T(8,128)(2,1)}, bf16[320,2,1408]{2,1,0:T(2,128)(2,1)}) custom-call(s32[2,128]{1,0:T(2,128)} %bitcast.27, s32[4,4]{1,0:T(4,128)} %labels_ref.3, bf16[128,1280]{1,0:T(8,128)(2,1)} %tokens_ref.3), custom_call_target="tpu_custom_call" | custom-call | flops 1 | bytes 1 | tf_op jit(solution)/shard_map/dispatch_x/pallas_call | solution.py:60
  3.7 11.5 %all-to-all-start = ((bf16[64,5,2,1408]{3,2,1,0:T(2,128)(2,1)}), bf16[64,5,2,1408]{3,2,1,0:T(2,128)(2,1)S(1)}, u32[]{:S(2)}, u32[]{:S(2)}) async-start(bf16[64,5,2,1408]{3,2,1,0:T(2,128)(2,1)} %bitcast.25), calls=%async_computation | async-start | bytes 3604480 | tf_op jit(solution)/shard_map/all_to_all | solution.py:423
  15.2 3.0 %dispatch_g.1 = bf16[320,2,1280]{2,1,0:T(2,128)(2,1)} custom-call(bf16[2,640,128]{2,1,0:T(8,128)(2,1)} %get-tuple-element.50.table_ref, bf16[128,1280]{1,0:T(8,128)(2,1)} %grad_ref.5, f32[2,128]{1,0:T(2,128)} %bitcast.28), custom_call_target="tpu_custom_call" | custom-call | flops 1 | bytes 1 | tf_op jit(solution)/shard_map/dispatch_g/pallas_call | solution.py:60
  18.2 23.5 %all-to-all-done = bf16[64,5,2,1408]{3,2,1,0:T(2,128)(2,1)S(1)} async-done(((bf16[64,5,2,1408]{3,2,1,0:T(2,128)(2,1)}), bf16[64,5,2,1408]{3,2,1,0:T(2,128)(2,1)S(1)}, u32[]{:S(2)}, u32[]{:S(2)}) %all-to-all-start) | async-done | bytes 1802272 | tf_op jit(solution)/shard_map/all_to_all | solution.py:423
  41.8 0.0 collective-permute-start
  41.8 6.0 %all-to-all-start.2 = ((bf16[64,5,2,1280]{3,2,1,0:T(2,128)(2,1)}), bf16[64,5,2,1280]{3,2,1,0:T(2,128)(2,1)S(1)}, u32[]{:S(2)}, u32[]{:S(2)}) async-start(bf16[64,5,2,1280]{3,2,1,0:T(2,128)(2,1)} %bitcast.24), calls=%async_computation.2 | async-start | bytes 3276800 | tf_op jit(solution)/shard_map/all_to_all | solution.py:423
  47.8 0.0 collective-permute-done.other_x
  47.8 15.4 %forward.1 = (bf16[1280,1280]{1,0:T(8,128)(2,1)}, bf16[1280,1280]{1,0:T(8,128)(2,1)}, bf16[1280,1280]{1,0:T(8,128)(2,1)}, f32[640,1280]{1,0:T(8,128)}, bf16[640,1280]{1,0:T(8,128)(2,1)}) custom-call(bf16[320,2,1408]{2,1,0:T(2,128)(2,1)S(1)} %bitcast.17, bf16[320,2,1408]{2,1,0:T(2,128)(2,1)} %collective-permute-done.other_x, bf16[1280,1280]{1,0:T(8,128)(2,1)} %w1_in.3, ...), custom_call_target="tpu_custom_call" | custom-call | flops 1 | bytes 1 | tf_op jit(solution)/shard_map/forward/pallas_call | solution.py:60
  63.3 0.3 collective-permute-start.1
  63.6 9.5 %all-to-all-done.2 = bf16[64,5,2,1280]{3,2,1,0:T(2,128)(2,1)S(1)} async-done(((bf16[64,5,2,1280]{3,2,1,0:T(2,128)(2,1)}), bf16[64,5,2,1280]{3,2,1,0:T(2,128)(2,1)S(1)}, u32[]{:S(2)}, u32[]{:S(2)}) %all-to-all-start.2) | async-done | bytes 1638432 | tf_op jit(solution)/shard_map/all_to_all | solution.py:423
  73.1 0.0 collective-permute-start.2
  73.1 0.0 collective-permute-done.1.other_ref
  73.1 3.6 %add_out.1 = bf16[320,2,1280]{2,1,0:T(2,128)(2,1)} custom-call(f32[640,1280]{1,0:T(8,128)} %get-tuple-element.53.own_ref, bf16[640,1280]{1,0:T(8,128)(2,1)} %collective-permute-done.1.other_ref), custom_call_target="tpu_custom_call" | custom-call | flops 1 | bytes 1 | tf_op jit(solution)/shard_map/add_out/pallas_call | solution.py:60
  76.7 6.2 %all-to-all-start.1 = ((bf16[64,5,2,1280]{3,2,1,0:T(2,128)(2,1)}), bf16[64,5,2,1280]{3,2,1,0:T(2,128)(2,1)}, u32[]{:S(2)}, u32[]{:S(2)}) async-start(bf16[64,5,2,1280]{3,2,1,0:T(2,128)(2,1)} %bitcast.23), calls=%async_computation.1 | async-start | bytes 3276800 | tf_op jit(solution)/shard_map/all_to_all | solution.py:423
  83.0 0.0 collective-permute-done.2.other_g
  83.0 14.4 %backward.1 = (bf16[1280,1280]{1,0:T(8,128)(2,1)}, bf16[1280,1280]{1,0:T(8,128)(2,1)}, f32[640,1280]{1,0:T(8,128)}, bf16[640,1280]{1,0:T(8,128)(2,1)}) custom-call(bf16[320,2,1280]{2,1,0:T(2,128)(2,1)S(1)} %bitcast.20, bf16[320,2,1280]{2,1,0:T(2,128)(2,1)} %collective-permute-done.2.other_g, bf16[1280,1280]{1,0:T(8,128)(2,1)} %get-tuple-element.58.slope_in, ...), custom_call_target="tpu_custom_call" | custom-call | flops 1 | bytes 1 | tf_op jit(solution)/shard_map/backward/pallas_call | solution.py:60
  97.4 0.3 collective-permute-start.3
  97.7 0.6 slice.12
  98.4 2.1 %labels.1 = (f32[4,2176]{1,0:T(4,128)}, f32[1,2176]{1,0:T(1,128)}) custom-call(s32[1]{0:T(128)} %bitcast.9.first_ref, bf16[64,128]{1,0:T(8,128)(2,1)} %bitcast.26, s32[4,4]{1,0:T(4,128)} %labels_ref.3), custom_call_target="tpu_custom_call" | custom-call | flops 1 | bytes 1 | tf_op jit(solution)/shard_map/labels/pallas_call | solution.py:60
  100.5 8.3 %d_w_out.1 = bf16[1280,1280]{1,0:T(8,128)(2,1)} custom-call(bf16[1280,1280]{1,0:T(8,128)(2,1)} %get-tuple-element.55.left_ref, bf16[1280,1280]{1,0:T(8,128)(2,1)} %get-tuple-element.59.right_ref), custom_call_target="tpu_custom_call" | custom-call | flops 1 | bytes 1 | tf_op jit(solution)/shard_map/d_w_out/pallas_call | solution.py:60
  108.7 0.0 all-to-all-done.1
  108.7 3.2 %mixed.1 = (bf16[128,1280]{1,0:T(8,128)(2,1)}, f32[2,128]{1,0:T(2,128)}, f32[1,1280]{1,0:T(1,128)}) custom-call(bf16[2,640,128]{2,1,0:T(8,128)(2,1)} %get-tuple-element.50.table_ref, bf16[320,2,1280]{2,1,0:T(2,128)(2,1)} %bitcast.5.in_ref, bf16[128,1280]{1,0:T(8,128)(2,1)} %tokens_ref.3, bf16[128,1280]{1,0:T(8,128)(2,1)} %grad_ref.5, f32[2,128]{1,0:T(2,128)} %bitcast.29), custom_call_target="tpu_custom_call" | custom-call | flops 17179869184 | bytes 67108864 | tf_op jit(solution)/shard_map/mixed/pallas_call | solution.py:60
  111.9 2.6 %psum.14.p0 = f32[1,1280]{1,0:T(1,128)S(1)} all-reduce(f32[1,1280]{1,0:T(1,128)} %get-tuple-element.65), channel_id=1, replica_groups=mesh['dp'=16,'yh'=2,'yl'=2,'core'=2] {'core'}, use_global_device_ids=true, to_apply=%region_0.0 | all-reduce | flops 1280 | bytes 10240 | tf_op jit(solution)/shard_map/psum | solution.py:483
  114.5 1.3 collective-permute-start.6
  115.8 2.7 %collective-permute-start.5 = (f32[1,1280]{1,0:T(1,128)S(1)}, f32[1,1280]{1,0:T(1,128)S(1)}, u32[]{:S(2)}, u32[]{:S(2)}) collective-permute-start(f32[1,1280]{1,0:T(1,128)S(1)} %psum.14.p0), channel_id=1, source_target_pairs={{4,0},{6,2},{0,4},{2,6},{5,1},{7,3},{1,5},{3,7},{12,8},{14,10},{8,... | collective-permute-start | bytes 15368 | tf_op jit(solution)/shard_map/ppermute | solution.py:321
  118.5 1.5 collective-permute-start.4
  119.9 0.0 collective-permute-done.3.other_ref
  119.9 3.1 %add_rows.1 = bf16[320,2,1280]{2,1,0:T(2,128)(2,1)} custom-call(f32[640,1280]{1,0:T(8,128)} %get-tuple-element.66.own_ref, bf16[640,1280]{1,0:T(8,128)(2,1)S(1)} %collective-permute-done.3.other_ref), custom_call_target="tpu_custom_call" | custom-call | flops 1 | bytes 1 | tf_op jit(solution)/shard_map/add_rows/pallas_call | solution.py:60
  123.0 0.0 collective-permute-done.6.p3
  123.0 0.0 collective-permute-done.5.p2
  123.0 0.0 collective-permute-done.4.p1
  123.0 9.0 %all-to-all-start.3 = ((bf16[64,5,2,1280]{3,2,1,0:T(2,128)(2,1)}), bf16[64,5,2,1280]{3,2,1,0:T(2,128)(2,1)S(1)}, u32[]{:S(2)}, u32[]{:S(2)}) async-start(bf16[64,5,2,1280]{3,2,1,0:T(2,128)(2,1)} %bitcast.22), calls=%async_computation.3 | async-start | bytes 3276800 | tf_op jit(solution)/shard_map/all_to_all | solution.py:423
  132.0 5.8 %head.1 = (f32[4,1280]{1,0:T(4,128)}, f32[4,1408]{1,0:T(4,128)}, bf16[16,4,2304]{2,1,0:T(4,128)(2,1)}) custom-call(s32[1]{0:T(128)} %bitcast.8.here_ref, f32[1,1280]{1,0:T(1,128)S(1)} %psum.14.p0, f32[1,1280]{1,0:T(1,128)S(1)} %collective-permute-done.4.p1, f32[1,1280]{1,0:T(1,128)S(1)} %collective-permute-done.5.p2, ...), custom_call_target="tpu_custom_call" | custom-call | flops 1 | bytes 1 | tf_op jit(solution)/shard_map/head/pallas_call | solution.py:60
  137.8 4.0 %psum.15.m0 = f32[4,1408]{1,0:T(4,128)S(1)} all-reduce(f32[4,1408]{1,0:T(4,128)} %get-tuple-element.79), channel_id=1, replica_groups=mesh['dp'=16,'yh'=2,'yl'=2,'core'=2] {'core'}, use_global_device_ids=true, to_apply=%region_1.0 | all-reduce | flops 5632 | bytes 45056 | tf_op jit(solution)/shard_map/psum | solution.py:500
  141.9 1.6 collective-permute-start.9
  143.5 2.7 %collective-permute-start.8 = (f32[4,1408]{1,0:T(4,128)S(1)}, f32[4,1408]{1,0:T(4,128)S(1)}, u32[]{:S(2)}, u32[]{:S(2)}) collective-permute-start(f32[4,1408]{1,0:T(4,128)S(1)} %psum.15.m0), channel_id=1, source_target_pairs={{4,0},{6,2},{0,4},{2,6},{5,1},{7,3},{1,5},{3,7},{12,8},{14,10},{8,... | collective-permute-start | bytes 67592 | tf_op jit(solution)/shard_map/ppermute | solution.py:321
  146.2 1.5 collective-permute-start.7
  147.6 8.3 %d_w_in.1 = bf16[1280,1280]{1,0:T(8,128)(2,1)} custom-call(bf16[1280,1280]{1,0:T(8,128)(2,1)} %get-tuple-element.81.left_ref, bf16[1280,1280]{1,0:T(8,128)(2,1)} %get-tuple-element.82.right_ref), custom_call_target="tpu_custom_call" | custom-call | flops 1 | bytes 1 | tf_op jit(solution)/shard_map/d_w_in/pallas_call | solution.py:60
  155.9 0.0 collective-permute-done.9.m3
  155.9 0.0 collective-permute-done.8.m2
  155.9 0.0 collective-permute-done.7.m1
  155.9 1.6 d_pooled.1
  157.5 0.0 all-to-all-done.3
  157.5 6.9 %all-to-all-start.4 = ((bf16[16,4,2304]{2,1,0:T(4,128)(2,1)}), bf16[16,4,2304]{2,1,0:T(4,128)(2,1)S(1)}, u32[]{:S(2)}, u32[]{:S(2)}) async-start(bf16[16,4,2304]{2,1,0:T(4,128)(2,1)} %get-tuple-element.91), calls=%async_computation.4 | async-start | bytes 589824 | tf_op jit(solution)/shard_map/all_to_all | solution.py:513
  164.5 2.3 %d_tokens.1 = bf16[128,1280]{1,0:T(8,128)(2,1)} custom-call(bf16[2,640,128]{2,1,0:T(8,128)(2,1)} %get-tuple-element.50.table_ref, bf16[320,2,1280]{2,1,0:T(2,128)(2,1)S(1)} %bitcast.21, bf16[128,1280]{1,0:T(8,128)(2,1)} %grad_ref.5), custom_call_target="tpu_custom_call" | custom-call | flops 1 | bytes 1 | tf_op jit(solution)/shard_map/d_tokens/pallas_call | solution.py:60
  166.8 6.6 %all-to-all-done.4 = bf16[16,4,2304]{2,1,0:T(4,128)(2,1)S(1)} async-done(((bf16[16,4,2304]{2,1,0:T(4,128)(2,1)}), bf16[16,4,2304]{2,1,0:T(4,128)(2,1)S(1)}, u32[]{:S(2)}, u32[]{:S(2)}) %all-to-all-start.4) | async-done | bytes 294944 | tf_op jit(solution)/shard_map/all_to_all | solution.py:513
  173.3 0.1 reshape.71
  173.4 1.0 convolution_convert_fusion
Async XLA Ops:
  3.7 38.0 %all-to-all-start = ((bf16[64,5,2,1408]{3,2,1,0:T(2,128)(2,1)}), bf16[64,5,2,1408]{3,2,1,0:T(2,128)(2,1)S(1)}, u32[]{:S(2)}, u32[]{:S(2)}) async-start(bf16[64,5,2,1408]{3,2,1,0:T(2,128)(2,1)} %bitcast.25), calls=%async_computation | async-start | bytes 3604480 | tf_op jit(solution)/shard_map/all_to_all | solution.py:423
  41.8 6.0 %collective-permute-start = (bf16[320,2,1408]{2,1,0:T(2,128)(2,1)S(1)}, bf16[320,2,1408]{2,1,0:T(2,128)(2,1)}, u32[]{:S(2)}, u32[]{:S(2)}) collective-permute-start(bf16[320,2,1408]{2,1,0:T(2,128)(2,1)S(1)} %bitcast.16), channel_id=1, source_target_pairs={{0,1},{1,0},{2,3},{3,2},{4,5},{5,4},{6,7},{7,6},{8,9},{9,8},{10,11... | collective-permute-start | bytes 5406728 | tf_op jit(solution)/shard_map/ppermute | solution.py:427
  41.8 31.3 %all-to-all-start.2 = ((bf16[64,5,2,1280]{3,2,1,0:T(2,128)(2,1)}), bf16[64,5,2,1280]{3,2,1,0:T(2,128)(2,1)S(1)}, u32[]{:S(2)}, u32[]{:S(2)}) async-start(bf16[64,5,2,1280]{3,2,1,0:T(2,128)(2,1)} %bitcast.24), calls=%async_computation.2 | async-start | bytes 3276800 | tf_op jit(solution)/shard_map/all_to_all | solution.py:423
  63.3 9.9 %collective-permute-start.1 = (bf16[640,1280]{1,0:T(8,128)(2,1)}, bf16[640,1280]{1,0:T(8,128)(2,1)}, u32[]{:S(2)}, u32[]{:S(2)}) collective-permute-start(bf16[640,1280]{1,0:T(8,128)(2,1)} %get-tuple-element.54), channel_id=1, source_target_pairs={{0,1},{1,0},{2,3},{3,2},{4,5},{5,4},{6,7},{7,6},{8,9},{9,8},{10,11... | collective-permute-start | bytes 4915208 | tf_op jit(solution)/shard_map/ppermute | solution.py:427
  73.1 9.9 %collective-permute-start.2 = (bf16[320,2,1280]{2,1,0:T(2,128)(2,1)S(1)}, bf16[320,2,1280]{2,1,0:T(2,128)(2,1)}, u32[]{:S(2)}, u32[]{:S(2)}) collective-permute-start(bf16[320,2,1280]{2,1,0:T(2,128)(2,1)S(1)} %bitcast.19), channel_id=1, source_target_pairs={{0,1},{1,0},{2,3},{3,2},{4,5},{5,4},{6,7},{7,6},{8,9},{9,8},{10,11... | collective-permute-start | bytes 4915208 | tf_op jit(solution)/shard_map/ppermute | solution.py:427
  76.7 32.0 %all-to-all-start.1 = ((bf16[64,5,2,1280]{3,2,1,0:T(2,128)(2,1)}), bf16[64,5,2,1280]{3,2,1,0:T(2,128)(2,1)}, u32[]{:S(2)}, u32[]{:S(2)}) async-start(bf16[64,5,2,1280]{3,2,1,0:T(2,128)(2,1)} %bitcast.23), calls=%async_computation.1 | async-start | bytes 3276800 | tf_op jit(solution)/shard_map/all_to_all | solution.py:423
  97.4 22.5 %collective-permute-start.3 = (bf16[640,1280]{1,0:T(8,128)(2,1)}, bf16[640,1280]{1,0:T(8,128)(2,1)S(1)}, u32[]{:S(2)}, u32[]{:S(2)}) collective-permute-start(bf16[640,1280]{1,0:T(8,128)(2,1)} %get-tuple-element.67), channel_id=1, source_target_pairs={{0,1},{1,0},{2,3},{3,2},{4,5},{5,4},{6,7},{7,6},{8,9},{9,8},{10,11... | collective-permute-start | bytes 4915208 | tf_op jit(solution)/shard_map/ppermute | solution.py:427
  114.5 8.5 %collective-permute-start.6 = (f32[1,1280]{1,0:T(1,128)S(1)}, f32[1,1280]{1,0:T(1,128)S(1)}, u32[]{:S(2)}, u32[]{:S(2)}) collective-permute-start(f32[1,1280]{1,0:T(1,128)S(1)} %psum.14.p0), channel_id=1, source_target_pairs={{6,0},{0,2},{2,4},{4,6},{7,1},{1,3},{3,5},{5,7},{14,8},{8,10},{10,... | collective-permute-start | bytes 15368 | tf_op jit(solution)/shard_map/ppermute | solution.py:321
  115.8 7.2 %collective-permute-start.5 = (f32[1,1280]{1,0:T(1,128)S(1)}, f32[1,1280]{1,0:T(1,128)S(1)}, u32[]{:S(2)}, u32[]{:S(2)}) collective-permute-start(f32[1,1280]{1,0:T(1,128)S(1)} %psum.14.p0), channel_id=1, source_target_pairs={{4,0},{6,2},{0,4},{2,6},{5,1},{7,3},{1,5},{3,7},{12,8},{14,10},{8,... | collective-permute-start | bytes 15368 | tf_op jit(solution)/shard_map/ppermute | solution.py:321
  118.5 4.6 %collective-permute-start.4 = (f32[1,1280]{1,0:T(1,128)S(1)}, f32[1,1280]{1,0:T(1,128)S(1)}, u32[]{:S(2)}, u32[]{:S(2)}) collective-permute-start(f32[1,1280]{1,0:T(1,128)S(1)} %psum.14.p0), channel_id=1, source_target_pairs={{2,0},{4,2},{6,4},{0,6},{3,1},{5,3},{7,5},{1,7},{10,8},{12,10},{14... | collective-permute-start | bytes 15368 | tf_op jit(solution)/shard_map/ppermute | solution.py:321
  123.0 34.5 %all-to-all-start.3 = ((bf16[64,5,2,1280]{3,2,1,0:T(2,128)(2,1)}), bf16[64,5,2,1280]{3,2,1,0:T(2,128)(2,1)S(1)}, u32[]{:S(2)}, u32[]{:S(2)}) async-start(bf16[64,5,2,1280]{3,2,1,0:T(2,128)(2,1)} %bitcast.22), calls=%async_computation.3 | async-start | bytes 3276800 | tf_op jit(solution)/shard_map/all_to_all | solution.py:423
  141.9 14.0 %collective-permute-start.9 = (f32[4,1408]{1,0:T(4,128)S(1)}, f32[4,1408]{1,0:T(4,128)S(1)}, u32[]{:S(2)}, u32[]{:S(2)}) collective-permute-start(f32[4,1408]{1,0:T(4,128)S(1)} %psum.15.m0), channel_id=1, source_target_pairs={{6,0},{0,2},{2,4},{4,6},{7,1},{1,3},{3,5},{5,7},{14,8},{8,10},{10,... | collective-permute-start | bytes 67592 | tf_op jit(solution)/shard_map/ppermute | solution.py:321
  143.5 12.4 %collective-permute-start.8 = (f32[4,1408]{1,0:T(4,128)S(1)}, f32[4,1408]{1,0:T(4,128)S(1)}, u32[]{:S(2)}, u32[]{:S(2)}) collective-permute-start(f32[4,1408]{1,0:T(4,128)S(1)} %psum.15.m0), channel_id=1, source_target_pairs={{4,0},{6,2},{0,4},{2,6},{5,1},{7,3},{1,5},{3,7},{12,8},{14,10},{8,... | collective-permute-start | bytes 67592 | tf_op jit(solution)/shard_map/ppermute | solution.py:321
  146.2 9.7 %collective-permute-start.7 = (f32[4,1408]{1,0:T(4,128)S(1)}, f32[4,1408]{1,0:T(4,128)S(1)}, u32[]{:S(2)}, u32[]{:S(2)}) collective-permute-start(f32[4,1408]{1,0:T(4,128)S(1)} %psum.15.m0), channel_id=1, source_target_pairs={{2,0},{4,2},{6,4},{0,6},{3,1},{5,3},{7,5},{1,7},{10,8},{12,10},{14... | collective-permute-start | bytes 67592 | tf_op jit(solution)/shard_map/ppermute | solution.py:321
  157.5 15.8 %all-to-all-start.4 = ((bf16[16,4,2304]{2,1,0:T(4,128)(2,1)}), bf16[16,4,2304]{2,1,0:T(4,128)(2,1)S(1)}, u32[]{:S(2)}, u32[]{:S(2)}) async-start(bf16[16,4,2304]{2,1,0:T(4,128)(2,1)} %get-tuple-element.91), calls=%async_computation.4 | async-start | bytes 589824 | tf_op jit(solution)/shard_map/all_to_all | solution.py:513

commit v6 on v5

--- a/solution.py
+++ b/solution.py
@@ -141,14 +141,22 @@
         xs[half] = (own_x, other_x)[n][:, :, :D].reshape(HALF, D)
         if n == 0:
             copies[0].wait()
-        for rows in chunks(half, 160):
-            h = dot(xs[rows, :], w1[...], 1, 0)
-            square = h * h
-            bend = jnp.tanh(h * (ROOT_2_PI + (ROOT_2_PI * CUBIC) * square))
-            act = 0.5 + 0.5 * bend
-            hidden[rows, :] = (h * act).astype(BF16)
-            tilt = (1.0 - bend * bend) * (0.5 * ROOT_2_PI + (1.5 * ROOT_2_PI * CUBIC) * square)
-            slope[rows, :] = (act + h * tilt).astype(BF16)
+
+        def activate(i, carry):
+            for low in (0, 160):
+                rows = pl.ds(pl.multiple_of(half.start + low + i * 320, 160), 160)
+                h = dot(xs[rows, :], w1[...], 1, 0)
+                square = h * h
+                bend = jnp.tanh(h * (ROOT_2_PI + (ROOT_2_PI * CUBIC) * square))
+                act = 0.5 + 0.5 * bend
+                hidden[rows, :] = (h * act).astype(BF16)
+                tilt = (1.0 - bend * bend) * (
+                    0.5 * ROOT_2_PI + (1.5 * ROOT_2_PI * CUBIC) * square
+                )
+                slope[rows, :] = (act + h * tilt).astype(BF16)
+            return carry
+
+        lax.fori_loop(0, 2, activate, 0)
         saved += start_all(
             [(v.at[half], o.at[half]) for v, o in ((xs, xs_out), (hidden, hidden_out), (slope, slope_out))],
             out_sems.at[n],
@@ -232,21 +240,27 @@
 GRAD_COLS = 640
 
 
-def weight_grad_body(left_ref, right_ref, out_ref):
-    out_ref[...] = dot(left_ref[...], right_ref[...], 0, 0).astype(BF16)
-
-
-def weight_grad(left, right, name):
-    return run(
+def weight_grad_body(left_ref, right_ref, *refs):
+    refs[-1][...] = dot(left_ref[...], right_ref[...], 0, 0).astype(BF16)
+
+
+def weight_grad(left, right, name, blocks=(0, 1), into=()):
+    first = blocks[0]
+    return pl.pallas_call(
         weight_grad_body,
-        shape((D, D), BF16),
-        left,
-        right,
-        grid=(D // GRAD_COLS,),
-        specs=[pl.BlockSpec((ROWS, GRAD_COLS), lambda i: (0, i)), pl.BlockSpec((ROWS, D), lambda i: (0, 0))],
-        out_specs=pl.BlockSpec((GRAD_COLS, D), lambda i: (i, 0)),
+        out_shape=shape((D, D), BF16),
+        grid=(len(blocks),),
+        in_specs=[
+            pl.BlockSpec((ROWS, GRAD_COLS), lambda i: (0, first + i)),
+            pl.BlockSpec((ROWS, D), lambda i: (0, 0)),
+            *[ANY for _ in into],
+        ],
+        out_specs=pl.BlockSpec((GRAD_COLS, D), lambda i: (first + i, 0)),
+        input_output_aliases={2: 0} if into else {},
         name=name,
-    )
+        cost_estimate=TINY,
+        compiler_params=pltpu.CompilerParams(vmem_limit_bytes=56 << 20),
+    )(left, right, *into)
 
 
 def mark_body(in_ref, out_ref):
@@ -328,33 +342,46 @@
     return away, lax.rsqrt(jnp.mean(away * away, axis=1, keepdims=True) + EPS)
 
 
-def head_body(here_ref, p0, p1, p2, p3, target_ref, weight_ref, w_ref, pooled_ref, part_ref, send_ref):
+CLASS_CUTS = (0, 640, 1152, 1664, COLS)
+
+
+def head_body(
+    here_ref, p0, p1, p2, p3, target_ref, weight_ref, w_in, pooled_ref, part_ref, send_ref, w_ref, sems
+):
+    spans = [slice(low, high) for low, high in zip(CLASS_CUTS, CLASS_CUTS[1:])]
+    copies = start_all([(w_in.at[:, span], w_ref.at[:, span]) for span in spans], sems)
     here = here_ref[0]
     parts = [p[...] for p in (p0, p1, p2, p3)]
     for j in range(4):
         pooled_ref[j : j + 1, :] = in_order(here, parts, j) * (1.0 / PATCHES)
     away, scale = centered(pooled_ref[...])
     normed = (away * scale).astype(BF16)
-    logits = dot(normed, w_ref[...], 1, 0)
-    hit = target_ref[...] > 0.5
-    signed = jnp.where(hit, -logits, logits)
-    small = jnp.exp(-jnp.abs(signed))
-    nll = jnp.maximum(signed, 0.0) + jnp.log1p(small)
-    inverse = 1.0 / (1.0 + small)
-    miss = jnp.where(signed >= 0.0, 1.0, small) * inverse
-    keep = jnp.where(signed >= 0.0, small, 1.0) * inverse
-    weight = weight_ref[...]
-    loss = jnp.sum(weight * (miss * miss) * nll, axis=1, keepdims=True)
-    slope = weight * (2.0 * miss * keep * nll + miss * miss) * miss
-    d_logits = jnp.where(hit, -slope, slope).astype(BF16)
-    part_ref[:, :D] = dot(d_logits, w_ref[...], 1, 1)
-    part_ref[:, D:] = jnp.broadcast_to(loss, (4, 128))
     zeros = jnp.zeros((4, 48), BF16)
     for d in range(16):
-        send_ref[d, :, :COLS] = d_logits
         send_ref[d, :, COLS : COLS + 128] = jnp.concatenate(
             [normed[:, 80 * d : 80 * d + 80], zeros], axis=1
         )
+    loss = jnp.zeros((4, 1), F32)
+    d_normed = jnp.zeros((4, D), F32)
+    for span, copy in zip(spans, copies):
+        copy.wait()
+        logits = dot(normed, w_ref[:, span], 1, 0)
+        hit = target_ref[:, span] > 0.5
+        signed = jnp.where(hit, -logits, logits)
+        small = jnp.exp(-jnp.abs(signed))
+        nll = jnp.maximum(signed, 0.0) + jnp.log1p(small)
+        inverse = 1.0 / (1.0 + small)
+        miss = jnp.where(signed >= 0.0, 1.0, small) * inverse
+        keep = jnp.where(signed >= 0.0, small, 1.0) * inverse
+        weight = weight_ref[:, span]
+        loss = loss + jnp.sum(weight * (miss * miss) * nll, axis=1, keepdims=True)
+        slope = weight * (2.0 * miss * keep * nll + miss * miss) * miss
+        d_logits = jnp.where(hit, -slope, slope).astype(BF16)
+        d_normed = d_normed + dot(d_logits, w_ref[:, span], 1, 1)
+        for d in range(16):
+            send_ref[d, :, span] = d_logits
+    part_ref[:, :D] = d_normed
+    part_ref[:, D:] = jnp.broadcast_to(loss, (4, 128))
 
 
 def pooled_body(here_ref, m0, m1, m2, m3, pooled_ref, d_ref, loss_ref):
@@ -457,7 +484,9 @@
         specs=[SMEM, VMEM, VMEM],
         name="labels",
     )
-    g_in, mark = lax.optimization_barrier((g_in, here))
+    g_in, targets, class_weight, mark = lax.optimization_barrier(
+        (g_in, targets, class_weight, here)
+    )
     mark = run(mark_body, shape((1,), I32), mark, specs=[SMEM], out_specs=SMEM, name="mark", cost=LONG)
     own, mark = lax.optimization_barrier((own, mark))
     out_in = chip_swap(add_cores(own, other, "add_out"))
@@ -466,9 +495,7 @@
     )
     other = core_swap(other)
     d_w_out = weight_grad(hidden, gs, "d_w_out")
-    out_in, d_w_out, targets, class_weight = lax.optimization_barrier(
-        (out_in, d_w_out, targets, class_weight)
-    )
+    out_in, d_w_out = lax.optimization_barrier((out_in, d_w_out))
     mixed_out, d_combine, token_sum = run(
         mixed_body,
         (shape((TOK, D), BF16), shape((2, TOK), F32), shape((1, D), F32)),
@@ -493,12 +520,13 @@
         targets,
         class_weight,
         head_w,
-        specs=[SMEM] + [VMEM] * 7,
+        specs=[SMEM] + [VMEM] * 6 + [ANY],
+        scratch=[pltpu.VMEM((D, COLS), BF16), pltpu.SemaphoreType.DMA((4,))],
         name="head",
     )
     xs, part = lax.optimization_barrier((xs, part))
     messages = y_parts(lax.psum(part, "core"))
-    d_w_in = weight_grad(xs, d_pre, "d_w_in")
+    d_w_in = weight_grad(xs, d_pre, "d_w_in_low", blocks=(0,))
     pooled, d_w_in = lax.optimization_barrier((pooled, d_w_in))
     d_pooled, losses = run(
         pooled_body,
@@ -509,9 +537,12 @@
         specs=[SMEM] + [VMEM] * 5,
         name="d_pooled",
     )
-    dp_send, rows_in, d_pooled = lax.optimization_barrier((dp_send, rows_in, d_pooled))
+    dp_send, rows_in, d_pooled, d_w_in = lax.optimization_barrier(
+        (dp_send, rows_in, d_pooled, d_w_in)
+    )
     dp_in = lax.all_to_all(dp_send, "dp", 0, 0, tiled=True).reshape(IMAGES, COLS + 128)
     d_tokens = run(tokens_body, shape((TOK, D), BF16), table, in_vmem(rows_in), out_grad, name="d_tokens")
+    d_w_in = weight_grad(xs, d_pre, "d_w_in_high", blocks=(1,), into=(d_w_in,))
     d_head = dot(dp_in[:, COLS : COLS + 80], dp_in[:, :COLS], 0, 0).astype(BF16)
     return (mixed_out, d_tokens, d_combine.T, d_w_in, d_w_out, losses.reshape(4), d_pooled, d_head)
 

time: 175 us -> 169 us (0.966)
  waiting for transfers between devices: 39.7 us -> 34.4 us
  starting transfers between devices: 51.4 us -> 47.2 us
  Pallas kernels: 74.2 us -> 77.6 us
    pallas_call x0 -> x3, Pallas kernels: none -> 20.1 us  [weight_grad(): pl.pallas_call(weight_grad_body, out_shape=shape((D, D), BF16), grid=(len...]
    pallas_call x13 -> x11, Pallas kernels: 74.2 us -> 57.5 us  [run(): pl.pallas_call(body, out_shape=outs, grid=grid, in_specs=specs or [VMEM]...]
    all_to_all x1, waiting for transfers between devices: 6.56 us -> 0.64 us  [shards(): lax.all_to_all(dp_send, 'dp', 0, 0, tiled=True).reshape(IMAGES, COLS + 128)]
    all_to_all x4, starting transfers between devices: 32.7 us -> 29.9 us  [chip_swap(): return lax.all_to_all(blocks, CHIP, 0, 0, tiled=True).reshape(dims)]
  transfers between devices with their start and end apart: 15 -> 15, of which waited for: 3 -> 5; matrix products, arithmetic and copies ran while one was open for 0% -> 0% of each run, Pallas kernels for 41% -> 44%
where the time goes in v6:
time: 169 us; the launch traced here: 168 us
  Pallas kernels  77.6 us (46%)
  starting transfers between devices  47.2 us (28%)
  waiting for transfers between devices  34.4 us (20%)
  blocking collectives  6.61 us (4%)
    pallas_call x11, Pallas kernels, run(): pl.pallas_call(body, out_shape=outs, grid=grid, in_specs=specs or [VMEM]...  57.5 us
    all_to_all x4, waiting for transfers between devices, chip_swap(): return lax.all_to_all(blocks, CHIP, 0, 0, tiled=True).reshape(dims)  33.8 us
    all_to_all x4, starting transfers between devices, chip_swap(): return lax.all_to_all(blocks, CHIP, 0, 0, tiled=True).reshape(dims)  29.9 us
    pallas_call x3, Pallas kernels, weight_grad(): pl.pallas_call(weight_grad_body, out_shape=shape((D, D), BF16), grid=(len...  20.1 us
    ppermute x6, starting transfers between devices, y_parts(): lax.ppermute(mine, Y, [((i + shift) % 4, i) for i in range(4)])  10 us
    all_to_all x1, starting transfers between devices, shards(): lax.all_to_all(dp_send, 'dp', 0, 0, tiled=True).reshape(IMAGES, COLS + 128)  6.44 us
    psum x1, blocking collectives, shards(): messages = y_parts(lax.psum(part, 'core'))  4.02 us
  transfers between devices with their start and end apart: 15, of which 5 were waited for; matrix products, arithmetic and copies ran while one was open for 0% of the time, Pallas kernels for 44%

profile of v6, /device:TPU:0, one launch (start us, length us, event | category | flops | bytes accessed | tf_op | source)
XLA Modules:
  0.0 168.2 jit_solution(5887565027202700327)
XLA Ops:
  0.6 3.1 %dispatch_x.1 = (bf16[2,640,128]{2,1,0:T(8,128)(2,1)}, bf16[320,2,1408]{2,1,0:T(2,128)(2,1)}) custom-call(s32[2,128]{1,0:T(2,128)} %bitcast.27, s32[4,4]{1,0:T(4,128)} %labels_ref.3, bf16[128,1280]{1,0:T(8,128)(2,1)} %tokens_ref.3), custom_call_target="tpu_custom_call" | custom-call | flops 1 | bytes 1 | tf_op jit(solution)/shard_map/dispatch_x/pallas_call | solution.py:60
  3.7 11.5 %all-to-all-start = ((bf16[64,5,2,1408]{3,2,1,0:T(2,128)(2,1)}), bf16[64,5,2,1408]{3,2,1,0:T(2,128)(2,1)S(1)}, u32[]{:S(2)}, u32[]{:S(2)}) async-start(bf16[64,5,2,1408]{3,2,1,0:T(2,128)(2,1)} %bitcast.25), calls=%async_computation | async-start | bytes 3604480 | tf_op jit(solution)/shard_map/all_to_all | solution.py:450
  15.2 3.1 %dispatch_g.1 = bf16[320,2,1280]{2,1,0:T(2,128)(2,1)} custom-call(bf16[2,640,128]{2,1,0:T(8,128)(2,1)} %get-tuple-element.51.table_ref, bf16[128,1280]{1,0:T(8,128)(2,1)} %grad_ref.5, f32[2,128]{1,0:T(2,128)} %bitcast.28), custom_call_target="tpu_custom_call" | custom-call | flops 1 | bytes 1 | tf_op jit(solution)/shard_map/dispatch_g/pallas_call | solution.py:60
  18.3 23.5 %all-to-all-done = bf16[64,5,2,1408]{3,2,1,0:T(2,128)(2,1)S(1)} async-done(((bf16[64,5,2,1408]{3,2,1,0:T(2,128)(2,1)}), bf16[64,5,2,1408]{3,2,1,0:T(2,128)(2,1)S(1)}, u32[]{:S(2)}, u32[]{:S(2)}) %all-to-all-start) | async-done | bytes 1802272 | tf_op jit(solution)/shard_map/all_to_all | solution.py:450
  41.8 0.0 collective-permute-start
  41.8 5.8 %all-to-all-start.2 = ((bf16[64,5,2,1280]{3,2,1,0:T(2,128)(2,1)}), bf16[64,5,2,1280]{3,2,1,0:T(2,128)(2,1)S(1)}, u32[]{:S(2)}, u32[]{:S(2)}) async-start(bf16[64,5,2,1280]{3,2,1,0:T(2,128)(2,1)} %bitcast.22), calls=%async_computation.2 | async-start | bytes 3276800 | tf_op jit(solution)/shard_map/all_to_all | solution.py:450
  47.6 0.0 collective-permute-done.other_x
  47.6 16.3 %forward.1 = (bf16[1280,1280]{1,0:T(8,128)(2,1)}, bf16[1280,1280]{1,0:T(8,128)(2,1)}, bf16[1280,1280]{1,0:T(8,128)(2,1)}, f32[640,1280]{1,0:T(8,128)}, bf16[640,1280]{1,0:T(8,128)(2,1)}) custom-call(bf16[320,2,1408]{2,1,0:T(2,128)(2,1)S(1)} %bitcast.17, bf16[320,2,1408]{2,1,0:T(2,128)(2,1)} %collective-permute-done.other_x, bf16[1280,1280]{1,0:T(8,128)(2,1)} %w1_in.3, ...), custom_call_target="tpu_custom_call" | custom-call | flops 1 | bytes 1 | tf_op jit(solution)/shard_map/forward/pallas_call | solution.py:60
  63.9 0.5 collective-permute-start.1
  64.4 0.6 slice.12
  65.0 2.1 %labels.1 = (f32[4,2176]{1,0:T(4,128)}, f32[1,2176]{1,0:T(1,128)}) custom-call(s32[1]{0:T(128)} %bitcast.8.first_ref, bf16[64,128]{1,0:T(8,128)(2,1)} %bitcast.26, s32[4,4]{1,0:T(4,128)} %labels_ref.3), custom_call_target="tpu_custom_call" | custom-call | flops 1 | bytes 1 | tf_op jit(solution)/shard_map/labels/pallas_call | solution.py:60
  67.1 6.0 %all-to-all-done.2 = bf16[64,5,2,1280]{3,2,1,0:T(2,128)(2,1)S(1)} async-done(((bf16[64,5,2,1280]{3,2,1,0:T(2,128)(2,1)}), bf16[64,5,2,1280]{3,2,1,0:T(2,128)(2,1)S(1)}, u32[]{:S(2)}, u32[]{:S(2)}) %all-to-all-start.2) | async-done | bytes 1638432 | tf_op jit(solution)/shard_map/all_to_all | solution.py:450
  73.1 0.0 collective-permute-start.2
  73.1 0.0 collective-permute-done.1.other_ref
  73.1 3.6 %add_out.1 = bf16[320,2,1280]{2,1,0:T(2,128)(2,1)} custom-call(f32[640,1280]{1,0:T(8,128)} %get-tuple-element.54.own_ref, bf16[640,1280]{1,0:T(8,128)(2,1)} %collective-permute-done.1.other_ref), custom_call_target="tpu_custom_call" | custom-call | flops 1 | bytes 1 | tf_op jit(solution)/shard_map/add_out/pallas_call | solution.py:60
  76.7 6.0 %all-to-all-start.1 = ((bf16[64,5,2,1280]{3,2,1,0:T(2,128)(2,1)}), bf16[64,5,2,1280]{3,2,1,0:T(2,128)(2,1)}, u32[]{:S(2)}, u32[]{:S(2)}) async-start(bf16[64,5,2,1280]{3,2,1,0:T(2,128)(2,1)} %bitcast.24), calls=%async_computation.1 | async-start | bytes 3276800 | tf_op jit(solution)/shard_map/all_to_all | solution.py:450
  82.8 0.0 collective-permute-done.2.other_g
  82.8 13.0 %backward.1 = (bf16[1280,1280]{1,0:T(8,128)(2,1)}, bf16[1280,1280]{1,0:T(8,128)(2,1)}, f32[640,1280]{1,0:T(8,128)}, bf16[640,1280]{1,0:T(8,128)(2,1)}) custom-call(bf16[320,2,1280]{2,1,0:T(2,128)(2,1)S(1)} %bitcast.20, bf16[320,2,1280]{2,1,0:T(2,128)(2,1)S(1)} %collective-permute-done.2.other_g, bf16[1280,1280]{1,0:T(8,128)(2,1)} %get-tuple-element.61.slope_in, ...), custom_call_target="tpu_custom_call" | custom-call | flops 1 | bytes 1 | tf_op jit(solution)/shard_map/backward/pallas_call | solution.py:60
  95.8 0.3 collective-permute-start.3
  96.1 8.3 %d_w_out.1 = bf16[1280,1280]{1,0:T(8,128)(2,1)} custom-call(bf16[1280,1280]{1,0:T(8,128)(2,1)} %get-tuple-element.56.left_ref, bf16[1280,1280]{1,0:T(8,128)(2,1)} %get-tuple-element.62.right_ref), custom_call_target="tpu_custom_call" | custom-call | flops 1 | bytes 1 | tf_op jit(solution)/shard_map/d_w_out/pallas_call | solution.py:249
  104.4 3.8 %all-to-all-done.1 = bf16[64,5,2,1280]{3,2,1,0:T(2,128)(2,1)} async-done(((bf16[64,5,2,1280]{3,2,1,0:T(2,128)(2,1)}), bf16[64,5,2,1280]{3,2,1,0:T(2,128)(2,1)}, u32[]{:S(2)}, u32[]{:S(2)}) %all-to-all-start.1) | async-done | bytes 1638432 | tf_op jit(solution)/shard_map/all_to_all | solution.py:450
  108.2 3.2 %mixed.1 = (bf16[128,1280]{1,0:T(8,128)(2,1)}, f32[2,128]{1,0:T(2,128)}, f32[1,1280]{1,0:T(1,128)}) custom-call(bf16[2,640,128]{2,1,0:T(8,128)(2,1)} %get-tuple-element.51.table_ref, bf16[320,2,1280]{2,1,0:T(2,128)(2,1)} %bitcast.5.in_ref, bf16[128,1280]{1,0:T(8,128)(2,1)} %tokens_ref.3, bf16[128,1280]{1,0:T(8,128)(2,1)} %grad_ref.5, f32[2,128]{1,0:T(2,128)} %bitcast.29), custom_call_target="tpu_custom_call" | custom-call | flops 17179869184 | bytes 67108864 | tf_op jit(solution)/shard_map/mixed/pallas_call | solution.py:60
  111.4 2.6 %psum.14.p0 = f32[1,1280]{1,0:T(1,128)S(1)} all-reduce(f32[1,1280]{1,0:T(1,128)} %get-tuple-element.66), channel_id=1, replica_groups=mesh['dp'=16,'yh'=2,'yl'=2,'core'=2] {'core'}, use_global_device_ids=true, to_apply=%region_0.0 | all-reduce | flops 1280 | bytes 10240 | tf_op jit(solution)/shard_map/psum | solution.py:510
  114.0 0.8 collective-permute-start.6
  114.8 1.4 collective-permute-start.5
  116.2 2.0 %collective-permute-start.4 = (f32[1,1280]{1,0:T(1,128)S(1)}, f32[1,1280]{1,0:T(1,128)S(1)}, u32[]{:S(2)}, u32[]{:S(2)}) collective-permute-start(f32[1,1280]{1,0:T(1,128)S(1)} %psum.14.p0), channel_id=1, source_target_pairs={{2,0},{4,2},{6,4},{0,6},{3,1},{5,3},{7,5},{1,7},{10,8},{12,10},{14... | collective-permute-start | bytes 15368 | tf_op jit(solution)/shard_map/ppermute | solution.py:335
  118.2 0.0 collective-permute-done.3.other_ref
  118.2 3.1 %add_rows.1 = bf16[320,2,1280]{2,1,0:T(2,128)(2,1)} custom-call(f32[640,1280]{1,0:T(8,128)} %get-tuple-element.67.own_ref, bf16[640,1280]{1,0:T(8,128)(2,1)S(1)} %collective-permute-done.3.other_ref), custom_call_target="tpu_custom_call" | custom-call | flops 1 | bytes 1 | tf_op jit(solution)/shard_map/add_rows/pallas_call | solution.py:60
  121.3 0.0 collective-permute-done.6.p3
  121.3 0.0 collective-permute-done.5.p2
  121.3 0.0 collective-permute-done.4.p1
  121.3 6.6 %all-to-all-start.3 = ((bf16[64,5,2,1280]{3,2,1,0:T(2,128)(2,1)}), bf16[64,5,2,1280]{3,2,1,0:T(2,128)(2,1)S(1)}, u32[]{:S(2)}, u32[]{:S(2)}) async-start(bf16[64,5,2,1280]{3,2,1,0:T(2,128)(2,1)} %bitcast.23), calls=%async_computation.3 | async-start | bytes 3276800 | tf_op jit(solution)/shard_map/all_to_all | solution.py:450
  127.9 6.1 %head.1 = (f32[4,1280]{1,0:T(4,128)}, f32[4,1408]{1,0:T(4,128)}, bf16[16,4,2304]{2,1,0:T(4,128)(2,1)}) custom-call(s32[1]{0:T(128)} %bitcast.11.here_ref, f32[1,1280]{1,0:T(1,128)S(1)} %psum.14.p0, f32[1,1280]{1,0:T(1,128)S(1)} %collective-permute-done.4.p1, f32[1,1280]{1,0:T(1,128)S(1)} %collective-permute-done.5.p2, ...), custom_call_target="tpu_custom_call" | custom-call | flops 1 | bytes 1 | tf_op jit(solution)/shard_map/head/pallas_call | solution.py:60
  134.0 4.0 %psum.15.m0 = f32[4,1408]{1,0:T(4,128)S(1)} all-reduce(f32[4,1408]{1,0:T(4,128)} %get-tuple-element.80), channel_id=1, replica_groups=mesh['dp'=16,'yh'=2,'yl'=2,'core'=2] {'core'}, use_global_device_ids=true, to_apply=%region_1.0 | all-reduce | flops 5632 | bytes 45056 | tf_op jit(solution)/shard_map/psum | solution.py:528
  138.0 1.6 collective-permute-start.9
  139.6 2.7 %collective-permute-start.8 = (f32[4,1408]{1,0:T(4,128)S(1)}, f32[4,1408]{1,0:T(4,128)S(1)}, u32[]{:S(2)}, u32[]{:S(2)}) collective-permute-start(f32[4,1408]{1,0:T(4,128)S(1)} %psum.15.m0), channel_id=1, source_target_pairs={{4,0},{6,2},{0,4},{2,6},{5,1},{7,3},{1,5},{3,7},{12,8},{14,10},{8,... | collective-permute-start | bytes 67592 | tf_op jit(solution)/shard_map/ppermute | solution.py:335
  142.3 1.5 collective-permute-start.7
  143.8 5.9 %d_w_in_low.1.refs_0_ = bf16[1280,1280]{1,0:T(8,128)(2,1)} custom-call(bf16[1280,1280]{1,0:T(8,128)(2,1)} %get-tuple-element.82.left_ref, bf16[1280,1280]{1,0:T(8,128)(2,1)} %get-tuple-element.83.right_ref), custom_call_target="tpu_custom_call" | custom-call | flops 1 | bytes 1 | tf_op jit(solution)/shard_map/d_w_in_low/pallas_call | solution.py:249
  149.7 0.0 collective-permute-done.9.m3
  149.7 0.0 collective-permute-done.8.m2
  149.7 1.6 d_pooled.1
  151.3 0.5 all-to-all-done.3
  151.8 6.4 %all-to-all-start.4 = ((bf16[16,4,2304]{2,1,0:T(4,128)(2,1)}), bf16[16,4,2304]{2,1,0:T(4,128)(2,1)S(1)}, u32[]{:S(2)}, u32[]{:S(2)}) async-start(bf16[16,4,2304]{2,1,0:T(4,128)(2,1)} %get-tuple-element.93), calls=%async_computation.4 | async-start | bytes 589824 | tf_op jit(solution)/shard_map/all_to_all | solution.py:543
  158.2 5.9 %d_w_in_high.1 = bf16[1280,1280]{1,0:T(8,128)(2,1)} custom-call(bf16[1280,1280]{1,0:T(8,128)(2,1)} %get-tuple-element.82.left_ref, bf16[1280,1280]{1,0:T(8,128)(2,1)} %get-tuple-element.83.right_ref, bf16[1280,1280]{1,0:T(8,128)(2,1)} %d_w_in_low.1.refs_0_), custom_call_target="tpu_custom_call", output_to_operand_aliasing={{}: (2, {})} | custom-call | flops 1 | bytes 1 | tf_op jit(solution)/shard_map/d_w_in_high/pallas_call | solution.py:249
  164.2 2.3 %d_tokens.1 = bf16[128,1280]{1,0:T(8,128)(2,1)} custom-call(bf16[2,640,128]{2,1,0:T(8,128)(2,1)} %get-tuple-element.51.table_ref, bf16[320,2,1280]{2,1,0:T(2,128)(2,1)S(1)} %bitcast.21, bf16[128,1280]{1,0:T(8,128)(2,1)} %grad_ref.5), custom_call_target="tpu_custom_call" | custom-call | flops 1 | bytes 1 | tf_op jit(solution)/shard_map/d_tokens/pallas_call | solution.py:60
  166.5 0.6 all-to-all-done.4
  167.1 0.1 reshape.71
  167.2 1.0 convolution_convert_fusion
  (1 shorter events, 0.0 us)
Async XLA Ops:
  3.7 38.0 %all-to-all-start = ((bf16[64,5,2,1408]{3,2,1,0:T(2,128)(2,1)}), bf16[64,5,2,1408]{3,2,1,0:T(2,128)(2,1)S(1)}, u32[]{:S(2)}, u32[]{:S(2)}) async-start(bf16[64,5,2,1408]{3,2,1,0:T(2,128)(2,1)} %bitcast.25), calls=%async_computation | async-start | bytes 3604480 | tf_op jit(solution)/shard_map/all_to_all | solution.py:450
  41.8 5.8 %collective-permute-start = (bf16[320,2,1408]{2,1,0:T(2,128)(2,1)S(1)}, bf16[320,2,1408]{2,1,0:T(2,128)(2,1)}, u32[]{:S(2)}, u32[]{:S(2)}) collective-permute-start(bf16[320,2,1408]{2,1,0:T(2,128)(2,1)S(1)} %bitcast.16), channel_id=1, source_target_pairs={{0,1},{1,0},{2,3},{3,2},{4,5},{5,4},{6,7},{7,6},{8,9},{9,8},{10,11... | collective-permute-start | bytes 5406728 | tf_op jit(solution)/shard_map/ppermute | solution.py:454
  41.8 31.3 %all-to-all-start.2 = ((bf16[64,5,2,1280]{3,2,1,0:T(2,128)(2,1)}), bf16[64,5,2,1280]{3,2,1,0:T(2,128)(2,1)S(1)}, u32[]{:S(2)}, u32[]{:S(2)}) async-start(bf16[64,5,2,1280]{3,2,1,0:T(2,128)(2,1)} %bitcast.22), calls=%async_computation.2 | async-start | bytes 3276800 | tf_op jit(solution)/shard_map/all_to_all | solution.py:450
  63.9 9.2 %collective-permute-start.1 = (bf16[640,1280]{1,0:T(8,128)(2,1)}, bf16[640,1280]{1,0:T(8,128)(2,1)}, u32[]{:S(2)}, u32[]{:S(2)}) collective-permute-start(bf16[640,1280]{1,0:T(8,128)(2,1)} %get-tuple-element.55), channel_id=1, source_target_pairs={{0,1},{1,0},{2,3},{3,2},{4,5},{5,4},{6,7},{7,6},{8,9},{9,8},{10,11... | collective-permute-start | bytes 4915208 | tf_op jit(solution)/shard_map/ppermute | solution.py:454
  73.1 9.6 %collective-permute-start.2 = (bf16[320,2,1280]{2,1,0:T(2,128)(2,1)S(1)}, bf16[320,2,1280]{2,1,0:T(2,128)(2,1)S(1)}, u32[]{:S(2)}, u32[]{:S(2)}) collective-permute-start(bf16[320,2,1280]{2,1,0:T(2,128)(2,1)S(1)} %bitcast.19), channel_id=1, source_target_pairs={{0,1},{1,0},{2,3},{3,2},{4,5},{5,4},{6,7},{7,6},{8,9},{9,8},{10,11... | collective-permute-start | bytes 4915208 | tf_op jit(solution)/shard_map/ppermute | solution.py:454
  76.7 31.4 %all-to-all-start.1 = ((bf16[64,5,2,1280]{3,2,1,0:T(2,128)(2,1)}), bf16[64,5,2,1280]{3,2,1,0:T(2,128)(2,1)}, u32[]{:S(2)}, u32[]{:S(2)}) async-start(bf16[64,5,2,1280]{3,2,1,0:T(2,128)(2,1)} %bitcast.24), calls=%async_computation.1 | async-start | bytes 3276800 | tf_op jit(solution)/shard_map/all_to_all | solution.py:450
  95.8 22.4 %collective-permute-start.3 = (bf16[640,1280]{1,0:T(8,128)(2,1)}, bf16[640,1280]{1,0:T(8,128)(2,1)S(1)}, u32[]{:S(2)}, u32[]{:S(2)}) collective-permute-start(bf16[640,1280]{1,0:T(8,128)(2,1)} %get-tuple-element.68), channel_id=1, source_target_pairs={{0,1},{1,0},{2,3},{3,2},{4,5},{5,4},{6,7},{7,6},{8,9},{9,8},{10,11... | collective-permute-start | bytes 4915208 | tf_op jit(solution)/shard_map/ppermute | solution.py:454
  114.0 7.4 %collective-permute-start.6 = (f32[1,1280]{1,0:T(1,128)S(1)}, f32[1,1280]{1,0:T(1,128)S(1)}, u32[]{:S(2)}, u32[]{:S(2)}) collective-permute-start(f32[1,1280]{1,0:T(1,128)S(1)} %psum.14.p0), channel_id=1, source_target_pairs={{6,0},{0,2},{2,4},{4,6},{7,1},{1,3},{3,5},{5,7},{14,8},{8,10},{10,... | collective-permute-start | bytes 15368 | tf_op jit(solution)/shard_map/ppermute | solution.py:335
  114.8 6.5 %collective-permute-start.5 = (f32[1,1280]{1,0:T(1,128)S(1)}, f32[1,1280]{1,0:T(1,128)S(1)}, u32[]{:S(2)}, u32[]{:S(2)}) collective-permute-start(f32[1,1280]{1,0:T(1,128)S(1)} %psum.14.p0), channel_id=1, source_target_pairs={{4,0},{6,2},{0,4},{2,6},{5,1},{7,3},{1,5},{3,7},{12,8},{14,10},{8,... | collective-permute-start | bytes 15368 | tf_op jit(solution)/shard_map/ppermute | solution.py:335
  116.2 5.1 %collective-permute-start.4 = (f32[1,1280]{1,0:T(1,128)S(1)}, f32[1,1280]{1,0:T(1,128)S(1)}, u32[]{:S(2)}, u32[]{:S(2)}) collective-permute-start(f32[1,1280]{1,0:T(1,128)S(1)} %psum.14.p0), channel_id=1, source_target_pairs={{2,0},{4,2},{6,4},{0,6},{3,1},{5,3},{7,5},{1,7},{10,8},{12,10},{14... | collective-permute-start | bytes 15368 | tf_op jit(solution)/shard_map/ppermute | solution.py:335
  121.3 30.5 %all-to-all-start.3 = ((bf16[64,5,2,1280]{3,2,1,0:T(2,128)(2,1)}), bf16[64,5,2,1280]{3,2,1,0:T(2,128)(2,1)S(1)}, u32[]{:S(2)}, u32[]{:S(2)}) async-start(bf16[64,5,2,1280]{3,2,1,0:T(2,128)(2,1)} %bitcast.23), calls=%async_computation.3 | async-start | bytes 3276800 | tf_op jit(solution)/shard_map/all_to_all | solution.py:450
  138.0 11.7 %collective-permute-start.9 = (f32[4,1408]{1,0:T(4,128)S(1)}, f32[4,1408]{1,0:T(4,128)S(1)}, u32[]{:S(2)}, u32[]{:S(2)}) collective-permute-start(f32[4,1408]{1,0:T(4,128)S(1)} %psum.15.m0), channel_id=1, source_target_pairs={{6,0},{0,2},{2,4},{4,6},{7,1},{1,3},{3,5},{5,7},{14,8},{8,10},{10,... | collective-permute-start | bytes 67592 | tf_op jit(solution)/shard_map/ppermute | solution.py:335
  139.6 10.1 %collective-permute-start.8 = (f32[4,1408]{1,0:T(4,128)S(1)}, f32[4,1408]{1,0:T(4,128)S(1)}, u32[]{:S(2)}, u32[]{:S(2)}) collective-permute-start(f32[4,1408]{1,0:T(4,128)S(1)} %psum.15.m0), channel_id=1, source_target_pairs={{4,0},{6,2},{0,4},{2,6},{5,1},{7,3},{1,5},{3,7},{12,8},{14,10},{8,... | collective-permute-start | bytes 67592 | tf_op jit(solution)/shard_map/ppermute | solution.py:335
  142.3 7.4 %collective-permute-start.7 = (f32[4,1408]{1,0:T(4,128)S(1)}, f32[4,1408]{1,0:T(4,128)S(1)}, u32[]{:S(2)}, u32[]{:S(2)}) collective-permute-start(f32[4,1408]{1,0:T(4,128)S(1)} %psum.15.m0), channel_id=1, source_target_pairs={{2,0},{4,2},{6,4},{0,6},{3,1},{5,3},{7,5},{1,7},{10,8},{12,10},{14... | collective-permute-start | bytes 67592 | tf_op jit(solution)/shard_map/ppermute | solution.py:335
  151.8 15.3 %all-to-all-start.4 = ((bf16[16,4,2304]{2,1,0:T(4,128)(2,1)}), bf16[16,4,2304]{2,1,0:T(4,128)(2,1)S(1)}, u32[]{:S(2)}, u32[]{:S(2)}) async-start(bf16[16,4,2304]{2,1,0:T(4,128)(2,1)} %get-tuple-element.93), calls=%async_computation.4 | async-start | bytes 589824 | tf_op jit(solution)/shard_map/all_to_all | solution.py:543

commit v7 on v6

--- a/solution.py
+++ b/solution.py
@@ -176,13 +176,13 @@
 
 
 def backward_body(
-    own_g, other_g, slope_in, w1_in, w2_in, gs_out, d_pre_out, own_out, other_out,
-    slope, w1, w2, gs, d_pre, own, other, in_sems, out_sems,
+    own_g, other_g, slope_in, w1_in, w2_in, hidden_in, xs_in, own_out, other_out, dw2_out, dw1_out,
+    slope, w1, w2, hidden, xs, gs, d_pre, own, other, dw2, dw1, in_sems, out_sems,
 ):
     first, last = HALVES
     pairs = (
         (w2_in, w2), (slope_in.at[first], slope.at[first]), (w1_in, w1),
-        (slope_in.at[last], slope.at[last]),
+        (slope_in.at[last], slope.at[last]), (hidden_in, hidden), (xs_in, xs),
     )
     copies = start_all(pairs, in_sems)
     saved = []
@@ -194,10 +194,6 @@
         for rows in chunks(half, 320):
             d_h = dot(gs[rows, :], w2[...], 1, 1)
             d_pre[rows, :] = (d_h * slope[rows, :].astype(F32)).astype(BF16)
-        saved += start_all(
-            [(v.at[half], o.at[half]) for v, o in ((gs, gs_out), (d_pre, d_pre_out))],
-            out_sems.at[n],
-        )
         if n == 0:
             copies[2].wait()
         for rows in chunks(half, 320):
@@ -207,60 +203,37 @@
                 own[there, :] = part
             else:
                 other[there, :] = part.astype(BF16)
-        saved += start_all([((own, other)[n], (own_out, other_out)[n])], out_sems.at[2 + n])
+        saved += start_all([((own, other)[n], (own_out, other_out)[n])], out_sems.at[n])
+    grads = ((hidden, gs, dw2, dw2_out), (xs, d_pre, dw1, dw1_out))
+    for n, (left, right, grad, grad_out) in enumerate(grads):
+        copies[4 + n].wait()
+        for m, cols in enumerate(HALVES):
+            grad[cols, :] = dot(left[:, cols], right[...], 0, 0).astype(BF16)
+            saved += start_all([(grad.at[cols], grad_out.at[cols])], out_sems.at[2 + 2 * n + m])
     for copy in saved:
         copy.wait()
 
 
 SQUARE = (ROWS, D)
-
-
-def expert_kernel(body, ins, kept, name):
-    outs = (*[shape(SQUARE, BF16)] * kept, shape((HALF, D), F32), shape((HALF, D), BF16))
-    scratch = [pltpu.VMEM((D, D), BF16)] * (len(ins) - 2)
-    scratch += [pltpu.VMEM(SQUARE, BF16)] * (kept if len(ins) == 4 else 2)
-    scratch += [pltpu.VMEM((HALF, D), F32), pltpu.VMEM((HALF, D), BF16)]
-    scratch += [
-        pltpu.SemaphoreType.DMA((4,)),
-        pltpu.SemaphoreType.DMA((4, 3)),
-    ]
+SENT = (shape((HALF, D), F32), shape((HALF, D), BF16))
+
+
+def expert_kernel(body, own, other, rest, outs, name):
+    inner = 2 if name == "backward" else 0
+    scratch = [pltpu.VMEM(SQUARE, BF16)] * (len(rest) + inner)
+    scratch += [pltpu.VMEM(out.shape, out.dtype) for out in outs]
+    scratch += [pltpu.SemaphoreType.DMA((6,)), pltpu.SemaphoreType.DMA((6, 3))]
     return run(
         body,
         outs,
-        in_vmem(ins[0]),
-        in_vmem(ins[1]),
-        *ins[2:],
-        specs=[VMEM] * 2 + [ANY] * (len(ins) - 2),
+        in_vmem(own),
+        in_vmem(other),
+        *rest,
+        specs=[VMEM] * 2 + [ANY] * len(rest),
         out_specs=tuple([ANY] * len(outs)),
         scratch=scratch,
         name=name,
     )
-
-
-GRAD_COLS = 640
-
-
-def weight_grad_body(left_ref, right_ref, *refs):
-    refs[-1][...] = dot(left_ref[...], right_ref[...], 0, 0).astype(BF16)
-
-
-def weight_grad(left, right, name, blocks=(0, 1), into=()):
-    first = blocks[0]
-    return pl.pallas_call(
-        weight_grad_body,
-        out_shape=shape((D, D), BF16),
-        grid=(len(blocks),),
-        in_specs=[
-            pl.BlockSpec((ROWS, GRAD_COLS), lambda i: (0, first + i)),
-            pl.BlockSpec((ROWS, D), lambda i: (0, 0)),
-            *[ANY for _ in into],
-        ],
-        out_specs=pl.BlockSpec((GRAD_COLS, D), lambda i: (first + i, 0)),
-        input_output_aliases={2: 0} if into else {},
-        name=name,
-        cost_estimate=TINY,
-        compiler_params=pltpu.CompilerParams(vmem_limit_bytes=56 << 20),
-    )(left, right, *into)
 
 
 def mark_body(in_ref, out_ref):
@@ -470,8 +443,9 @@
     g_send = run(g_body, shape(PACKED, BF16), table, out_grad, combine, name="dispatch_g")
     x_in, g_send = lax.optimization_barrier((x_in, g_send))
     g_in = chip_swap(g_send)
+    square = shape(SQUARE, BF16)
     xs, hidden, slope, own, other = expert_kernel(
-        forward_body, (x_in, core_swap(x_in), w_in, w_out), 3, "forward"
+        forward_body, x_in, core_swap(x_in), (w_in, w_out), (square, square, square, *SENT), "forward"
     )
     other = core_swap(other)
     digits = x_in.reshape(16, 2 * CAP, 2, WIDE)[:, :2, :, D:].reshape(IMAGES, 128)
@@ -490,12 +464,15 @@
     mark = run(mark_body, shape((1,), I32), mark, specs=[SMEM], out_specs=SMEM, name="mark", cost=LONG)
     own, mark = lax.optimization_barrier((own, mark))
     out_in = chip_swap(add_cores(own, other, "add_out"))
-    gs, d_pre, own, other = expert_kernel(
-        backward_body, (g_in, core_swap(g_in), slope, w_in, w_out), 2, "backward"
+    own, other, d_w_out, d_w_in = expert_kernel(
+        backward_body,
+        g_in,
+        core_swap(g_in),
+        (slope, w_in, w_out, hidden, xs),
+        (*SENT, square, square),
+        "backward",
     )
     other = core_swap(other)
-    d_w_out = weight_grad(hidden, gs, "d_w_out")
-    out_in, d_w_out = lax.optimization_barrier((out_in, d_w_out))
     mixed_out, d_combine, token_sum = run(
         mixed_body,
         (shape((TOK, D), BF16), shape((2, TOK), F32), shape((1, D), F32)),
@@ -524,10 +501,7 @@
         scratch=[pltpu.VMEM((D, COLS), BF16), pltpu.SemaphoreType.DMA((4,))],
         name="head",
     )
-    xs, part = lax.optimization_barrier((xs, part))
     messages = y_parts(lax.psum(part, "core"))
-    d_w_in = weight_grad(xs, d_pre, "d_w_in_low", blocks=(0,))
-    pooled, d_w_in = lax.optimization_barrier((pooled, d_w_in))
     d_pooled, losses = run(
         pooled_body,
         (shape((4, D), F32), shape((1, 4), F32)),
@@ -537,12 +511,9 @@
         specs=[SMEM] + [VMEM] * 5,
         name="d_pooled",
     )
-    dp_send, rows_in, d_pooled, d_w_in = lax.optimization_barrier(
-        (dp_send, rows_in, d_pooled, d_w_in)
-    )
+    dp_send, rows_in, d_pooled = lax.optimization_barrier((dp_send, rows_in, d_pooled))
     dp_in = lax.all_to_all(dp_send, "dp", 0, 0, tiled=True).reshape(IMAGES, COLS + 128)
     d_tokens = run(tokens_body, shape((TOK, D), BF16), table, in_vmem(rows_in), out_grad, name="d_tokens")
-    d_w_in = weight_grad(xs, d_pre, "d_w_in_high", blocks=(1,), into=(d_w_in,))
     d_head = dot(dp_in[:, COLS : COLS + 80], dp_in[:, :COLS], 0, 0).astype(BF16)
     return (mixed_out, d_tokens, d_combine.T, d_w_in, d_w_out, losses.reshape(4), d_pooled, d_head)
 

time: 169 us -> 169 us (level)
  Pallas kernels: 77.6 us -> 66.8 us
  waiting for transfers between devices: 34.4 us -> 45 us
    pallas_call x3 -> x0, Pallas kernels: 20.1 us -> none  [weight_grad(): pl.pallas_call(weight_grad_body, out_shape=shape((D, D), BF16), grid=(len...]
    pallas_call x11, Pallas kernels: 57.5 us -> 66.8 us  [run(): pl.pallas_call(body, out_shape=outs, grid=grid, in_specs=specs or [VMEM]...]
    all_to_all x1, waiting for transfers between devices: 0.64 us -> 6.56 us  [shards(): lax.all_to_all(dp_send, 'dp', 0, 0, tiled=True).reshape(IMAGES, COLS + 128)]
    ppermute x6, waiting for transfers between devices: 0.02 us -> 3.1 us  [y_parts(): lax.ppermute(mine, Y, [((i + shift) % 4, i) for i in range(4)])]
  transfers between devices with their start and end apart: 15 -> 15, of which waited for: 5 -> 6; matrix products, arithmetic and copies ran while one was open for 0% -> 0% of each run, Pallas kernels for 44% -> 38%
where the time goes in v7:
time: 169 us; the launch traced here: 168 us
  Pallas kernels  66.8 us (40%)
  starting transfers between devices  47.1 us (28%)
  waiting for transfers between devices  45 us (27%)
  blocking collectives  6.61 us (4%)
    pallas_call x11, Pallas kernels, run(): pl.pallas_call(body, out_shape=outs, grid=grid, in_specs=specs or [VMEM]...  66.8 us
    all_to_all x4, waiting for transfers between devices, chip_swap(): return lax.all_to_all(blocks, CHIP, 0, 0, tiled=True).reshape(dims)  35.3 us
    all_to_all x4, starting transfers between devices, chip_swap(): return lax.all_to_all(blocks, CHIP, 0, 0, tiled=True).reshape(dims)  31.1 us
    ppermute x6, starting transfers between devices, y_parts(): lax.ppermute(mine, Y, [((i + shift) % 4, i) for i in range(4)])  10.1 us
    all_to_all x1, waiting for transfers between devices, shards(): lax.all_to_all(dp_send, 'dp', 0, 0, tiled=True).reshape(IMAGES, COLS + 128)  6.56 us
    all_to_all x1, starting transfers between devices, shards(): lax.all_to_all(dp_send, 'dp', 0, 0, tiled=True).reshape(IMAGES, COLS + 128)  5.29 us
    psum x1, blocking collectives, shards(): messages = y_parts(lax.psum(part, 'core'))  4.02 us
  transfers between devices with their start and end apart: 15, of which 6 were waited for; matrix products, arithmetic and copies ran while one was open for 0% of the time, Pallas kernels for 38%

profile of v7, /device:TPU:0, one launch (start us, length us, event | category | flops | bytes accessed | tf_op | source)
XLA Modules:
  0.0 167.9 jit_solution(12346934810600542482)
XLA Ops:
  0.6 3.1 %dispatch_x.1 = (bf16[2,640,128]{2,1,0:T(8,128)(2,1)}, bf16[320,2,1408]{2,1,0:T(2,128)(2,1)}) custom-call(s32[2,128]{1,0:T(2,128)} %bitcast.27, s32[4,4]{1,0:T(4,128)} %labels_ref.3, bf16[128,1280]{1,0:T(8,128)(2,1)} %tokens_ref.3), custom_call_target="tpu_custom_call" | custom-call | flops 1 | bytes 1 | tf_op jit(solution)/shard_map/dispatch_x/pallas_call | solution.py:60
  3.7 11.5 %all-to-all-start = ((bf16[64,5,2,1408]{3,2,1,0:T(2,128)(2,1)}), bf16[64,5,2,1408]{3,2,1,0:T(2,128)(2,1)S(1)}, u32[]{:S(2)}, u32[]{:S(2)}) async-start(bf16[64,5,2,1408]{3,2,1,0:T(2,128)(2,1)} %bitcast.25), calls=%async_computation | async-start | bytes 3604480 | tf_op jit(solution)/shard_map/all_to_all | solution.py:423
  15.2 3.1 %dispatch_g.1 = bf16[320,2,1280]{2,1,0:T(2,128)(2,1)} custom-call(bf16[2,640,128]{2,1,0:T(8,128)(2,1)} %get-tuple-element.44.table_ref, bf16[128,1280]{1,0:T(8,128)(2,1)} %grad_ref.5, f32[2,128]{1,0:T(2,128)} %bitcast.28), custom_call_target="tpu_custom_call" | custom-call | flops 1 | bytes 1 | tf_op jit(solution)/shard_map/dispatch_g/pallas_call | solution.py:60
  18.3 23.5 %all-to-all-done = bf16[64,5,2,1408]{3,2,1,0:T(2,128)(2,1)S(1)} async-done(((bf16[64,5,2,1408]{3,2,1,0:T(2,128)(2,1)}), bf16[64,5,2,1408]{3,2,1,0:T(2,128)(2,1)S(1)}, u32[]{:S(2)}, u32[]{:S(2)}) %all-to-all-start) | async-done | bytes 1802272 | tf_op jit(solution)/shard_map/all_to_all | solution.py:423
  41.8 0.0 collective-permute-start
  41.8 5.8 %all-to-all-start.2 = ((bf16[64,5,2,1280]{3,2,1,0:T(2,128)(2,1)}), bf16[64,5,2,1280]{3,2,1,0:T(2,128)(2,1)S(1)}, u32[]{:S(2)}, u32[]{:S(2)}) async-start(bf16[64,5,2,1280]{3,2,1,0:T(2,128)(2,1)} %bitcast.22), calls=%async_computation.2 | async-start | bytes 3276800 | tf_op jit(solution)/shard_map/all_to_all | solution.py:423
  47.6 0.0 collective-permute-done.other_x
  47.6 16.3 %forward.1 = (bf16[1280,1280]{1,0:T(8,128)(2,1)}, bf16[1280,1280]{1,0:T(8,128)(2,1)}, bf16[1280,1280]{1,0:T(8,128)(2,1)}, f32[640,1280]{1,0:T(8,128)}, bf16[640,1280]{1,0:T(8,128)(2,1)}) custom-call(bf16[320,2,1408]{2,1,0:T(2,128)(2,1)S(1)} %bitcast.17, bf16[320,2,1408]{2,1,0:T(2,128)(2,1)} %collective-permute-done.other_x, bf16[1280,1280]{1,0:T(8,128)(2,1)} %w1_in.3, ...), custom_call_target="tpu_custom_call" | custom-call | flops 1 | bytes 1 | tf_op jit(solution)/shard_map/forward/pallas_call | solution.py:60
  64.0 0.3 collective-permute-start.1
  64.3 0.6 slice.12
  64.9 2.1 %labels.1 = (f32[4,2176]{1,0:T(4,128)}, f32[1,2176]{1,0:T(1,128)}) custom-call(s32[1]{0:T(128)} %bitcast.9.first_ref, bf16[64,128]{1,0:T(8,128)(2,1)} %bitcast.26, s32[4,4]{1,0:T(4,128)} %labels_ref.3), custom_call_target="tpu_custom_call" | custom-call | flops 1 | bytes 1 | tf_op jit(solution)/shard_map/labels/pallas_call | solution.py:60
  67.0 6.1 %all-to-all-done.2 = bf16[64,5,2,1280]{3,2,1,0:T(2,128)(2,1)S(1)} async-done(((bf16[64,5,2,1280]{3,2,1,0:T(2,128)(2,1)}), bf16[64,5,2,1280]{3,2,1,0:T(2,128)(2,1)S(1)}, u32[]{:S(2)}, u32[]{:S(2)}) %all-to-all-start.2) | async-done | bytes 1638432 | tf_op jit(solution)/shard_map/all_to_all | solution.py:423
  73.1 0.0 collective-permute-start.2
  73.1 0.0 collective-permute-done.1.other_ref
  73.1 3.6 %add_out.1 = bf16[320,2,1280]{2,1,0:T(2,128)(2,1)} custom-call(f32[640,1280]{1,0:T(8,128)} %get-tuple-element.47.own_ref, bf16[640,1280]{1,0:T(8,128)(2,1)} %collective-permute-done.1.other_ref), custom_call_target="tpu_custom_call" | custom-call | flops 1 | bytes 1 | tf_op jit(solution)/shard_map/add_out/pallas_call | solution.py:60
  76.7 6.2 %all-to-all-start.1 = ((bf16[64,5,2,1280]{3,2,1,0:T(2,128)(2,1)}), bf16[64,5,2,1280]{3,2,1,0:T(2,128)(2,1)}, u32[]{:S(2)}, u32[]{:S(2)}) async-start(bf16[64,5,2,1280]{3,2,1,0:T(2,128)(2,1)} %bitcast.24), calls=%async_computation.1 | async-start | bytes 3276800 | tf_op jit(solution)/shard_map/all_to_all | solution.py:423
  83.0 0.0 collective-permute-done.2.other_g
  83.0 22.2 %backward.1 = (f32[640,1280]{1,0:T(8,128)}, bf16[640,1280]{1,0:T(8,128)(2,1)}, bf16[1280,1280]{1,0:T(8,128)(2,1)}, bf16[1280,1280]{1,0:T(8,128)(2,1)}) custom-call(bf16[320,2,1280]{2,1,0:T(2,128)(2,1)S(1)} %bitcast.20, bf16[320,2,1280]{2,1,0:T(2,128)(2,1)S(1)} %collective-permute-done.2.other_g, bf16[1280,1280]{1,0:T(8,128)(2,1)} %get-tuple-element.54.slope_in, ...), custom_call_target="tpu_custom_call" | custom-call | flops 1 | bytes 1 | tf_op jit(solution)/shard_map/backward/pallas_call | solution.py:60
  105.2 0.3 collective-permute-start.3
  105.5 2.7 %all-to-all-done.1 = bf16[64,5,2,1280]{3,2,1,0:T(2,128)(2,1)} async-done(((bf16[64,5,2,1280]{3,2,1,0:T(2,128)(2,1)}), bf16[64,5,2,1280]{3,2,1,0:T(2,128)(2,1)}, u32[]{:S(2)}, u32[]{:S(2)}) %all-to-all-start.1) | async-done | bytes 1638432 | tf_op jit(solution)/shard_map/all_to_all | solution.py:423
  108.2 3.2 %mixed.1 = (bf16[128,1280]{1,0:T(8,128)(2,1)}, f32[2,128]{1,0:T(2,128)}, f32[1,1280]{1,0:T(1,128)}) custom-call(bf16[2,640,128]{2,1,0:T(8,128)(2,1)} %get-tuple-element.44.table_ref, bf16[320,2,1280]{2,1,0:T(2,128)(2,1)} %bitcast.5.in_ref, bf16[128,1280]{1,0:T(8,128)(2,1)} %tokens_ref.3, bf16[128,1280]{1,0:T(8,128)(2,1)} %grad_ref.5, f32[2,128]{1,0:T(2,128)} %bitcast.29), custom_call_target="tpu_custom_call" | custom-call | flops 17179869184 | bytes 67108864 | tf_op jit(solution)/shard_map/mixed/pallas_call | solution.py:60
  111.4 2.6 %psum.14.p0 = f32[1,1280]{1,0:T(1,128)S(1)} all-reduce(f32[1,1280]{1,0:T(1,128)} %get-tuple-element.58), channel_id=1, replica_groups=mesh['dp'=16,'yh'=2,'yl'=2,'core'=2] {'core'}, use_global_device_ids=true, to_apply=%region_0.0 | all-reduce | flops 1280 | bytes 10240 | tf_op jit(solution)/shard_map/psum | solution.py:487
  114.0 0.8 collective-permute-start.6
  114.8 1.4 collective-permute-start.5
  116.2 2.0 %collective-permute-start.4 = (f32[1,1280]{1,0:T(1,128)S(1)}, f32[1,1280]{1,0:T(1,128)S(1)}, u32[]{:S(2)}, u32[]{:S(2)}) collective-permute-start(f32[1,1280]{1,0:T(1,128)S(1)} %psum.14.p0), channel_id=1, source_target_pairs={{2,0},{4,2},{6,4},{0,6},{3,1},{5,3},{7,5},{1,7},{10,8},{12,10},{14... | collective-permute-start | bytes 15368 | tf_op jit(solution)/shard_map/ppermute | solution.py:308
  118.2 0.0 collective-permute-done.3.other_ref
  118.2 3.1 %add_rows.1 = bf16[320,2,1280]{2,1,0:T(2,128)(2,1)} custom-call(f32[640,1280]{1,0:T(8,128)} %get-tuple-element.59.own_ref, bf16[640,1280]{1,0:T(8,128)(2,1)S(1)} %collective-permute-done.3.other_ref), custom_call_target="tpu_custom_call" | custom-call | flops 1 | bytes 1 | tf_op jit(solution)/shard_map/add_rows/pallas_call | solution.py:60
  121.4 0.0 collective-permute-done.6.p3
  121.4 0.0 collective-permute-done.5.p2
  121.4 0.0 collective-permute-done.4.p1
  121.4 7.6 %all-to-all-start.3 = ((bf16[64,5,2,1280]{3,2,1,0:T(2,128)(2,1)}), bf16[64,5,2,1280]{3,2,1,0:T(2,128)(2,1)S(1)}, u32[]{:S(2)}, u32[]{:S(2)}) async-start(bf16[64,5,2,1280]{3,2,1,0:T(2,128)(2,1)} %bitcast.23), calls=%async_computation.3 | async-start | bytes 3276800 | tf_op jit(solution)/shard_map/all_to_all | solution.py:423
  129.0 6.1 %head.1 = (f32[4,1280]{1,0:T(4,128)}, f32[4,1408]{1,0:T(4,128)}, bf16[16,4,2304]{2,1,0:T(4,128)(2,1)}) custom-call(s32[1]{0:T(128)} %bitcast.6.here_ref, f32[1,1280]{1,0:T(1,128)S(1)} %psum.14.p0, f32[1,1280]{1,0:T(1,128)S(1)} %collective-permute-done.4.p1, f32[1,1280]{1,0:T(1,128)S(1)} %collective-permute-done.5.p2, ...), custom_call_target="tpu_custom_call" | custom-call | flops 1 | bytes 1 | tf_op jit(solution)/shard_map/head/pallas_call | solution.py:60
  135.1 4.0 %psum.15.m0 = f32[4,1408]{1,0:T(4,128)S(1)} all-reduce(f32[4,1408]{1,0:T(4,128)} %get-tuple-element.70), channel_id=1, replica_groups=mesh['dp'=16,'yh'=2,'yl'=2,'core'=2] {'core'}, use_global_device_ids=true, to_apply=%region_1.0 | all-reduce | flops 5632 | bytes 45056 | tf_op jit(solution)/shard_map/psum | solution.py:504
  139.1 1.6 collective-permute-start.9
  140.7 2.7 %collective-permute-start.8 = (f32[4,1408]{1,0:T(4,128)S(1)}, f32[4,1408]{1,0:T(4,128)S(1)}, u32[]{:S(2)}, u32[]{:S(2)}) collective-permute-start(f32[4,1408]{1,0:T(4,128)S(1)} %psum.15.m0), channel_id=1, source_target_pairs={{4,0},{6,2},{0,4},{2,6},{5,1},{7,3},{1,5},{3,7},{12,8},{14,10},{8,... | collective-permute-start | bytes 67592 | tf_op jit(solution)/shard_map/ppermute | solution.py:308
  143.4 1.5 collective-permute-start.7
  144.9 3.1 %collective-permute-done.9.m3 = f32[4,1408]{1,0:T(4,128)S(1)} collective-permute-done((f32[4,1408]{1,0:T(4,128)S(1)}, f32[4,1408]{1,0:T(4,128)S(1)}, u32[]{:S(2)}, u32[]{:S(2)}) %collective-permute-start.9) | collective-permute-done | bytes 22560 | tf_op jit(solution)/shard_map/ppermute | solution.py:308
  147.9 0.0 collective-permute-done.8.m2
  148.0 0.0 collective-permute-done.7.m1
  148.0 1.6 d_pooled.1
  149.6 3.0 %all-to-all-done.3 = bf16[64,5,2,1280]{3,2,1,0:T(2,128)(2,1)S(1)} async-done(((bf16[64,5,2,1280]{3,2,1,0:T(2,128)(2,1)}), bf16[64,5,2,1280]{3,2,1,0:T(2,128)(2,1)S(1)}, u32[]{:S(2)}, u32[]{:S(2)}) %all-to-all-start.3) | async-done | bytes 1638432 | tf_op jit(solution)/shard_map/all_to_all | solution.py:423
  152.6 5.3 %all-to-all-start.4 = ((bf16[16,4,2304]{2,1,0:T(4,128)(2,1)}), bf16[16,4,2304]{2,1,0:T(4,128)(2,1)S(1)}, u32[]{:S(2)}, u32[]{:S(2)}) async-start(bf16[16,4,2304]{2,1,0:T(4,128)(2,1)} %get-tuple-element.79), calls=%async_computation.4 | async-start | bytes 589824 | tf_op jit(solution)/shard_map/all_to_all | solution.py:515
  157.9 2.3 %d_tokens.1 = bf16[128,1280]{1,0:T(8,128)(2,1)} custom-call(bf16[2,640,128]{2,1,0:T(8,128)(2,1)} %get-tuple-element.44.table_ref, bf16[320,2,1280]{2,1,0:T(2,128)(2,1)S(1)} %bitcast.21, bf16[128,1280]{1,0:T(8,128)(2,1)} %grad_ref.5), custom_call_target="tpu_custom_call" | custom-call | flops 1 | bytes 1 | tf_op jit(solution)/shard_map/d_tokens/pallas_call | solution.py:60
  160.2 6.6 %all-to-all-done.4 = bf16[16,4,2304]{2,1,0:T(4,128)(2,1)S(1)} async-done(((bf16[16,4,2304]{2,1,0:T(4,128)(2,1)}), bf16[16,4,2304]{2,1,0:T(4,128)(2,1)S(1)}, u32[]{:S(2)}, u32[]{:S(2)}) %all-to-all-start.4) | async-done | bytes 294944 | tf_op jit(solution)/shard_map/all_to_all | solution.py:515
  166.8 0.1 reshape.71
  166.9 1.0 convolution_convert_fusion
Async XLA Ops:
  3.7 38.0 %all-to-all-start = ((bf16[64,5,2,1408]{3,2,1,0:T(2,128)(2,1)}), bf16[64,5,2,1408]{3,2,1,0:T(2,128)(2,1)S(1)}, u32[]{:S(2)}, u32[]{:S(2)}) async-start(bf16[64,5,2,1408]{3,2,1,0:T(2,128)(2,1)} %bitcast.25), calls=%async_computation | async-start | bytes 3604480 | tf_op jit(solution)/shard_map/all_to_all | solution.py:423
  41.8 5.8 %collective-permute-start = (bf16[320,2,1408]{2,1,0:T(2,128)(2,1)S(1)}, bf16[320,2,1408]{2,1,0:T(2,128)(2,1)}, u32[]{:S(2)}, u32[]{:S(2)}) collective-permute-start(bf16[320,2,1408]{2,1,0:T(2,128)(2,1)S(1)} %bitcast.16), channel_id=1, source_target_pairs={{0,1},{1,0},{2,3},{3,2},{4,5},{5,4},{6,7},{7,6},{8,9},{9,8},{10,11... | collective-permute-start | bytes 5406728 | tf_op jit(solution)/shard_map/ppermute | solution.py:427
  41.8 31.3 %all-to-all-start.2 = ((bf16[64,5,2,1280]{3,2,1,0:T(2,128)(2,1)}), bf16[64,5,2,1280]{3,2,1,0:T(2,128)(2,1)S(1)}, u32[]{:S(2)}, u32[]{:S(2)}) async-start(bf16[64,5,2,1280]{3,2,1,0:T(2,128)(2,1)} %bitcast.22), calls=%async_computation.2 | async-start | bytes 3276800 | tf_op jit(solution)/shard_map/all_to_all | solution.py:423
  64.0 9.2 %collective-permute-start.1 = (bf16[640,1280]{1,0:T(8,128)(2,1)}, bf16[640,1280]{1,0:T(8,128)(2,1)}, u32[]{:S(2)}, u32[]{:S(2)}) collective-permute-start(bf16[640,1280]{1,0:T(8,128)(2,1)} %get-tuple-element.48), channel_id=1, source_target_pairs={{0,1},{1,0},{2,3},{3,2},{4,5},{5,4},{6,7},{7,6},{8,9},{9,8},{10,11... | collective-permute-start | bytes 4915208 | tf_op jit(solution)/shard_map/ppermute | solution.py:427
  73.1 9.8 %collective-permute-start.2 = (bf16[320,2,1280]{2,1,0:T(2,128)(2,1)S(1)}, bf16[320,2,1280]{2,1,0:T(2,128)(2,1)S(1)}, u32[]{:S(2)}, u32[]{:S(2)}) collective-permute-start(bf16[320,2,1280]{2,1,0:T(2,128)(2,1)S(1)} %bitcast.19), channel_id=1, source_target_pairs={{0,1},{1,0},{2,3},{3,2},{4,5},{5,4},{6,7},{7,6},{8,9},{9,8},{10,11... | collective-permute-start | bytes 4915208 | tf_op jit(solution)/shard_map/ppermute | solution.py:427
  76.7 31.4 %all-to-all-start.1 = ((bf16[64,5,2,1280]{3,2,1,0:T(2,128)(2,1)}), bf16[64,5,2,1280]{3,2,1,0:T(2,128)(2,1)}, u32[]{:S(2)}, u32[]{:S(2)}) async-start(bf16[64,5,2,1280]{3,2,1,0:T(2,128)(2,1)} %bitcast.24), calls=%async_computation.1 | async-start | bytes 3276800 | tf_op jit(solution)/shard_map/all_to_all | solution.py:423
  105.2 13.1 %collective-permute-start.3 = (bf16[640,1280]{1,0:T(8,128)(2,1)}, bf16[640,1280]{1,0:T(8,128)(2,1)S(1)}, u32[]{:S(2)}, u32[]{:S(2)}) collective-permute-start(bf16[640,1280]{1,0:T(8,128)(2,1)} %get-tuple-element.60), channel_id=1, source_target_pairs={{0,1},{1,0},{2,3},{3,2},{4,5},{5,4},{6,7},{7,6},{8,9},{9,8},{10,11... | collective-permute-start | bytes 4915208 | tf_op jit(solution)/shard_map/ppermute | solution.py:427
  114.0 7.4 %collective-permute-start.6 = (f32[1,1280]{1,0:T(1,128)S(1)}, f32[1,1280]{1,0:T(1,128)S(1)}, u32[]{:S(2)}, u32[]{:S(2)}) collective-permute-start(f32[1,1280]{1,0:T(1,128)S(1)} %psum.14.p0), channel_id=1, source_target_pairs={{6,0},{0,2},{2,4},{4,6},{7,1},{1,3},{3,5},{5,7},{14,8},{8,10},{10,... | collective-permute-start | bytes 15368 | tf_op jit(solution)/shard_map/ppermute | solution.py:308
  114.8 6.6 %collective-permute-start.5 = (f32[1,1280]{1,0:T(1,128)S(1)}, f32[1,1280]{1,0:T(1,128)S(1)}, u32[]{:S(2)}, u32[]{:S(2)}) collective-permute-start(f32[1,1280]{1,0:T(1,128)S(1)} %psum.14.p0), channel_id=1, source_target_pairs={{4,0},{6,2},{0,4},{2,6},{5,1},{7,3},{1,5},{3,7},{12,8},{14,10},{8,... | collective-permute-start | bytes 15368 | tf_op jit(solution)/shard_map/ppermute | solution.py:308
  116.2 5.2 %collective-permute-start.4 = (f32[1,1280]{1,0:T(1,128)S(1)}, f32[1,1280]{1,0:T(1,128)S(1)}, u32[]{:S(2)}, u32[]{:S(2)}) collective-permute-start(f32[1,1280]{1,0:T(1,128)S(1)} %psum.14.p0), channel_id=1, source_target_pairs={{2,0},{4,2},{6,4},{0,6},{3,1},{5,3},{7,5},{1,7},{10,8},{12,10},{14... | collective-permute-start | bytes 15368 | tf_op jit(solution)/shard_map/ppermute | solution.py:308
  121.4 31.2 %all-to-all-start.3 = ((bf16[64,5,2,1280]{3,2,1,0:T(2,128)(2,1)}), bf16[64,5,2,1280]{3,2,1,0:T(2,128)(2,1)S(1)}, u32[]{:S(2)}, u32[]{:S(2)}) async-start(bf16[64,5,2,1280]{3,2,1,0:T(2,128)(2,1)} %bitcast.23), calls=%async_computation.3 | async-start | bytes 3276800 | tf_op jit(solution)/shard_map/all_to_all | solution.py:423
  139.1 8.9 %collective-permute-start.9 = (f32[4,1408]{1,0:T(4,128)S(1)}, f32[4,1408]{1,0:T(4,128)S(1)}, u32[]{:S(2)}, u32[]{:S(2)}) collective-permute-start(f32[4,1408]{1,0:T(4,128)S(1)} %psum.15.m0), channel_id=1, source_target_pairs={{6,0},{0,2},{2,4},{4,6},{7,1},{1,3},{3,5},{5,7},{14,8},{8,10},{10,... | collective-permute-start | bytes 67592 | tf_op jit(solution)/shard_map/ppermute | solution.py:308
  140.7 7.2 %collective-permute-start.8 = (f32[4,1408]{1,0:T(4,128)S(1)}, f32[4,1408]{1,0:T(4,128)S(1)}, u32[]{:S(2)}, u32[]{:S(2)}) collective-permute-start(f32[4,1408]{1,0:T(4,128)S(1)} %psum.15.m0), channel_id=1, source_target_pairs={{4,0},{6,2},{0,4},{2,6},{5,1},{7,3},{1,5},{3,7},{12,8},{14,10},{8,... | collective-permute-start | bytes 67592 | tf_op jit(solution)/shard_map/ppermute | solution.py:308
  143.4 4.6 %collective-permute-start.7 = (f32[4,1408]{1,0:T(4,128)S(1)}, f32[4,1408]{1,0:T(4,128)S(1)}, u32[]{:S(2)}, u32[]{:S(2)}) collective-permute-start(f32[4,1408]{1,0:T(4,128)S(1)} %psum.15.m0), channel_id=1, source_target_pairs={{2,0},{4,2},{6,4},{0,6},{3,1},{5,3},{7,5},{1,7},{10,8},{12,10},{14... | collective-permute-start | bytes 67592 | tf_op jit(solution)/shard_map/ppermute | solution.py:308
  152.6 14.2 %all-to-all-start.4 = ((bf16[16,4,2304]{2,1,0:T(4,128)(2,1)}), bf16[16,4,2304]{2,1,0:T(4,128)(2,1)S(1)}, u32[]{:S(2)}, u32[]{:S(2)}) async-start(bf16[16,4,2304]{2,1,0:T(4,128)(2,1)} %get-tuple-element.79), calls=%async_computation.4 | async-start | bytes 589824 | tf_op jit(solution)/shard_map/all_to_all | solution.py:515

commit v8 on v7

--- a/solution.py
+++ b/solution.py
@@ -484,11 +484,9 @@
         name="mixed",
         cost=LONG,
     )
-    token_sum = lax.psum(token_sum, "core")
     own, token_sum = lax.optimization_barrier((own, token_sum))
-    rows_send = add_cores(own, other, "add_rows")
-    rows_send, *sums = lax.optimization_barrier((rows_send, *y_parts(token_sum)))
-    rows_in = chip_swap(rows_send)
+    rows_in = chip_swap(add_cores(own, other, "add_rows"))
+    sums = y_parts(lax.psum(token_sum, "core"))
     pooled, part, dp_send = run(
         head_body,
         (shape((4, D), F32), shape((4, D + 128), F32), shape((16, 4, COLS + 128), BF16)),
@@ -501,7 +499,8 @@
         scratch=[pltpu.VMEM((D, COLS), BF16), pltpu.SemaphoreType.DMA((4,))],
         name="head",
     )
-    messages = y_parts(lax.psum(part, "core"))
+    part, rows_in = lax.optimization_barrier((lax.psum(part, "core"), rows_in))
+    messages = y_parts(part)
     d_pooled, losses = run(
         pooled_body,
         (shape((4, D), F32), shape((1, 4), F32)),
@@ -511,7 +510,7 @@
         specs=[SMEM] + [VMEM] * 5,
         name="d_pooled",
     )
-    dp_send, rows_in, d_pooled = lax.optimization_barrier((dp_send, rows_in, d_pooled))
+    dp_send, rows_in = lax.optimization_barrier((dp_send, rows_in))
     dp_in = lax.all_to_all(dp_send, "dp", 0, 0, tiled=True).reshape(IMAGES, COLS + 128)
     d_tokens = run(tokens_body, shape((TOK, D), BF16), table, in_vmem(rows_in), out_grad, name="d_tokens")
     d_head = dot(dp_in[:, COLS : COLS + 80], dp_in[:, :COLS], 0, 0).astype(BF16)

time: 169 us -> 173 us (1.024)
  starting transfers between devices: 47.1 us -> 53.3 us
  waiting for transfers between devices: 45 us -> 42.4 us
    all_to_all x1, starting transfers between devices: 5.29 us -> 11.7 us  [shards(): lax.all_to_all(dp_send, 'dp', 0, 0, tiled=True).reshape(IMAGES, COLS + 128)]
    ppermute x6, waiting for transfers between devices: 3.1 us -> 8.37 us  [y_parts(): lax.ppermute(mine, Y, [((i + shift) % 4, i) for i in range(4)])]
    all_to_all x1, waiting for transfers between devices: 6.56 us -> 1.73 us  [shards(): lax.all_to_all(dp_send, 'dp', 0, 0, tiled=True).reshape(IMAGES, COLS + 128)]
    all_to_all x4, waiting for transfers between devices: 35.3 us -> 32.3 us  [chip_swap(): return lax.all_to_all(blocks, CHIP, 0, 0, tiled=True).reshape(dims)]
  transfers between devices with their start and end apart: 15 -> 15, of which waited for: 6 -> 7; matrix products, arithmetic and copies ran while one was open for 0% -> 0% of each run, Pallas kernels for 38% -> 35%
where the time goes in v8:
time: 173 us; the launch traced here: 171 us
  Pallas kernels  66.8 us (39%)
  starting transfers between devices  53.3 us (31%)
  waiting for transfers between devices  42.4 us (25%)
  blocking collectives  6.51 us (4%)
    pallas_call x11, Pallas kernels, run(): pl.pallas_call(body, out_shape=outs, grid=grid, in_specs=specs or [VMEM]...  66.8 us
    all_to_all x4, waiting for transfers between devices, chip_swap(): return lax.all_to_all(blocks, CHIP, 0, 0, tiled=True).reshape(dims)  32.3 us
    all_to_all x4, starting transfers between devices, chip_swap(): return lax.all_to_all(blocks, CHIP, 0, 0, tiled=True).reshape(dims)  31.5 us
    all_to_all x1, starting transfers between devices, shards(): lax.all_to_all(dp_send, 'dp', 0, 0, tiled=True).reshape(IMAGES, COLS + 128)  11.7 us
    ppermute x6, starting transfers between devices, y_parts(): lax.ppermute(mine, Y, [((i + shift) % 4, i) for i in range(4)])  9.43 us
    ppermute x6, waiting for transfers between devices, y_parts(): lax.ppermute(mine, Y, [((i + shift) % 4, i) for i in range(4)])  8.37 us
    psum x1, blocking collectives, shards(): part, rows_in = lax.optimization_barrier((lax.psum(part, 'core'), rows_in))  4.02 us
  transfers between devices with their start and end apart: 15, of which 7 were waited for; matrix products, arithmetic and copies ran while one was open for 0% of the time, Pallas kernels for 35%

profile of v8, /device:TPU:0, one launch (start us, length us, event | category | flops | bytes accessed | tf_op | source)
XLA Modules:
  0.0 171.4 jit_solution(14363218770564550386)
XLA Ops:
  0.6 3.1 %dispatch_x.1 = (bf16[2,640,128]{2,1,0:T(8,128)(2,1)}, bf16[320,2,1408]{2,1,0:T(2,128)(2,1)}) custom-call(s32[2,128]{1,0:T(2,128)} %bitcast.27, s32[4,4]{1,0:T(4,128)} %labels_ref.3, bf16[128,1280]{1,0:T(8,128)(2,1)} %tokens_ref.3), custom_call_target="tpu_custom_call" | custom-call | flops 1 | bytes 1 | tf_op jit(solution)/shard_map/dispatch_x/pallas_call | solution.py:60
  3.7 11.5 %all-to-all-start = ((bf16[64,5,2,1408]{3,2,1,0:T(2,128)(2,1)}), bf16[64,5,2,1408]{3,2,1,0:T(2,128)(2,1)S(1)}, u32[]{:S(2)}, u32[]{:S(2)}) async-start(bf16[64,5,2,1408]{3,2,1,0:T(2,128)(2,1)} %bitcast.25), calls=%async_computation | async-start | bytes 3604480 | tf_op jit(solution)/shard_map/all_to_all | solution.py:423
  15.2 3.1 %dispatch_g.1 = bf16[320,2,1280]{2,1,0:T(2,128)(2,1)} custom-call(bf16[2,640,128]{2,1,0:T(8,128)(2,1)} %get-tuple-element.40.table_ref, bf16[128,1280]{1,0:T(8,128)(2,1)} %grad_ref.5, f32[2,128]{1,0:T(2,128)} %bitcast.28), custom_call_target="tpu_custom_call" | custom-call | flops 1 | bytes 1 | tf_op jit(solution)/shard_map/dispatch_g/pallas_call | solution.py:60
  18.3 23.5 %all-to-all-done = bf16[64,5,2,1408]{3,2,1,0:T(2,128)(2,1)S(1)} async-done(((bf16[64,5,2,1408]{3,2,1,0:T(2,128)(2,1)}), bf16[64,5,2,1408]{3,2,1,0:T(2,128)(2,1)S(1)}, u32[]{:S(2)}, u32[]{:S(2)}) %all-to-all-start) | async-done | bytes 1802272 | tf_op jit(solution)/shard_map/all_to_all | solution.py:423
  41.8 0.0 collective-permute-start
  41.8 5.8 %all-to-all-start.2 = ((bf16[64,5,2,1280]{3,2,1,0:T(2,128)(2,1)}), bf16[64,5,2,1280]{3,2,1,0:T(2,128)(2,1)S(1)}, u32[]{:S(2)}, u32[]{:S(2)}) async-start(bf16[64,5,2,1280]{3,2,1,0:T(2,128)(2,1)} %bitcast.22), calls=%async_computation.2 | async-start | bytes 3276800 | tf_op jit(solution)/shard_map/all_to_all | solution.py:423
  47.6 0.0 collective-permute-done.other_x
  47.6 16.3 %forward.1 = (bf16[1280,1280]{1,0:T(8,128)(2,1)}, bf16[1280,1280]{1,0:T(8,128)(2,1)}, bf16[1280,1280]{1,0:T(8,128)(2,1)}, f32[640,1280]{1,0:T(8,128)}, bf16[640,1280]{1,0:T(8,128)(2,1)}) custom-call(bf16[320,2,1408]{2,1,0:T(2,128)(2,1)S(1)} %bitcast.17, bf16[320,2,1408]{2,1,0:T(2,128)(2,1)} %collective-permute-done.other_x, bf16[1280,1280]{1,0:T(8,128)(2,1)} %w1_in.3, ...), custom_call_target="tpu_custom_call" | custom-call | flops 1 | bytes 1 | tf_op jit(solution)/shard_map/forward/pallas_call | solution.py:60
  64.0 0.3 collective-permute-start.1
  64.3 0.6 slice.12
  64.9 2.1 %labels.1 = (f32[4,2176]{1,0:T(4,128)}, f32[1,2176]{1,0:T(1,128)}) custom-call(s32[1]{0:T(128)} %bitcast.9.first_ref, bf16[64,128]{1,0:T(8,128)(2,1)} %bitcast.26, s32[4,4]{1,0:T(4,128)} %labels_ref.3), custom_call_target="tpu_custom_call" | custom-call | flops 1 | bytes 1 | tf_op jit(solution)/shard_map/labels/pallas_call | solution.py:60
  67.0 6.1 %all-to-all-done.2 = bf16[64,5,2,1280]{3,2,1,0:T(2,128)(2,1)S(1)} async-done(((bf16[64,5,2,1280]{3,2,1,0:T(2,128)(2,1)}), bf16[64,5,2,1280]{3,2,1,0:T(2,128)(2,1)S(1)}, u32[]{:S(2)}, u32[]{:S(2)}) %all-to-all-start.2) | async-done | bytes 1638432 | tf_op jit(solution)/shard_map/all_to_all | solution.py:423
  73.1 0.0 collective-permute-start.2
  73.1 0.0 collective-permute-done.1.other_ref
  73.1 3.6 %add_out.1 = bf16[320,2,1280]{2,1,0:T(2,128)(2,1)} custom-call(f32[640,1280]{1,0:T(8,128)} %get-tuple-element.43.own_ref, bf16[640,1280]{1,0:T(8,128)(2,1)} %collective-permute-done.1.other_ref), custom_call_target="tpu_custom_call" | custom-call | flops 1 | bytes 1 | tf_op jit(solution)/shard_map/add_out/pallas_call | solution.py:60
  76.7 6.2 %all-to-all-start.1 = ((bf16[64,5,2,1280]{3,2,1,0:T(2,128)(2,1)}), bf16[64,5,2,1280]{3,2,1,0:T(2,128)(2,1)}, u32[]{:S(2)}, u32[]{:S(2)}) async-start(bf16[64,5,2,1280]{3,2,1,0:T(2,128)(2,1)} %bitcast.24), calls=%async_computation.1 | async-start | bytes 3276800 | tf_op jit(solution)/shard_map/all_to_all | solution.py:423
  83.0 0.0 collective-permute-done.2.other_g
  83.0 22.2 %backward.1 = (f32[640,1280]{1,0:T(8,128)}, bf16[640,1280]{1,0:T(8,128)(2,1)}, bf16[1280,1280]{1,0:T(8,128)(2,1)}, bf16[1280,1280]{1,0:T(8,128)(2,1)}) custom-call(bf16[320,2,1280]{2,1,0:T(2,128)(2,1)S(1)} %bitcast.20, bf16[320,2,1280]{2,1,0:T(2,128)(2,1)S(1)} %collective-permute-done.2.other_g, bf16[1280,1280]{1,0:T(8,128)(2,1)} %get-tuple-element.50.slope_in, ...), custom_call_target="tpu_custom_call" | custom-call | flops 1 | bytes 1 | tf_op jit(solution)/shard_map/backward/pallas_call | solution.py:60
  105.2 0.3 collective-permute-start.6
  105.5 2.7 %all-to-all-done.1 = bf16[64,5,2,1280]{3,2,1,0:T(2,128)(2,1)} async-done(((bf16[64,5,2,1280]{3,2,1,0:T(2,128)(2,1)}), bf16[64,5,2,1280]{3,2,1,0:T(2,128)(2,1)}, u32[]{:S(2)}, u32[]{:S(2)}) %all-to-all-start.1) | async-done | bytes 1638432 | tf_op jit(solution)/shard_map/all_to_all | solution.py:423
  108.2 3.2 %mixed.1 = (bf16[128,1280]{1,0:T(8,128)(2,1)}, f32[2,128]{1,0:T(2,128)}, f32[1,1280]{1,0:T(1,128)}) custom-call(bf16[2,640,128]{2,1,0:T(8,128)(2,1)} %get-tuple-element.40.table_ref, bf16[320,2,1280]{2,1,0:T(2,128)(2,1)} %bitcast.5.in_ref, bf16[128,1280]{1,0:T(8,128)(2,1)} %tokens_ref.3, bf16[128,1280]{1,0:T(8,128)(2,1)} %grad_ref.5, f32[2,128]{1,0:T(2,128)} %bitcast.29), custom_call_target="tpu_custom_call" | custom-call | flops 17179869184 | bytes 67108864 | tf_op jit(solution)/shard_map/mixed/pallas_call | solution.py:60
  111.4 0.0 collective-permute-done.6.other_ref
  111.4 3.1 %add_rows.1 = bf16[320,2,1280]{2,1,0:T(2,128)(2,1)} custom-call(f32[640,1280]{1,0:T(8,128)} %get-tuple-element.60.own_ref, bf16[640,1280]{1,0:T(8,128)(2,1)S(1)} %collective-permute-done.6.other_ref), custom_call_target="tpu_custom_call" | custom-call | flops 1 | bytes 1 | tf_op jit(solution)/shard_map/add_rows/pallas_call | solution.py:60
  114.5 0.0 copy-start
  114.5 8.0 %all-to-all-start.3 = ((bf16[64,5,2,1280]{3,2,1,0:T(2,128)(2,1)}), bf16[64,5,2,1280]{3,2,1,0:T(2,128)(2,1)S(1)}, u32[]{:S(2)}, u32[]{:S(2)}) async-start(bf16[64,5,2,1280]{3,2,1,0:T(2,128)(2,1)} %bitcast.23), calls=%async_computation.3 | async-start | bytes 3276800 | tf_op jit(solution)/shard_map/all_to_all | solution.py:423
  122.5 0.0 copy-done
  122.5 2.5 %psum.14.p0 = f32[1,1280]{1,0:T(1,128)S(1)} all-reduce(f32[1,1280]{1,0:T(1,128)S(1)} %copy-done), channel_id=1, replica_groups=mesh['dp'=16,'yh'=2,'yl'=2,'core'=2] {'core'}, use_global_device_ids=true, to_apply=%region_0.0 | all-reduce | flops 1280 | bytes 10240 | tf_op jit(solution)/shard_map/psum | solution.py:489
  125.0 1.6 collective-permute-start.5
  126.6 2.7 %collective-permute-start.4 = (f32[1,1280]{1,0:T(1,128)S(1)}, f32[1,1280]{1,0:T(1,128)S(1)}, u32[]{:S(2)}, u32[]{:S(2)}) collective-permute-start(f32[1,1280]{1,0:T(1,128)S(1)} %psum.14.p0), channel_id=1, source_target_pairs={{4,0},{6,2},{0,4},{2,6},{5,1},{7,3},{1,5},{3,7},{12,8},{14,10},{8,... | collective-permute-start | bytes 15368 | tf_op jit(solution)/shard_map/ppermute | solution.py:308
  129.3 1.5 collective-permute-start.3
  130.7 5.6 %collective-permute-done.5.p3 = f32[1,1280]{1,0:T(1,128)S(1)} collective-permute-done((f32[1,1280]{1,0:T(1,128)S(1)}, f32[1,1280]{1,0:T(1,128)S(1)}, u32[]{:S(2)}, u32[]{:S(2)}) %collective-permute-start.5) | collective-permute-done | bytes 5152 | tf_op jit(solution)/shard_map/ppermute | solution.py:308
  136.3 2.6 %collective-permute-done.4.p2 = f32[1,1280]{1,0:T(1,128)S(1)} collective-permute-done((f32[1,1280]{1,0:T(1,128)S(1)}, f32[1,1280]{1,0:T(1,128)S(1)}, u32[]{:S(2)}, u32[]{:S(2)}) %collective-permute-start.4) | collective-permute-done | bytes 5152 | tf_op jit(solution)/shard_map/ppermute | solution.py:308
  138.9 0.0 collective-permute-done.3.p1
  138.9 6.1 %head.1 = (f32[4,1280]{1,0:T(4,128)}, f32[4,1408]{1,0:T(4,128)}, bf16[16,4,2304]{2,1,0:T(4,128)(2,1)}) custom-call(s32[1]{0:T(128)} %bitcast.6.here_ref, f32[1,1280]{1,0:T(1,128)S(1)} %psum.14.p0, f32[1,1280]{1,0:T(1,128)S(1)} %collective-permute-done.3.p1, f32[1,1280]{1,0:T(1,128)S(1)} %collective-permute-done.4.p2, ...), custom_call_target="tpu_custom_call" | custom-call | flops 1 | bytes 1 | tf_op jit(solution)/shard_map/head/pallas_call | solution.py:60
  145.0 4.0 %psum.15.m0 = f32[4,1408]{1,0:T(4,128)S(1)} all-reduce(f32[4,1408]{1,0:T(4,128)} %get-tuple-element.59), channel_id=1, replica_groups=mesh['dp'=16,'yh'=2,'yl'=2,'core'=2] {'core'}, use_global_device_ids=true, to_apply=%region_1.0 | all-reduce | flops 5632 | bytes 45056 | tf_op jit(solution)/shard_map/psum | solution.py:502
  149.0 0.0 all-to-all-done.3
  149.1 11.7 %all-to-all-start.4 = ((bf16[16,4,2304]{2,1,0:T(4,128)(2,1)}), bf16[16,4,2304]{2,1,0:T(4,128)(2,1)S(1)}, u32[]{:S(2)}, u32[]{:S(2)}) async-start(bf16[16,4,2304]{2,1,0:T(4,128)(2,1)} %get-tuple-element.71), calls=%async_computation.4 | async-start | bytes 589824 | tf_op jit(solution)/shard_map/all_to_all | solution.py:514
  160.8 0.4 collective-permute-start.9
  161.2 1.9 %collective-permute-start.8 = (f32[4,1408]{1,0:T(4,128)S(1)}, f32[4,1408]{1,0:T(4,128)S(1)}, u32[]{:S(2)}, u32[]{:S(2)}) collective-permute-start(f32[4,1408]{1,0:T(4,128)S(1)} %psum.15.m0), channel_id=1, source_target_pairs={{4,0},{6,2},{0,4},{2,6},{5,1},{7,3},{1,5},{3,7},{12,8},{14,10},{8,... | collective-permute-start | bytes 67592 | tf_op jit(solution)/shard_map/ppermute | solution.py:308
  163.1 1.4 collective-permute-start.7
  164.5 2.3 %d_tokens.1 = bf16[128,1280]{1,0:T(8,128)(2,1)} custom-call(bf16[2,640,128]{2,1,0:T(8,128)(2,1)} %get-tuple-element.40.table_ref, bf16[320,2,1280]{2,1,0:T(2,128)(2,1)S(1)} %bitcast.21, bf16[128,1280]{1,0:T(8,128)(2,1)} %grad_ref.5), custom_call_target="tpu_custom_call" | custom-call | flops 1 | bytes 1 | tf_op jit(solution)/shard_map/d_tokens/pallas_call | solution.py:60
  166.8 0.0 collective-permute-done.9.m3
  166.8 0.0 collective-permute-done.8.m2
  166.8 0.2 collective-permute-done.7.m1
  167.0 1.6 d_pooled.1
  168.6 1.7 %all-to-all-done.4 = bf16[16,4,2304]{2,1,0:T(4,128)(2,1)S(1)} async-done(((bf16[16,4,2304]{2,1,0:T(4,128)(2,1)}), bf16[16,4,2304]{2,1,0:T(4,128)(2,1)S(1)}, u32[]{:S(2)}, u32[]{:S(2)}) %all-to-all-start.4) | async-done | bytes 294944 | tf_op jit(solution)/shard_map/all_to_all | solution.py:514
  170.3 0.1 reshape.71
  170.4 1.0 convolution_convert_fusion
Async XLA Ops:
  3.7 38.0 %all-to-all-start = ((bf16[64,5,2,1408]{3,2,1,0:T(2,128)(2,1)}), bf16[64,5,2,1408]{3,2,1,0:T(2,128)(2,1)S(1)}, u32[]{:S(2)}, u32[]{:S(2)}) async-start(bf16[64,5,2,1408]{3,2,1,0:T(2,128)(2,1)} %bitcast.25), calls=%async_computation | async-start | bytes 3604480 | tf_op jit(solution)/shard_map/all_to_all | solution.py:423
  41.8 5.8 %collective-permute-start = (bf16[320,2,1408]{2,1,0:T(2,128)(2,1)S(1)}, bf16[320,2,1408]{2,1,0:T(2,128)(2,1)}, u32[]{:S(2)}, u32[]{:S(2)}) collective-permute-start(bf16[320,2,1408]{2,1,0:T(2,128)(2,1)S(1)} %bitcast.16), channel_id=1, source_target_pairs={{0,1},{1,0},{2,3},{3,2},{4,5},{5,4},{6,7},{7,6},{8,9},{9,8},{10,11... | collective-permute-start | bytes 5406728 | tf_op jit(solution)/shard_map/ppermute | solution.py:427
  41.8 31.3 %all-to-all-start.2 = ((bf16[64,5,2,1280]{3,2,1,0:T(2,128)(2,1)}), bf16[64,5,2,1280]{3,2,1,0:T(2,128)(2,1)S(1)}, u32[]{:S(2)}, u32[]{:S(2)}) async-start(bf16[64,5,2,1280]{3,2,1,0:T(2,128)(2,1)} %bitcast.22), calls=%async_computation.2 | async-start | bytes 3276800 | tf_op jit(solution)/shard_map/all_to_all | solution.py:423
  64.0 9.2 %collective-permute-start.1 = (bf16[640,1280]{1,0:T(8,128)(2,1)}, bf16[640,1280]{1,0:T(8,128)(2,1)}, u32[]{:S(2)}, u32[]{:S(2)}) collective-permute-start(bf16[640,1280]{1,0:T(8,128)(2,1)} %get-tuple-element.44), channel_id=1, source_target_pairs={{0,1},{1,0},{2,3},{3,2},{4,5},{5,4},{6,7},{7,6},{8,9},{9,8},{10,11... | collective-permute-start | bytes 4915208 | tf_op jit(solution)/shard_map/ppermute | solution.py:427
  73.1 9.8 %collective-permute-start.2 = (bf16[320,2,1280]{2,1,0:T(2,128)(2,1)S(1)}, bf16[320,2,1280]{2,1,0:T(2,128)(2,1)S(1)}, u32[]{:S(2)}, u32[]{:S(2)}) collective-permute-start(bf16[320,2,1280]{2,1,0:T(2,128)(2,1)S(1)} %bitcast.19), channel_id=1, source_target_pairs={{0,1},{1,0},{2,3},{3,2},{4,5},{5,4},{6,7},{7,6},{8,9},{9,8},{10,11... | collective-permute-start | bytes 4915208 | tf_op jit(solution)/shard_map/ppermute | solution.py:427
  76.7 31.4 %all-to-all-start.1 = ((bf16[64,5,2,1280]{3,2,1,0:T(2,128)(2,1)}), bf16[64,5,2,1280]{3,2,1,0:T(2,128)(2,1)}, u32[]{:S(2)}, u32[]{:S(2)}) async-start(bf16[64,5,2,1280]{3,2,1,0:T(2,128)(2,1)} %bitcast.24), calls=%async_computation.1 | async-start | bytes 3276800 | tf_op jit(solution)/shard_map/all_to_all | solution.py:423
  105.2 6.2 %collective-permute-start.6 = (bf16[640,1280]{1,0:T(8,128)(2,1)}, bf16[640,1280]{1,0:T(8,128)(2,1)S(1)}, u32[]{:S(2)}, u32[]{:S(2)}) collective-permute-start(bf16[640,1280]{1,0:T(8,128)(2,1)} %get-tuple-element.61), channel_id=1, source_target_pairs={{0,1},{1,0},{2,3},{3,2},{4,5},{5,4},{6,7},{7,6},{8,9},{9,8},{10,11... | collective-permute-start | bytes 4915208 | tf_op jit(solution)/shard_map/ppermute | solution.py:427
  114.5 8.0 %copy-start = (f32[1,1280]{1,0:T(1,128)S(1)}, f32[1,1280]{1,0:T(1,128)}, u32[]{:S(2)}) copy-start(f32[1,1280]{1,0:T(1,128)} %get-tuple-element.55) | copy-start | bytes 15364
  114.5 34.5 %all-to-all-start.3 = ((bf16[64,5,2,1280]{3,2,1,0:T(2,128)(2,1)}), bf16[64,5,2,1280]{3,2,1,0:T(2,128)(2,1)S(1)}, u32[]{:S(2)}, u32[]{:S(2)}) async-start(bf16[64,5,2,1280]{3,2,1,0:T(2,128)(2,1)} %bitcast.23), calls=%async_computation.3 | async-start | bytes 3276800 | tf_op jit(solution)/shard_map/all_to_all | solution.py:423
  125.0 11.3 %collective-permute-start.5 = (f32[1,1280]{1,0:T(1,128)S(1)}, f32[1,1280]{1,0:T(1,128)S(1)}, u32[]{:S(2)}, u32[]{:S(2)}) collective-permute-start(f32[1,1280]{1,0:T(1,128)S(1)} %psum.14.p0), channel_id=1, source_target_pairs={{6,0},{0,2},{2,4},{4,6},{7,1},{1,3},{3,5},{5,7},{14,8},{8,10},{10,... | collective-permute-start | bytes 15368 | tf_op jit(solution)/shard_map/ppermute | solution.py:308
  126.6 12.3 %collective-permute-start.4 = (f32[1,1280]{1,0:T(1,128)S(1)}, f32[1,1280]{1,0:T(1,128)S(1)}, u32[]{:S(2)}, u32[]{:S(2)}) collective-permute-start(f32[1,1280]{1,0:T(1,128)S(1)} %psum.14.p0), channel_id=1, source_target_pairs={{4,0},{6,2},{0,4},{2,6},{5,1},{7,3},{1,5},{3,7},{12,8},{14,10},{8,... | collective-permute-start | bytes 15368 | tf_op jit(solution)/shard_map/ppermute | solution.py:308
  129.3 9.7 %collective-permute-start.3 = (f32[1,1280]{1,0:T(1,128)S(1)}, f32[1,1280]{1,0:T(1,128)S(1)}, u32[]{:S(2)}, u32[]{:S(2)}) collective-permute-start(f32[1,1280]{1,0:T(1,128)S(1)} %psum.14.p0), channel_id=1, source_target_pairs={{2,0},{4,2},{6,4},{0,6},{3,1},{5,3},{7,5},{1,7},{10,8},{12,10},{14... | collective-permute-start | bytes 15368 | tf_op jit(solution)/shard_map/ppermute | solution.py:308
  149.1 21.3 %all-to-all-start.4 = ((bf16[16,4,2304]{2,1,0:T(4,128)(2,1)}), bf16[16,4,2304]{2,1,0:T(4,128)(2,1)S(1)}, u32[]{:S(2)}, u32[]{:S(2)}) async-start(bf16[16,4,2304]{2,1,0:T(4,128)(2,1)} %get-tuple-element.71), calls=%async_computation.4 | async-start | bytes 589824 | tf_op jit(solution)/shard_map/all_to_all | solution.py:514
  160.8 6.0 %collective-permute-start.9 = (f32[4,1408]{1,0:T(4,128)S(1)}, f32[4,1408]{1,0:T(4,128)S(1)}, u32[]{:S(2)}, u32[]{:S(2)}) collective-permute-start(f32[4,1408]{1,0:T(4,128)S(1)} %psum.15.m0), channel_id=1, source_target_pairs={{6,0},{0,2},{2,4},{4,6},{7,1},{1,3},{3,5},{5,7},{14,8},{8,10},{10,... | collective-permute-start | bytes 67592 | tf_op jit(solution)/shard_map/ppermute | solution.py:308
  161.2 5.6 %collective-permute-start.8 = (f32[4,1408]{1,0:T(4,128)S(1)}, f32[4,1408]{1,0:T(4,128)S(1)}, u32[]{:S(2)}, u32[]{:S(2)}) collective-permute-start(f32[4,1408]{1,0:T(4,128)S(1)} %psum.15.m0), channel_id=1, source_target_pairs={{4,0},{6,2},{0,4},{2,6},{5,1},{7,3},{1,5},{3,7},{12,8},{14,10},{8,... | collective-permute-start | bytes 67592 | tf_op jit(solution)/shard_map/ppermute | solution.py:308
  163.1 3.9 %collective-permute-start.7 = (f32[4,1408]{1,0:T(4,128)S(1)}, f32[4,1408]{1,0:T(4,128)S(1)}, u32[]{:S(2)}, u32[]{:S(2)}) collective-permute-start(f32[4,1408]{1,0:T(4,128)S(1)} %psum.15.m0), channel_id=1, source_target_pairs={{2,0},{4,2},{6,4},{0,6},{3,1},{5,3},{7,5},{1,7},{10,8},{12,10},{14... | collective-permute-start | bytes 67592 | tf_op jit(solution)/shard_map/ppermute | solution.py:308

commit v9 on v7

--- a/solution.py
+++ b/solution.py
@@ -167,7 +167,7 @@
             part = dot(hidden[rows, :], w2[...], 1, 0)
             there = slice(rows.start - half.start, rows.stop - half.start)
             if n == 0:
-                own[there, :] = part
+                own[there, :] = part.astype(BF16)
             else:
                 other[there, :] = part.astype(BF16)
         saved += start_all([((own, other)[n], (own_out, other_out)[n])], out_sems.at[2 + n])
@@ -200,7 +200,7 @@
             part = dot(d_pre[rows, :], w1[...], 1, 1)
             there = slice(rows.start - half.start, rows.stop - half.start)
             if n == 0:
-                own[there, :] = part
+                own[there, :] = part.astype(BF16)
             else:
                 other[there, :] = part.astype(BF16)
         saved += start_all([((own, other)[n], (own_out, other_out)[n])], out_sems.at[n])
@@ -215,7 +215,7 @@
 
 
 SQUARE = (ROWS, D)
-SENT = (shape((HALF, D), F32), shape((HALF, D), BF16))
+SENT = (shape((HALF, D), BF16), shape((HALF, D), BF16))
 
 
 def expert_kernel(body, own, other, rest, outs, name):
@@ -242,7 +242,7 @@
 
 def add_body(own_ref, other_ref, send_ref):
     rows = pl.ds(pl.multiple_of(pl.program_id(0) * ADD_ROWS, ADD_ROWS), ADD_ROWS)
-    pack_rows(send_ref, own_ref[...] + other_ref[rows, :].astype(F32))
+    pack_rows(send_ref, own_ref[...].astype(F32) + other_ref[rows, :].astype(F32))
 
 
 ADD_ROWS = 320

time: 169 us -> 169 us (level)
  no operation moved by 1% of the time
where the time goes in v9:
time: 169 us; the launch traced here: 168 us
  Pallas kernels  66 us (39%)
  starting transfers between devices  47.5 us (28%)
  waiting for transfers between devices  45 us (27%)
  blocking collectives  6.61 us (4%)
    pallas_call x11, Pallas kernels, run(): pl.pallas_call(body, out_shape=outs, grid=grid, in_specs=specs or [VMEM]...  66 us
    all_to_all x4, waiting for transfers between devices, chip_swap(): return lax.all_to_all(blocks, CHIP, 0, 0, tiled=True).reshape(dims)  35.3 us
    all_to_all x4, starting transfers between devices, chip_swap(): return lax.all_to_all(blocks, CHIP, 0, 0, tiled=True).reshape(dims)  31.5 us
    ppermute x6, starting transfers between devices, y_parts(): lax.ppermute(mine, Y, [((i + shift) % 4, i) for i in range(4)])  10 us
    all_to_all x1, waiting for transfers between devices, shards(): lax.all_to_all(dp_send, 'dp', 0, 0, tiled=True).reshape(IMAGES, COLS + 128)  6.56 us
    all_to_all x1, starting transfers between devices, shards(): lax.all_to_all(dp_send, 'dp', 0, 0, tiled=True).reshape(IMAGES, COLS + 128)  5.29 us
    psum x1, blocking collectives, shards(): messages = y_parts(lax.psum(part, 'core'))  4.02 us
  transfers between devices with their start and end apart: 15, of which 6 were waited for; matrix products, arithmetic and copies ran while one was open for 0% of the time, Pallas kernels for 38%

profile of v9, /device:TPU:0, one launch (start us, length us, event | category | flops | bytes accessed | tf_op | source)
XLA Modules:
  0.0 167.5 jit_solution(7972019212087593788)
XLA Ops:
  0.6 3.1 %dispatch_x.1 = (bf16[2,640,128]{2,1,0:T(8,128)(2,1)}, bf16[320,2,1408]{2,1,0:T(2,128)(2,1)}) custom-call(s32[2,128]{1,0:T(2,128)} %bitcast.27, s32[4,4]{1,0:T(4,128)} %labels_ref.3, bf16[128,1280]{1,0:T(8,128)(2,1)} %tokens_ref.3), custom_call_target="tpu_custom_call" | custom-call | flops 1 | bytes 1 | tf_op jit(solution)/shard_map/dispatch_x/pallas_call | solution.py:60
  3.7 11.5 %all-to-all-start = ((bf16[64,5,2,1408]{3,2,1,0:T(2,128)(2,1)}), bf16[64,5,2,1408]{3,2,1,0:T(2,128)(2,1)S(1)}, u32[]{:S(2)}, u32[]{:S(2)}) async-start(bf16[64,5,2,1408]{3,2,1,0:T(2,128)(2,1)} %bitcast.25), calls=%async_computation | async-start | bytes 3604480 | tf_op jit(solution)/shard_map/all_to_all | solution.py:423
  15.2 3.1 %dispatch_g.1 = bf16[320,2,1280]{2,1,0:T(2,128)(2,1)} custom-call(bf16[2,640,128]{2,1,0:T(8,128)(2,1)} %get-tuple-element.44.table_ref, bf16[128,1280]{1,0:T(8,128)(2,1)} %grad_ref.5, f32[2,128]{1,0:T(2,128)} %bitcast.28), custom_call_target="tpu_custom_call" | custom-call | flops 1 | bytes 1 | tf_op jit(solution)/shard_map/dispatch_g/pallas_call | solution.py:60
  18.3 23.5 %all-to-all-done = bf16[64,5,2,1408]{3,2,1,0:T(2,128)(2,1)S(1)} async-done(((bf16[64,5,2,1408]{3,2,1,0:T(2,128)(2,1)}), bf16[64,5,2,1408]{3,2,1,0:T(2,128)(2,1)S(1)}, u32[]{:S(2)}, u32[]{:S(2)}) %all-to-all-start) | async-done | bytes 1802272 | tf_op jit(solution)/shard_map/all_to_all | solution.py:423
  41.8 0.0 collective-permute-start
  41.8 5.8 %all-to-all-start.2 = ((bf16[64,5,2,1280]{3,2,1,0:T(2,128)(2,1)}), bf16[64,5,2,1280]{3,2,1,0:T(2,128)(2,1)S(1)}, u32[]{:S(2)}, u32[]{:S(2)}) async-start(bf16[64,5,2,1280]{3,2,1,0:T(2,128)(2,1)} %bitcast.22), calls=%async_computation.2 | async-start | bytes 3276800 | tf_op jit(solution)/shard_map/all_to_all | solution.py:423
  47.6 0.0 collective-permute-done.other_x
  47.6 16.3 %forward.1 = (bf16[1280,1280]{1,0:T(8,128)(2,1)}, bf16[1280,1280]{1,0:T(8,128)(2,1)}, bf16[1280,1280]{1,0:T(8,128)(2,1)}, bf16[640,1280]{1,0:T(8,128)(2,1)}, bf16[640,1280]{1,0:T(8,128)(2,1)}) custom-call(bf16[320,2,1408]{2,1,0:T(2,128)(2,1)S(1)} %bitcast.17, bf16[320,2,1408]{2,1,0:T(2,128)(2,1)} %collective-permute-done.other_x, bf16[1280,1280]{1,0:T(8,128)(2,1)} %w1_in.3, ...), custom_call_target="tpu_custom_call" | custom-call | flops 1 | bytes 1 | tf_op jit(solution)/shard_map/forward/pallas_call | solution.py:60
  64.0 0.3 collective-permute-start.1
  64.3 0.6 slice.12
  64.9 2.1 %labels.1 = (f32[4,2176]{1,0:T(4,128)}, f32[1,2176]{1,0:T(1,128)}) custom-call(s32[1]{0:T(128)} %bitcast.9.first_ref, bf16[64,128]{1,0:T(8,128)(2,1)} %bitcast.26, s32[4,4]{1,0:T(4,128)} %labels_ref.3), custom_call_target="tpu_custom_call" | custom-call | flops 1 | bytes 1 | tf_op jit(solution)/shard_map/labels/pallas_call | solution.py:60
  67.0 6.1 %all-to-all-done.2 = bf16[64,5,2,1280]{3,2,1,0:T(2,128)(2,1)S(1)} async-done(((bf16[64,5,2,1280]{3,2,1,0:T(2,128)(2,1)}), bf16[64,5,2,1280]{3,2,1,0:T(2,128)(2,1)S(1)}, u32[]{:S(2)}, u32[]{:S(2)}) %all-to-all-start.2) | async-done | bytes 1638432 | tf_op jit(solution)/shard_map/all_to_all | solution.py:423
  73.1 0.0 collective-permute-start.2
  73.1 0.0 collective-permute-done.1.other_ref
  73.1 3.2 %add_out.1 = bf16[320,2,1280]{2,1,0:T(2,128)(2,1)} custom-call(bf16[640,1280]{1,0:T(8,128)(2,1)} %get-tuple-element.47.own_ref, bf16[640,1280]{1,0:T(8,128)(2,1)} %collective-permute-done.1.other_ref), custom_call_target="tpu_custom_call" | custom-call | flops 1 | bytes 1 | tf_op jit(solution)/shard_map/add_out/pallas_call | solution.py:60
  76.4 6.2 %all-to-all-start.1 = ((bf16[64,5,2,1280]{3,2,1,0:T(2,128)(2,1)}), bf16[64,5,2,1280]{3,2,1,0:T(2,128)(2,1)}, u32[]{:S(2)}, u32[]{:S(2)}) async-start(bf16[64,5,2,1280]{3,2,1,0:T(2,128)(2,1)} %bitcast.24), calls=%async_computation.1 | async-start | bytes 3276800 | tf_op jit(solution)/shard_map/all_to_all | solution.py:423
  82.6 0.0 collective-permute-done.2.other_g
  82.6 22.2 %backward.1 = (bf16[640,1280]{1,0:T(8,128)(2,1)}, bf16[640,1280]{1,0:T(8,128)(2,1)}, bf16[1280,1280]{1,0:T(8,128)(2,1)}, bf16[1280,1280]{1,0:T(8,128)(2,1)}) custom-call(bf16[320,2,1280]{2,1,0:T(2,128)(2,1)S(1)} %bitcast.20, bf16[320,2,1280]{2,1,0:T(2,128)(2,1)S(1)} %collective-permute-done.2.other_g, bf16[1280,1280]{1,0:T(8,128)(2,1)} %get-tuple-element.54.slope_in, ...), custom_call_target="tpu_custom_call" | custom-call | flops 1 | bytes 1 | tf_op jit(solution)/shard_map/backward/pallas_call | solution.py:60
  104.8 0.3 collective-permute-start.3
  105.1 2.7 %all-to-all-done.1 = bf16[64,5,2,1280]{3,2,1,0:T(2,128)(2,1)} async-done(((bf16[64,5,2,1280]{3,2,1,0:T(2,128)(2,1)}), bf16[64,5,2,1280]{3,2,1,0:T(2,128)(2,1)}, u32[]{:S(2)}, u32[]{:S(2)}) %all-to-all-start.1) | async-done | bytes 1638432 | tf_op jit(solution)/shard_map/all_to_all | solution.py:423
  107.8 3.2 %mixed.1 = (bf16[128,1280]{1,0:T(8,128)(2,1)}, f32[2,128]{1,0:T(2,128)}, f32[1,1280]{1,0:T(1,128)}) custom-call(bf16[2,640,128]{2,1,0:T(8,128)(2,1)} %get-tuple-element.44.table_ref, bf16[320,2,1280]{2,1,0:T(2,128)(2,1)} %bitcast.5.in_ref, bf16[128,1280]{1,0:T(8,128)(2,1)} %tokens_ref.3, bf16[128,1280]{1,0:T(8,128)(2,1)} %grad_ref.5, f32[2,128]{1,0:T(2,128)} %bitcast.29), custom_call_target="tpu_custom_call" | custom-call | flops 17179869184 | bytes 67108864 | tf_op jit(solution)/shard_map/mixed/pallas_call | solution.py:60
  111.0 2.6 %psum.14.p0 = f32[1,1280]{1,0:T(1,128)S(1)} all-reduce(f32[1,1280]{1,0:T(1,128)} %get-tuple-element.58), channel_id=1, replica_groups=mesh['dp'=16,'yh'=2,'yl'=2,'core'=2] {'core'}, use_global_device_ids=true, to_apply=%region_0.0 | all-reduce | flops 1280 | bytes 10240 | tf_op jit(solution)/shard_map/psum | solution.py:487
  113.6 0.8 collective-permute-start.6
  114.4 1.4 collective-permute-start.5
  115.8 2.0 %collective-permute-start.4 = (f32[1,1280]{1,0:T(1,128)S(1)}, f32[1,1280]{1,0:T(1,128)S(1)}, u32[]{:S(2)}, u32[]{:S(2)}) collective-permute-start(f32[1,1280]{1,0:T(1,128)S(1)} %psum.14.p0), channel_id=1, source_target_pairs={{2,0},{4,2},{6,4},{0,6},{3,1},{5,3},{7,5},{1,7},{10,8},{12,10},{14... | collective-permute-start | bytes 15368 | tf_op jit(solution)/shard_map/ppermute | solution.py:308
  117.9 0.0 collective-permute-done.3.other_ref
  117.9 2.7 %add_rows.1 = bf16[320,2,1280]{2,1,0:T(2,128)(2,1)} custom-call(bf16[640,1280]{1,0:T(8,128)(2,1)} %get-tuple-element.59.own_ref, bf16[640,1280]{1,0:T(8,128)(2,1)S(1)} %collective-permute-done.3.other_ref), custom_call_target="tpu_custom_call" | custom-call | flops 1 | bytes 1 | tf_op jit(solution)/shard_map/add_rows/pallas_call | solution.py:60
  120.6 0.0 collective-permute-done.6.p3
  120.6 0.0 collective-permute-done.5.p2
  120.6 0.0 collective-permute-done.4.p1
  120.6 8.0 %all-to-all-start.3 = ((bf16[64,5,2,1280]{3,2,1,0:T(2,128)(2,1)}), bf16[64,5,2,1280]{3,2,1,0:T(2,128)(2,1)S(1)}, u32[]{:S(2)}, u32[]{:S(2)}) async-start(bf16[64,5,2,1280]{3,2,1,0:T(2,128)(2,1)} %bitcast.23), calls=%async_computation.3 | async-start | bytes 3276800 | tf_op jit(solution)/shard_map/all_to_all | solution.py:423
  128.6 6.1 %head.1 = (f32[4,1280]{1,0:T(4,128)}, f32[4,1408]{1,0:T(4,128)}, bf16[16,4,2304]{2,1,0:T(4,128)(2,1)}) custom-call(s32[1]{0:T(128)} %bitcast.6.here_ref, f32[1,1280]{1,0:T(1,128)S(1)} %psum.14.p0, f32[1,1280]{1,0:T(1,128)S(1)} %collective-permute-done.4.p1, f32[1,1280]{1,0:T(1,128)S(1)} %collective-permute-done.5.p2, ...), custom_call_target="tpu_custom_call" | custom-call | flops 1 | bytes 1 | tf_op jit(solution)/shard_map/head/pallas_call | solution.py:60
  134.7 4.0 %psum.15.m0 = f32[4,1408]{1,0:T(4,128)S(1)} all-reduce(f32[4,1408]{1,0:T(4,128)} %get-tuple-element.70), channel_id=1, replica_groups=mesh['dp'=16,'yh'=2,'yl'=2,'core'=2] {'core'}, use_global_device_ids=true, to_apply=%region_1.0 | all-reduce | flops 5632 | bytes 45056 | tf_op jit(solution)/shard_map/psum | solution.py:504
  138.7 1.6 collective-permute-start.9
  140.3 2.7 %collective-permute-start.8 = (f32[4,1408]{1,0:T(4,128)S(1)}, f32[4,1408]{1,0:T(4,128)S(1)}, u32[]{:S(2)}, u32[]{:S(2)}) collective-permute-start(f32[4,1408]{1,0:T(4,128)S(1)} %psum.15.m0), channel_id=1, source_target_pairs={{4,0},{6,2},{0,4},{2,6},{5,1},{7,3},{1,5},{3,7},{12,8},{14,10},{8,... | collective-permute-start | bytes 67592 | tf_op jit(solution)/shard_map/ppermute | solution.py:308
  143.0 1.5 collective-permute-start.7
  144.5 3.1 %collective-permute-done.9.m3 = f32[4,1408]{1,0:T(4,128)S(1)} collective-permute-done((f32[4,1408]{1,0:T(4,128)S(1)}, f32[4,1408]{1,0:T(4,128)S(1)}, u32[]{:S(2)}, u32[]{:S(2)}) %collective-permute-start.9) | collective-permute-done | bytes 22560 | tf_op jit(solution)/shard_map/ppermute | solution.py:308
  147.6 0.0 collective-permute-done.8.m2
  147.6 0.0 collective-permute-done.7.m1
  147.6 1.6 d_pooled.1
  149.2 3.0 %all-to-all-done.3 = bf16[64,5,2,1280]{3,2,1,0:T(2,128)(2,1)S(1)} async-done(((bf16[64,5,2,1280]{3,2,1,0:T(2,128)(2,1)}), bf16[64,5,2,1280]{3,2,1,0:T(2,128)(2,1)S(1)}, u32[]{:S(2)}, u32[]{:S(2)}) %all-to-all-start.3) | async-done | bytes 1638432 | tf_op jit(solution)/shard_map/all_to_all | solution.py:423
  152.2 5.3 %all-to-all-start.4 = ((bf16[16,4,2304]{2,1,0:T(4,128)(2,1)}), bf16[16,4,2304]{2,1,0:T(4,128)(2,1)S(1)}, u32[]{:S(2)}, u32[]{:S(2)}) async-start(bf16[16,4,2304]{2,1,0:T(4,128)(2,1)} %get-tuple-element.79), calls=%async_computation.4 | async-start | bytes 589824 | tf_op jit(solution)/shard_map/all_to_all | solution.py:515
  157.5 2.3 %d_tokens.1 = bf16[128,1280]{1,0:T(8,128)(2,1)} custom-call(bf16[2,640,128]{2,1,0:T(8,128)(2,1)} %get-tuple-element.44.table_ref, bf16[320,2,1280]{2,1,0:T(2,128)(2,1)S(1)} %bitcast.21, bf16[128,1280]{1,0:T(8,128)(2,1)} %grad_ref.5), custom_call_target="tpu_custom_call" | custom-call | flops 1 | bytes 1 | tf_op jit(solution)/shard_map/d_tokens/pallas_call | solution.py:60
  159.8 6.6 %all-to-all-done.4 = bf16[16,4,2304]{2,1,0:T(4,128)(2,1)S(1)} async-done(((bf16[16,4,2304]{2,1,0:T(4,128)(2,1)}), bf16[16,4,2304]{2,1,0:T(4,128)(2,1)S(1)}, u32[]{:S(2)}, u32[]{:S(2)}) %all-to-all-start.4) | async-done | bytes 294944 | tf_op jit(solution)/shard_map/all_to_all | solution.py:515
  166.4 0.1 reshape.71
  166.5 1.0 convolution_convert_fusion
Async XLA Ops:
  3.7 38.0 %all-to-all-start = ((bf16[64,5,2,1408]{3,2,1,0:T(2,128)(2,1)}), bf16[64,5,2,1408]{3,2,1,0:T(2,128)(2,1)S(1)}, u32[]{:S(2)}, u32[]{:S(2)}) async-start(bf16[64,5,2,1408]{3,2,1,0:T(2,128)(2,1)} %bitcast.25), calls=%async_computation | async-start | bytes 3604480 | tf_op jit(solution)/shard_map/all_to_all | solution.py:423
  41.8 5.8 %collective-permute-start = (bf16[320,2,1408]{2,1,0:T(2,128)(2,1)S(1)}, bf16[320,2,1408]{2,1,0:T(2,128)(2,1)}, u32[]{:S(2)}, u32[]{:S(2)}) collective-permute-start(bf16[320,2,1408]{2,1,0:T(2,128)(2,1)S(1)} %bitcast.16), channel_id=1, source_target_pairs={{0,1},{1,0},{2,3},{3,2},{4,5},{5,4},{6,7},{7,6},{8,9},{9,8},{10,11... | collective-permute-start | bytes 5406728 | tf_op jit(solution)/shard_map/ppermute | solution.py:427
  41.8 31.3 %all-to-all-start.2 = ((bf16[64,5,2,1280]{3,2,1,0:T(2,128)(2,1)}), bf16[64,5,2,1280]{3,2,1,0:T(2,128)(2,1)S(1)}, u32[]{:S(2)}, u32[]{:S(2)}) async-start(bf16[64,5,2,1280]{3,2,1,0:T(2,128)(2,1)} %bitcast.22), calls=%async_computation.2 | async-start | bytes 3276800 | tf_op jit(solution)/shard_map/all_to_all | solution.py:423
  64.0 9.2 %collective-permute-start.1 = (bf16[640,1280]{1,0:T(8,128)(2,1)}, bf16[640,1280]{1,0:T(8,128)(2,1)}, u32[]{:S(2)}, u32[]{:S(2)}) collective-permute-start(bf16[640,1280]{1,0:T(8,128)(2,1)} %get-tuple-element.48), channel_id=1, source_target_pairs={{0,1},{1,0},{2,3},{3,2},{4,5},{5,4},{6,7},{7,6},{8,9},{9,8},{10,11... | collective-permute-start | bytes 4915208 | tf_op jit(solution)/shard_map/ppermute | solution.py:427
  73.1 9.5 %collective-permute-start.2 = (bf16[320,2,1280]{2,1,0:T(2,128)(2,1)S(1)}, bf16[320,2,1280]{2,1,0:T(2,128)(2,1)S(1)}, u32[]{:S(2)}, u32[]{:S(2)}) collective-permute-start(bf16[320,2,1280]{2,1,0:T(2,128)(2,1)S(1)} %bitcast.19), channel_id=1, source_target_pairs={{0,1},{1,0},{2,3},{3,2},{4,5},{5,4},{6,7},{7,6},{8,9},{9,8},{10,11... | collective-permute-start | bytes 4915208 | tf_op jit(solution)/shard_map/ppermute | solution.py:427
  76.4 31.4 %all-to-all-start.1 = ((bf16[64,5,2,1280]{3,2,1,0:T(2,128)(2,1)}), bf16[64,5,2,1280]{3,2,1,0:T(2,128)(2,1)}, u32[]{:S(2)}, u32[]{:S(2)}) async-start(bf16[64,5,2,1280]{3,2,1,0:T(2,128)(2,1)} %bitcast.24), calls=%async_computation.1 | async-start | bytes 3276800 | tf_op jit(solution)/shard_map/all_to_all | solution.py:423
  104.8 13.1 %collective-permute-start.3 = (bf16[640,1280]{1,0:T(8,128)(2,1)}, bf16[640,1280]{1,0:T(8,128)(2,1)S(1)}, u32[]{:S(2)}, u32[]{:S(2)}) collective-permute-start(bf16[640,1280]{1,0:T(8,128)(2,1)} %get-tuple-element.60), channel_id=1, source_target_pairs={{0,1},{1,0},{2,3},{3,2},{4,5},{5,4},{6,7},{7,6},{8,9},{9,8},{10,11... | collective-permute-start | bytes 4915208 | tf_op jit(solution)/shard_map/ppermute | solution.py:427
  113.6 7.0 %collective-permute-start.6 = (f32[1,1280]{1,0:T(1,128)S(1)}, f32[1,1280]{1,0:T(1,128)S(1)}, u32[]{:S(2)}, u32[]{:S(2)}) collective-permute-start(f32[1,1280]{1,0:T(1,128)S(1)} %psum.14.p0), channel_id=1, source_target_pairs={{6,0},{0,2},{2,4},{4,6},{7,1},{1,3},{3,5},{5,7},{14,8},{8,10},{10,... | collective-permute-start | bytes 15368 | tf_op jit(solution)/shard_map/ppermute | solution.py:308
  114.4 6.2 %collective-permute-start.5 = (f32[1,1280]{1,0:T(1,128)S(1)}, f32[1,1280]{1,0:T(1,128)S(1)}, u32[]{:S(2)}, u32[]{:S(2)}) collective-permute-start(f32[1,1280]{1,0:T(1,128)S(1)} %psum.14.p0), channel_id=1, source_target_pairs={{4,0},{6,2},{0,4},{2,6},{5,1},{7,3},{1,5},{3,7},{12,8},{14,10},{8,... | collective-permute-start | bytes 15368 | tf_op jit(solution)/shard_map/ppermute | solution.py:308
  115.8 4.8 %collective-permute-start.4 = (f32[1,1280]{1,0:T(1,128)S(1)}, f32[1,1280]{1,0:T(1,128)S(1)}, u32[]{:S(2)}, u32[]{:S(2)}) collective-permute-start(f32[1,1280]{1,0:T(1,128)S(1)} %psum.14.p0), channel_id=1, source_target_pairs={{2,0},{4,2},{6,4},{0,6},{3,1},{5,3},{7,5},{1,7},{10,8},{12,10},{14... | collective-permute-start | bytes 15368 | tf_op jit(solution)/shard_map/ppermute | solution.py:308
  120.6 31.6 %all-to-all-start.3 = ((bf16[64,5,2,1280]{3,2,1,0:T(2,128)(2,1)}), bf16[64,5,2,1280]{3,2,1,0:T(2,128)(2,1)S(1)}, u32[]{:S(2)}, u32[]{:S(2)}) async-start(bf16[64,5,2,1280]{3,2,1,0:T(2,128)(2,1)} %bitcast.23), calls=%async_computation.3 | async-start | bytes 3276800 | tf_op jit(solution)/shard_map/all_to_all | solution.py:423
  138.7 8.9 %collective-permute-start.9 = (f32[4,1408]{1,0:T(4,128)S(1)}, f32[4,1408]{1,0:T(4,128)S(1)}, u32[]{:S(2)}, u32[]{:S(2)}) collective-permute-start(f32[4,1408]{1,0:T(4,128)S(1)} %psum.15.m0), channel_id=1, source_target_pairs={{6,0},{0,2},{2,4},{4,6},{7,1},{1,3},{3,5},{5,7},{14,8},{8,10},{10,... | collective-permute-start | bytes 67592 | tf_op jit(solution)/shard_map/ppermute | solution.py:308
  140.3 7.2 %collective-permute-start.8 = (f32[4,1408]{1,0:T(4,128)S(1)}, f32[4,1408]{1,0:T(4,128)S(1)}, u32[]{:S(2)}, u32[]{:S(2)}) collective-permute-start(f32[4,1408]{1,0:T(4,128)S(1)} %psum.15.m0), channel_id=1, source_target_pairs={{4,0},{6,2},{0,4},{2,6},{5,1},{7,3},{1,5},{3,7},{12,8},{14,10},{8,... | collective-permute-start | bytes 67592 | tf_op jit(solution)/shard_map/ppermute | solution.py:308
  143.0 4.6 %collective-permute-start.7 = (f32[4,1408]{1,0:T(4,128)S(1)}, f32[4,1408]{1,0:T(4,128)S(1)}, u32[]{:S(2)}, u32[]{:S(2)}) collective-permute-start(f32[4,1408]{1,0:T(4,128)S(1)} %psum.15.m0), channel_id=1, source_target_pairs={{2,0},{4,2},{6,4},{0,6},{3,1},{5,3},{7,5},{1,7},{10,8},{12,10},{14... | collective-permute-start | bytes 67592 | tf_op jit(solution)/shard_map/ppermute | solution.py:308
  152.2 14.2 %all-to-all-start.4 = ((bf16[16,4,2304]{2,1,0:T(4,128)(2,1)}), bf16[16,4,2304]{2,1,0:T(4,128)(2,1)S(1)}, u32[]{:S(2)}, u32[]{:S(2)}) async-start(bf16[16,4,2304]{2,1,0:T(4,128)(2,1)} %get-tuple-element.79), calls=%async_computation.4 | async-start | bytes 589824 | tf_op jit(solution)/shard_map/all_to_all | solution.py:515
